TPU v7x, 32 devices: a whole 2x2x4 slice. The times are simulated.
32 devices in a mesh: mod: 4 (over z), dp: 8 (over y, x, core).
Axes of the slice: x: 2, y: 2, z: 4, core: 2. Of those that a mesh axis runs over, the one named last changes fastest.
Arguments:
- train_grads: float32 [1024, 16, 512], P('dp', 'mod'), may hold values from -50 to 50
- queries: float32 [32, 16, 512], P('dp', 'mod'), may hold values from -6 to 6
- damping: float32 [16], P('mod'), may hold values from 0.05 to 0.5
Outputs:
- scores: float32 [1024, 32], P('dp', 'mod')
All inputs are finite; a program needn't handle non-finite values.
Results may differ from a plain program's by a relative error of at most 0.012.
Values sent between devices are 32-bit elements; how exact they have to be, the bound alone decides.
No kernel may reach another device: no remote copies, remote signals or barrier semaphores. Data moves between devices by JAX's collectives and lax.ppermute only.
A program may use at most 128 MiB of HBM per device.

v0:
```python
import functools
import math

import jax
import jax.numpy as jnp
from jax import lax
from jax.experimental import pallas as pl
from jax.experimental.pallas import tpu as pltpu
from jax.sharding import PartitionSpec as P

NEWTON_STEPS = 8
CORES = 2

epsilon = 1e-06

VMEM = pl.BlockSpec(memory_space=pltpu.VMEM)
SMEM = pl.BlockSpec(memory_space=pltpu.SMEM)


def halves(value):
    high = value.astype(jnp.bfloat16)
    return high, (value - high.astype(jnp.float32)).astype(jnp.bfloat16)


def product(left, right, dims=(((1,), (0,)), ((), ()))):
    return lax.dot_general(left, right, dims, preferred_element_type=jnp.float32)


def product_3(left_high, left_low, right_high, right_low, dims=(((1,), (0,)), ((), ()))):
    return (
        product(left_high, right_high, dims)
        + product(left_high, right_low, dims)
        + product(left_low, right_high, dims)
    )


def pack_kernel(offsets, rows_ref, queries_ref, *blocks):
    chip = lax.axis_index("dp") // CORES
    rows = rows_ref.shape[0]
    for offset, block in zip(offsets, blocks):
        module = lax.bitwise_xor(chip, jnp.int32(offset))
        block[0:rows] = rows_ref[:, module, :]
        block[rows:] = queries_ref[:, module, :]


def pack(offsets, train_grads, queries):
    rows, _, width = train_grads.shape
    block = jax.ShapeDtypeStruct((rows + queries.shape[0], width), jnp.float32)
    return pl.pallas_call(
        functools.partial(pack_kernel, offsets),
        out_shape=[block] * len(offsets),
        in_specs=[VMEM, VMEM],
        out_specs=[VMEM] * len(offsets),
        name="pack",
    )(train_grads, queries)


def add_gram(rows, blocks, left_ref, right_ref, stack):
    half = left_ref.shape[0]
    for place, block in enumerate(blocks):
        stack[place * rows : (place + 1) * rows] = block[0:rows]
    high, low = halves(stack[...])
    dims = (((0,), (0,)), ((), ()))
    left_ref[...] += product_3(high[:, :half], low[:, :half], high[:, :half], low[:, :half], dims)
    right_ref[...] += product_3(high, low, high[:, half:], low[:, half:], dims)


def gram_kernel(count, rows, *refs):
    blocks, refs = refs[:count], refs[count:]
    given, (left_ref, right_ref, stack) = refs[:-3], refs[-3:]
    if given:
        left_ref[...] = given[0][...]
        right_ref[...] = given[1][...]
    else:
        left_ref[...] = jnp.zeros_like(left_ref)
        right_ref[...] = jnp.zeros_like(right_ref)
    add_gram(rows, blocks, left_ref, right_ref, stack)


def gram(rows, blocks, given):
    width = blocks[0].shape[1]
    half = width // 2
    return pl.pallas_call(
        functools.partial(gram_kernel, len(blocks), rows),
        out_shape=[
            jax.ShapeDtypeStruct((half, half), jnp.float32),
            jax.ShapeDtypeStruct((width, half), jnp.float32),
        ],
        in_specs=[VMEM] * (len(blocks) + len(given)),
        out_specs=[VMEM] * 2,
        scratch_shapes=[pltpu.VMEM((len(blocks) * rows, width), jnp.float32)],
        name="gram",
    )(*blocks, *given)


def solve_kernel(sizes, *refs):
    chips, rows, per_device, groups, total_rows, scale = sizes
    refs = list(refs)
    damping_ref, left_ref, right_ref = refs[:3]
    arrived = refs[3 : 3 + chips]
    passed = refs[3 + chips : 3 + 2 * chips]
    scores = refs[3 + 2 * chips : 3 + 3 * chips]
    left, right, stack, state, high, low, asked = refs[3 + 3 * chips :]
    half = left_ref.shape[0]
    width = 2 * half
    index = lax.axis_index("dp")
    chip, core = index // CORES, index % CORES
    pair = CORES * per_device
    total_queries = chips * pair
    group = total_queries // groups
    group_here = lax.axis_index("mod")

    for offset in range(chips):
        mine = arrived[offset][rows : rows + per_device]
        other = passed[offset][rows : rows + per_device]
        both = jnp.where(
            core == 0, jnp.concatenate([mine, other], 0), jnp.concatenate([other, mine], 0)
        )
        source = lax.bitwise_xor(chip, jnp.int32(offset))
        asked[pl.ds(pl.multiple_of(source * pair, pair), pair)] = both

    left[...] = left_ref[...]
    right[...] = right_ref[...]
    add_gram(rows, passed[1:], left, right, stack)

    diagonal = lax.broadcasted_iota(jnp.int32, (half, half), 0) == lax.broadcasted_iota(
        jnp.int32, (half, half), 1
    )
    eye = diagonal.astype(jnp.float32)
    first, cross, last = left[...], right[0:half], right[half:]
    trace = jnp.sum((first + last) * eye, keepdims=True).reshape(1, 1) / total_rows
    shift = damping_ref[chip] * trace / width
    first = first / total_rows + shift * eye
    last = last / total_rows + shift * eye
    cross = cross / total_rows
    squares = first * first + last * last + 2.0 * (cross * cross)
    inverse_norm = lax.rsqrt(jnp.sum(squares, keepdims=True).reshape(1, 1) + epsilon)
    cross = cross * inverse_norm
    state[0:half, 0:half] = first * inverse_norm
    state[0:half, half:] = cross
    state[half:width, 0:half] = cross.T
    state[half:width, half:] = last * inverse_norm
    for offset in range(groups):
        source = lax.bitwise_xor(group_here, jnp.int32(offset))
        state[width + offset * group : width + (offset + 1) * group] = (
            asked[pl.ds(pl.multiple_of(source * group, group), group)] * inverse_norm
        )

    for _ in range(NEWTON_STEPS - 1):
        high[...], low[...] = halves(state[...])

        def part(start, stop, column):
            columns = slice(column, column + half)
            return product_3(
                high[start:stop],
                low[start:stop],
                high[0:width, columns],
                low[0:width, columns],
            )

        state[0:half, 0:half] = 2.0 * state[0:half, 0:half] - part(0, half, 0)
        new = 2.0 * state[0:width, half:] - part(0, width, half)
        state[0:width, half:] = new
        state[half:width, 0:half] = new[0:half].T
        state[width:, 0:half] = 2.0 * state[width:, 0:half] - part(width, width + total_queries, 0)
        state[width:, half:] = 2.0 * state[width:, half:] - part(width, width + total_queries, half)

    high[...], low[...] = halves(state[...])
    conditioned = 2.0 * state[width:] - product_3(
        high[width:], low[width:], high[0:width], low[0:width]
    )
    conditioned_high, conditioned_low = halves(conditioned * scale)
    for offset in range(chips):
        block_high, block_low = halves(arrived[offset][0:rows])
        scores[offset][...] = product_3(
            conditioned_high, conditioned_low, block_high, block_low, (((1,), (1,)), ((), ()))
        )


def solve(sizes, damping, given, arrived, passed):
    chips, rows, per_device = sizes[:3]
    width = arrived[0].shape[1]
    half = width // 2
    total_queries = chips * CORES * per_device
    return pl.pallas_call(
        functools.partial(solve_kernel, sizes),
        out_shape=[jax.ShapeDtypeStruct((total_queries, rows), jnp.float32)] * chips,
        in_specs=[SMEM] + [VMEM] * (2 + 2 * chips),
        out_specs=[VMEM] * chips,
        scratch_shapes=[
            pltpu.VMEM((half, half), jnp.float32),
            pltpu.VMEM((width, half), jnp.float32),
            pltpu.VMEM(((chips - 1) * rows, width), jnp.float32),
            pltpu.VMEM((width + total_queries, width), jnp.float32),
            pltpu.VMEM((width + total_queries, width), jnp.bfloat16),
            pltpu.VMEM((width + total_queries, width), jnp.bfloat16),
            pltpu.VMEM((total_queries, width), jnp.float32),
        ],
        name="solve",
    )(damping, *given, *arrived, *passed)


def swap(value, axis, offset):
    return lax.ppermute(value, axis, [(i, i ^ offset) for i in range(lax.axis_size(axis))])


def per_device(train_grads, queries, damping):
    rows, modules, width = train_grads.shape
    asked = queries.shape[0]
    devices = lax.axis_size("dp")
    groups = lax.axis_size("mod")
    chips = devices // CORES
    far = list(range(chips - 1, 0, -1))
    arrived = [None] * chips
    passed = [None] * chips
    packed = [None] * chips
    for offset in far + [0]:
        (packed[offset],) = pack((offset,), train_grads, queries)
    arrived[0] = packed[0]
    for offset in far:
        arrived[offset] = swap(packed[offset], "dp", offset * CORES)
    for offset in [0] + far:
        passed[offset] = swap(arrived[offset], "dp", 1)
    given = gram(rows, [arrived[0], passed[0]], ())
    given = gram(rows, [arrived[offset] for offset in far], given)
    sizes = (
        chips,
        rows,
        asked,
        groups,
        rows * devices,
        1.0 / math.sqrt(modules * groups * width),
    )
    scores = solve(sizes, damping, given, arrived, passed)
    total = scores[0]
    for offset in far:
        total = total + swap(scores[offset], "dp", offset * CORES)
    bit = groups // 2
    while bit:
        keep = total.shape[0] // 2
        total = total[:keep] + swap(total[keep:], "mod", bit)
        bit //= 2
    return total.T


def solution(mesh):
    return jax.shard_map(
        per_device,
        mesh=mesh,
        in_specs=(P("dp", "mod", None), P("dp", "mod", None), P("mod")),
        out_specs=P("dp", "mod"),
        check_vma=False,
    )
```

profile of v0, /device:TPU:0, one launch (start us, length us, event | category | flops | bytes accessed | tf_op | source)
XLA Modules:
  0.0 55.6 jit_solution(7401456018339184722)
XLA Ops:
  0.0 2.0 %pack.6 = f32[132,512]{1,0:T(8,128)} custom-call(f32[128,4,512]{2,1,0:T(4,128)} %rows_ref.7, f32[4,4,512]{2,1,0:T(4,128)} %queries_ref.7), custom_call_target="tpu_custom_call" | custom-call | tf_op jit(solution)/shard_map/pack/pallas_call | solution.py:49
  2.0 3.0 %collective-permute-start.2 = (f32[132,512]{1,0:T(8,128)}, f32[132,512]{1,0:T(8,128)S(1)}, u32[]{:S(2)}, u32[]{:S(2)}) collective-permute-start(f32[132,512]{1,0:T(8,128)} %pack.6), channel_id=1, source_target_pairs={{0,2},{1,3},{2,0},{3,1},{4,6},{5,7},{6,4},{7,5},{8,10},{9,11},{10,... | collective-permute-start | bytes 811016 | tf_op jit(solution)/shard_map/ppermute | solution.py:204
  5.0 2.0 %pack.5 = f32[132,512]{1,0:T(8,128)} custom-call(f32[128,4,512]{2,1,0:T(4,128)} %rows_ref.7, f32[4,4,512]{2,1,0:T(4,128)} %queries_ref.7), custom_call_target="tpu_custom_call" | custom-call | tf_op jit(solution)/shard_map/pack/pallas_call | solution.py:49
  6.9 1.5 %collective-permute-start.1 = (f32[132,512]{1,0:T(8,128)}, f32[132,512]{1,0:T(8,128)S(1)}, u32[]{:S(2)}, u32[]{:S(2)}) collective-permute-start(f32[132,512]{1,0:T(8,128)} %pack.5), channel_id=1, source_target_pairs={{0,4},{1,5},{2,6},{3,7},{4,0},{5,1},{6,2},{7,3},{8,12},{9,13},{10,... | collective-permute-start | bytes 811016 | tf_op jit(solution)/shard_map/ppermute | solution.py:204
  8.5 2.0 %pack.4 = f32[132,512]{1,0:T(8,128)} custom-call(f32[128,4,512]{2,1,0:T(4,128)} %rows_ref.7, f32[4,4,512]{2,1,0:T(4,128)} %queries_ref.7), custom_call_target="tpu_custom_call" | custom-call | tf_op jit(solution)/shard_map/pack/pallas_call | solution.py:49
  10.5 0.0 collective-permute-start
  10.5 2.0 %pack.7.refs_0_.refs_3_ = f32[132,512]{1,0:T(8,128)} custom-call(f32[128,4,512]{2,1,0:T(4,128)} %rows_ref.7, f32[4,4,512]{2,1,0:T(4,128)} %queries_ref.7), custom_call_target="tpu_custom_call" | custom-call | tf_op jit(solution)/shard_map/pack/pallas_call | solution.py:49
  12.4 0.0 collective-permute-start.3
  12.4 0.0 collective-permute-done.2.refs_2_.refs_4_
  12.4 0.0 copy-start
  12.5 0.5 collective-permute-start.4
  13.0 8.3 %collective-permute-done.1.refs_1_.refs_5_ = f32[132,512]{1,0:T(8,128)S(1)} collective-permute-done((f32[132,512]{1,0:T(8,128)}, f32[132,512]{1,0:T(8,128)S(1)}, u32[]{:S(2)}, u32[]{:S(2)}) %collective-permute-start.1) | collective-permute-done | bytes 270368 | tf_op jit(solution)/shard_map/ppermute | solution.py:204
  21.2 0.0 copy-start.1
  21.2 0.0 collective-permute-start.5
  21.2 0.0 collective-permute-done.refs_0_.refs_6_
  21.2 0.0 copy-start.2
  21.3 0.5 collective-permute-start.6
  21.8 0.0 collective-permute-done.3.refs_1_.refs_7_
  21.8 0.0 copy-start.3
  21.8 0.7 %copy-done.3 = f32[132,512]{1,0:T(8,128)} copy-done((f32[132,512]{1,0:T(8,128)}, f32[132,512]{1,0:T(8,128)S(1)}, u32[]{:S(2)}) %copy-start.3) | copy-done | bytes 270360
  22.5 2.4 %gram.2 = (f32[256,256]{1,0:T(8,128)}, f32[512,256]{1,0:T(8,128)}) custom-call(f32[132,512]{1,0:T(8,128)} %pack.7.refs_0_.refs_3_, f32[132,512]{1,0:T(8,128)} %copy-done.3), custom_call_target="tpu_custom_call" | custom-call | tf_op jit(solution)/shard_map/gram/pallas_call | solution.py:83
  24.8 0.0 copy-done
  24.8 0.0 copy-done.1
  24.8 0.0 copy-done.2
  24.8 3.0 %gram.3 = (f32[256,256]{1,0:T(8,128)}, f32[512,256]{1,0:T(8,128)}) custom-call(f32[132,512]{1,0:T(8,128)} %copy-done.2, f32[132,512]{1,0:T(8,128)} %copy-done.1, f32[132,512]{1,0:T(8,128)} %copy-done, f32[256,256]{1,0:T(8,128)} %get-tuple-element.13.refs_3_, f32[512,256]{1,0:T(8,128)} %get-tuple-element.14.refs_4_), custom_call_target="tpu_custom_call" | custom-call | tf_op jit(solution)/shard_map/gram/pallas_call | solution.py:83
  27.8 0.0 collective-permute-done.4.refs_8_
  27.9 0.0 copy-start.4
  27.9 0.0 collective-permute-done.5.refs_9_
  27.9 0.0 copy-start.5
  27.9 0.0 collective-permute-done.6.refs_10_
  27.9 0.0 copy-start.6
  27.9 0.7 %copy-done.4 = f32[132,512]{1,0:T(8,128)} copy-done((f32[132,512]{1,0:T(8,128)}, f32[132,512]{1,0:T(8,128)S(1)}, u32[]{:S(2)}) %copy-start.4) | copy-done | bytes 270360
  28.6 0.1 copy-done.5
  28.7 0.1 copy-done.6
  28.8 11.6 %solve.1 = (f32[32,128]{1,0:T(8,128)}, f32[32,128]{1,0:T(8,128)}, f32[32,128]{1,0:T(8,128)}, f32[32,128]{1,0:T(8,128)}) custom-call(f32[4]{0:T(128)} %refs_0_.1, f32[256,256]{1,0:T(8,128)} %get-tuple-element.15.refs_1_, f32[512,256]{1,0:T(8,128)} %get-tuple-element.16.refs_2_, f32[132,512]{1,0:T(8,128)} %pack.7.refs_0_.refs_3_, f32[132,512]{1,0:T(8,128)} %copy-done, ...), custom_call_target="tpu_custom_call" | custom-call | tf_op jit(solution)/shard_map/solve/pallas_call | solution.py:185
  40.3 1.5 %collective-permute-start.7 = (f32[32,128]{1,0:T(8,128)}, f32[32,128]{1,0:T(8,128)S(1)}, u32[]{:S(2)}, u32[]{:S(2)}) collective-permute-start(f32[32,128]{1,0:T(8,128)} %get-tuple-element.18), channel_id=1, source_target_pairs={{0,6},{1,7},{2,4},{3,5},{4,2},{5,3},{6,0},{7,1},{8,14},{9,15},{10,... | collective-permute-start | bytes 49160 | tf_op jit(solution)/shard_map/ppermute | solution.py:204
  41.8 0.3 collective-permute-start.8
  42.1 1.7 %collective-permute-start.9 = (f32[32,128]{1,0:T(8,128)}, f32[32,128]{1,0:T(8,128)S(1)}, u32[]{:S(2)}, u32[]{:S(2)}) collective-permute-start(f32[32,128]{1,0:T(8,128)} %get-tuple-element.20), channel_id=1, source_target_pairs={{0,2},{1,3},{2,0},{3,1},{4,6},{5,7},{6,4},{7,5},{8,10},{9,11},{10,... | collective-permute-start | bytes 49160 | tf_op jit(solution)/shard_map/ppermute | solution.py:204
  43.8 1.4 %collective-permute-done.7 = f32[32,128]{1,0:T(8,128)S(1)} collective-permute-done((f32[32,128]{1,0:T(8,128)}, f32[32,128]{1,0:T(8,128)S(1)}, u32[]{:S(2)}, u32[]{:S(2)}) %collective-permute-start.7) | collective-permute-done | bytes 16416 | tf_op jit(solution)/shard_map/ppermute | solution.py:204
  45.2 0.6 %collective-permute-done.8 = f32[32,128]{1,0:T(8,128)S(1)} collective-permute-done((f32[32,128]{1,0:T(8,128)}, f32[32,128]{1,0:T(8,128)S(1)}, u32[]{:S(2)}, u32[]{:S(2)}) %collective-permute-start.8) | collective-permute-done | bytes 16416 | tf_op jit(solution)/shard_map/ppermute | solution.py:204
  45.8 0.3 collective-permute-done.9
  46.1 0.7 %add_add_fusion = f32[32,128]{1,0:T(8,128)S(1)} fusion(f32[32,128]{1,0:T(8,128)S(1)} %collective-permute-done.9, f32[32,128]{1,0:T(8,128)S(1)} %collective-permute-done.8, f32[32,128]{1,0:T(8,128)} %get-tuple-element.17, f32[32,128]{1,0:T(8,128)S(1)} %collective-permute-done.7), kind=kLoop, calls=%fused_computation | loop fusion | flops 12288 | bytes 81920 | tf_op jit(solution)/shard_map/add | solution.py:237
  46.8 2.9 %collective-permute-start.10 = (f32[16,128]{1,0:T(8,128)S(1)}, f32[16,128]{1,0:T(8,128)S(1)}, u32[]{:S(2)}, u32[]{:S(2)}) collective-permute-start(f32[16,128]{1,0:T(8,128)S(1)} %slice.17), channel_id=1, source_target_pairs={{0,16},{8,24},{16,0},{24,8},{1,17},{9,25},{17,1},{25,9},{2,18},{10... | collective-permute-start | bytes 24584 | tf_op jit(solution)/shard_map/ppermute | solution.py:204
  49.7 1.7 %collective-permute-done.10 = f32[16,128]{1,0:T(8,128)S(1)} collective-permute-done((f32[16,128]{1,0:T(8,128)S(1)}, f32[16,128]{1,0:T(8,128)S(1)}, u32[]{:S(2)}, u32[]{:S(2)}) %collective-permute-start.10) | collective-permute-done | bytes 8224 | tf_op jit(solution)/shard_map/ppermute | solution.py:204
  51.4 1.8 %collective-permute-start.11 = (f32[8,128]{1,0:T(8,128)S(1)}, f32[8,128]{1,0:T(8,128)S(1)}, u32[]{:S(2)}, u32[]{:S(2)}) collective-permute-start(f32[8,128]{1,0:T(8,128)S(1)} %slice.19), channel_id=1, source_target_pairs={{0,8},{8,0},{16,24},{24,16},{1,9},{9,1},{17,25},{25,17},{2,10},{10... | collective-permute-start | bytes 12296 | tf_op jit(solution)/shard_map/ppermute | solution.py:204
  53.2 1.8 %collective-permute-done.11 = f32[8,128]{1,0:T(8,128)S(1)} collective-permute-done((f32[8,128]{1,0:T(8,128)S(1)}, f32[8,128]{1,0:T(8,128)S(1)}, u32[]{:S(2)}, u32[]{:S(2)}) %collective-permute-start.11) | collective-permute-done | bytes 4128 | tf_op jit(solution)/shard_map/ppermute | solution.py:204
  55.0 0.6 %fusion = f32[128,8]{0,1:T(8,128)} fusion(f32[8,128]{1,0:T(8,128)S(1)} %collective-permute-done.11, f32[16,128]{1,0:T(8,128)S(1)} %slice_add_fusion), kind=kLoop, calls=%fused_computation.3 | loop fusion | flops 1024 | bytes 12288 | tf_op jit(solution)/shard_map/transpose | solution.py:243
  (3 shorter events, 0.0 us)
Async XLA Ops:
  2.0 10.5 %collective-permute-start.2 = (f32[132,512]{1,0:T(8,128)}, f32[132,512]{1,0:T(8,128)S(1)}, u32[]{:S(2)}, u32[]{:S(2)}) collective-permute-start(f32[132,512]{1,0:T(8,128)} %pack.6), channel_id=1, source_target_pairs={{0,2},{1,3},{2,0},{3,1},{4,6},{5,7},{6,4},{7,5},{8,10},{9,11},{10,... | collective-permute-start | bytes 811016 | tf_op jit(solution)/shard_map/ppermute | solution.py:204
  6.9 14.3 %collective-permute-start.1 = (f32[132,512]{1,0:T(8,128)}, f32[132,512]{1,0:T(8,128)S(1)}, u32[]{:S(2)}, u32[]{:S(2)}) collective-permute-start(f32[132,512]{1,0:T(8,128)} %pack.5), channel_id=1, source_target_pairs={{0,4},{1,5},{2,6},{3,7},{4,0},{5,1},{6,2},{7,3},{8,12},{9,13},{10,... | collective-permute-start | bytes 811016 | tf_op jit(solution)/shard_map/ppermute | solution.py:204
  10.5 10.8 %collective-permute-start = (f32[132,512]{1,0:T(8,128)}, f32[132,512]{1,0:T(8,128)S(1)}, u32[]{:S(2)}, u32[]{:S(2)}) collective-permute-start(f32[132,512]{1,0:T(8,128)} %pack.4), channel_id=1, source_target_pairs={{0,6},{1,7},{2,4},{3,5},{4,2},{5,3},{6,0},{7,1},{8,14},{9,15},{10,... | collective-permute-start | bytes 811016 | tf_op jit(solution)/shard_map/ppermute | solution.py:204
  12.4 9.3 %collective-permute-start.3 = (f32[132,512]{1,0:T(8,128)}, f32[132,512]{1,0:T(8,128)S(1)}, u32[]{:S(2)}, u32[]{:S(2)}) collective-permute-start(f32[132,512]{1,0:T(8,128)} %pack.7.refs_0_.refs_3_), channel_id=1, source_target_pairs={{0,1},{1,0},{2,3},{3,2},{4,5},{5,4},{6,7},{7,6},{8,9},{9,8},{10,11... | collective-permute-start | bytes 811016 | tf_op jit(solution)/shard_map/ppermute | solution.py:204
  12.4 12.4 %copy-start = (f32[132,512]{1,0:T(8,128)}, f32[132,512]{1,0:T(8,128)S(1)}, u32[]{:S(2)}) copy-start(f32[132,512]{1,0:T(8,128)S(1)} %collective-permute-done.2.refs_2_.refs_4_) | copy-start | bytes 811012
  12.5 15.4 %collective-permute-start.4 = (f32[132,512]{1,0:T(8,128)S(1)}, f32[132,512]{1,0:T(8,128)S(1)}, u32[]{:S(2)}, u32[]{:S(2)}) collective-permute-start(f32[132,512]{1,0:T(8,128)S(1)} %collective-permute-done.2.refs_2_.refs_4_), channel_id=1, source_target_pairs={{0,1},{1,0},{2,3},{3,2},{4,5},{5,4},{6,7},{7,6},{8,9},{9,8},{10,11... | collective-permute-start | bytes 811016 | tf_op jit(solution)/shard_map/ppermute | solution.py:204
  21.2 3.6 %copy-start.1 = (f32[132,512]{1,0:T(8,128)}, f32[132,512]{1,0:T(8,128)S(1)}, u32[]{:S(2)}) copy-start(f32[132,512]{1,0:T(8,128)S(1)} %collective-permute-done.1.refs_1_.refs_5_) | copy-start | bytes 811012
  21.2 6.6 %collective-permute-start.5 = (f32[132,512]{1,0:T(8,128)S(1)}, f32[132,512]{1,0:T(8,128)S(1)}, u32[]{:S(2)}, u32[]{:S(2)}) collective-permute-start(f32[132,512]{1,0:T(8,128)S(1)} %collective-permute-done.1.refs_1_.refs_5_), channel_id=1, source_target_pairs={{0,1},{1,0},{2,3},{3,2},{4,5},{5,4},{6,7},{7,6},{8,9},{9,8},{10,11... | collective-permute-start | bytes 811016 | tf_op jit(solution)/shard_map/ppermute | solution.py:204
  21.2 3.6 %copy-start.2 = (f32[132,512]{1,0:T(8,128)}, f32[132,512]{1,0:T(8,128)S(1)}, u32[]{:S(2)}) copy-start(f32[132,512]{1,0:T(8,128)S(1)} %collective-permute-done.refs_0_.refs_6_) | copy-start | bytes 811012
  21.3 6.6 %collective-permute-start.6 = (f32[132,512]{1,0:T(8,128)S(1)}, f32[132,512]{1,0:T(8,128)S(1)}, u32[]{:S(2)}, u32[]{:S(2)}) collective-permute-start(f32[132,512]{1,0:T(8,128)S(1)} %collective-permute-done.refs_0_.refs_6_), channel_id=1, source_target_pairs={{0,1},{1,0},{2,3},{3,2},{4,5},{5,4},{6,7},{7,6},{8,9},{9,8},{10,11... | collective-permute-start | bytes 811016 | tf_op jit(solution)/shard_map/ppermute | solution.py:204
  21.8 0.7 %copy-start.3 = (f32[132,512]{1,0:T(8,128)}, f32[132,512]{1,0:T(8,128)S(1)}, u32[]{:S(2)}) copy-start(f32[132,512]{1,0:T(8,128)S(1)} %collective-permute-done.3.refs_1_.refs_7_) | copy-start | bytes 811012
  27.9 0.7 %copy-start.4 = (f32[132,512]{1,0:T(8,128)}, f32[132,512]{1,0:T(8,128)S(1)}, u32[]{:S(2)}) copy-start(f32[132,512]{1,0:T(8,128)S(1)} %collective-permute-done.4.refs_8_) | copy-start | bytes 811012
  27.9 0.8 %copy-start.5 = (f32[132,512]{1,0:T(8,128)}, f32[132,512]{1,0:T(8,128)S(1)}, u32[]{:S(2)}) copy-start(f32[132,512]{1,0:T(8,128)S(1)} %collective-permute-done.5.refs_9_) | copy-start | bytes 811012
  27.9 0.9 %copy-start.6 = (f32[132,512]{1,0:T(8,128)}, f32[132,512]{1,0:T(8,128)S(1)}, u32[]{:S(2)}) copy-start(f32[132,512]{1,0:T(8,128)S(1)} %collective-permute-done.6.refs_10_) | copy-start | bytes 811012
  40.3 4.8 %collective-permute-start.7 = (f32[32,128]{1,0:T(8,128)}, f32[32,128]{1,0:T(8,128)S(1)}, u32[]{:S(2)}, u32[]{:S(2)}) collective-permute-start(f32[32,128]{1,0:T(8,128)} %get-tuple-element.18), channel_id=1, source_target_pairs={{0,6},{1,7},{2,4},{3,5},{4,2},{5,3},{6,0},{7,1},{8,14},{9,15},{10,... | collective-permute-start | bytes 49160 | tf_op jit(solution)/shard_map/ppermute | solution.py:204
  41.8 3.9 %collective-permute-start.8 = (f32[32,128]{1,0:T(8,128)}, f32[32,128]{1,0:T(8,128)S(1)}, u32[]{:S(2)}, u32[]{:S(2)}) collective-permute-start(f32[32,128]{1,0:T(8,128)} %get-tuple-element.19), channel_id=1, source_target_pairs={{0,4},{1,5},{2,6},{3,7},{4,0},{5,1},{6,2},{7,3},{8,12},{9,13},{10,... | collective-permute-start | bytes 49160 | tf_op jit(solution)/shard_map/ppermute | solution.py:204
  42.1 3.9 %collective-permute-start.9 = (f32[32,128]{1,0:T(8,128)}, f32[32,128]{1,0:T(8,128)S(1)}, u32[]{:S(2)}, u32[]{:S(2)}) collective-permute-start(f32[32,128]{1,0:T(8,128)} %get-tuple-element.20), channel_id=1, source_target_pairs={{0,2},{1,3},{2,0},{3,1},{4,6},{5,7},{6,4},{7,5},{8,10},{9,11},{10,... | collective-permute-start | bytes 49160 | tf_op jit(solution)/shard_map/ppermute | solution.py:204
  46.8 4.6 %collective-permute-start.10 = (f32[16,128]{1,0:T(8,128)S(1)}, f32[16,128]{1,0:T(8,128)S(1)}, u32[]{:S(2)}, u32[]{:S(2)}) collective-permute-start(f32[16,128]{1,0:T(8,128)S(1)} %slice.17), channel_id=1, source_target_pairs={{0,16},{8,24},{16,0},{24,8},{1,17},{9,25},{17,1},{25,9},{2,18},{10... | collective-permute-start | bytes 24584 | tf_op jit(solution)/shard_map/ppermute | solution.py:204
  51.4 3.6 %collective-permute-start.11 = (f32[8,128]{1,0:T(8,128)S(1)}, f32[8,128]{1,0:T(8,128)S(1)}, u32[]{:S(2)}, u32[]{:S(2)}) collective-permute-start(f32[8,128]{1,0:T(8,128)S(1)} %slice.19), channel_id=1, source_target_pairs={{0,8},{8,0},{16,24},{24,16},{1,9},{9,1},{17,25},{25,17},{2,10},{10... | collective-permute-start | bytes 12296 | tf_op jit(solution)/shard_map/ppermute | solution.py:204
where the time goes:
time: 56 us; the launch traced here: 55.6 us
  Pallas kernels  24.9 us (44%)
  waiting for transfers between devices  14.1 us (25%)
  starting transfers between devices  13.6 us (24%)
  local copies, waits for them, and re-layouts  1.6 us (3%)
  other arithmetic  1.32 us (2%)
    ppermute x12, waiting for transfers between devices, swap(): lax.ppermute(value, axis, [(i, i ^ offset) for i in range(lax.axis_size(a...  14.1 us
    ppermute x12, starting transfers between devices, swap(): lax.ppermute(value, axis, [(i, i ^ offset) for i in range(lax.axis_size(a...  13.6 us
    pallas_call x1, Pallas kernels, solve(): pl.pallas_call(functools.partial(solve_kernel, sizes), out_shape=[jax.Sha...  11.6 us
    pallas_call x4, Pallas kernels, pack(): pl.pallas_call(functools.partial(pack_kernel, offsets), out_shape=[block]...  7.95 us
    pallas_call x2, Pallas kernels, gram(): pl.pallas_call(functools.partial(gram_kernel, len(blocks), rows), out_sha...  5.37 us
    unnamed x14, local copies, waits for them, and re-layouts  1.59 us
  transfers between devices with their start and end apart: 12, of which 6 were waited for; matrix products, arithmetic and copies ran while one was open for 0% of the time, Pallas kernels for 20%

commit v1 on v0

--- a/solution.py
+++ b/solution.py
@@ -15,6 +15,22 @@
 
 VMEM = pl.BlockSpec(memory_space=pltpu.VMEM)
 SMEM = pl.BlockSpec(memory_space=pltpu.SMEM)
+
+
+def near(shape):
+    return pltpu.VMEM(shape, jnp.float32)
+
+
+def hold(*values):
+    return [pltpu.with_memory_space_constraint(value, pltpu.VMEM) for value in values]
+
+
+def grant(mebibytes):
+    return pltpu.CompilerParams(vmem_limit_bytes=mebibytes << 20)
+
+
+def cost(microseconds):
+    return pl.CostEstimate(flops=int(microseconds * 1e9), bytes_accessed=0, transcendentals=0)
 
 
 def halves(value):
@@ -45,14 +61,16 @@
 
 def pack(offsets, train_grads, queries):
     rows, _, width = train_grads.shape
-    block = jax.ShapeDtypeStruct((rows + queries.shape[0], width), jnp.float32)
+    block = near((rows + queries.shape[0], width))
     return pl.pallas_call(
         functools.partial(pack_kernel, offsets),
         out_shape=[block] * len(offsets),
         in_specs=[VMEM, VMEM],
         out_specs=[VMEM] * len(offsets),
+        cost_estimate=cost(0.4 * len(offsets)),
+        compiler_params=grant(8),
         name="pack",
-    )(train_grads, queries)
+    )(*hold(train_grads, queries))
 
 
 def add_gram(rows, blocks, left_ref, right_ref, stack):
@@ -83,14 +101,16 @@
     return pl.pallas_call(
         functools.partial(gram_kernel, len(blocks), rows),
         out_shape=[
-            jax.ShapeDtypeStruct((half, half), jnp.float32),
-            jax.ShapeDtypeStruct((width, half), jnp.float32),
+            near((half, half)),
+            near((width, half)),
         ],
         in_specs=[VMEM] * (len(blocks) + len(given)),
         out_specs=[VMEM] * 2,
         scratch_shapes=[pltpu.VMEM((len(blocks) * rows, width), jnp.float32)],
+        cost_estimate=cost(0.4 * len(blocks)),
+        compiler_params=grant(16),
         name="gram",
-    )(*blocks, *given)
+    )(*hold(*blocks, *given))
 
 
 def solve_kernel(sizes, *refs):
@@ -184,7 +204,7 @@
     total_queries = chips * CORES * per_device
     return pl.pallas_call(
         functools.partial(solve_kernel, sizes),
-        out_shape=[jax.ShapeDtypeStruct((total_queries, rows), jnp.float32)] * chips,
+        out_shape=[near((total_queries, rows))] * chips,
         in_specs=[SMEM] + [VMEM] * (2 + 2 * chips),
         out_specs=[VMEM] * chips,
         scratch_shapes=[
@@ -196,8 +216,10 @@
             pltpu.VMEM((width + total_queries, width), jnp.bfloat16),
             pltpu.VMEM((total_queries, width), jnp.float32),
         ],
+        cost_estimate=cost(9.0),
+        compiler_params=grant(24),
         name="solve",
-    )(damping, *given, *arrived, *passed)
+    )(damping, *hold(*given, *arrived, *passed))
 
 
 def swap(value, axis, offset):

time: 56 us -> 47 us (0.84)
  Pallas kernels: 24.9 us -> 11.3 us
  waiting for transfers between devices: 14.1 us -> 19.1 us
  local copies, waits for them, and re-layouts: 1.6 us -> 2.65 us
  other arithmetic: 1.32 us -> 0.61 us
  starting transfers between devices: 13.6 us -> 13 us
    pallas_call x4, Pallas kernels: 7.95 us -> 0.24 us  [pack(): pl.pallas_call(functools.partial(pack_kernel, offsets), out_shape=[block]...]
    ppermute x12, waiting for transfers between devices: 14.1 us -> 19.1 us  [swap(): lax.ppermute(value, axis, [(i, i ^ offset) for i in range(lax.axis_size(a...]
    pallas_call x2, Pallas kernels: 5.37 us -> 1.33 us  [gram(): pl.pallas_call(functools.partial(gram_kernel, len(blocks), rows), out_sha...]
    pallas_call x1, Pallas kernels: 11.6 us -> 9.72 us  [solve(): pl.pallas_call(functools.partial(solve_kernel, sizes), out_shape=[near((t...]
    unnamed x14 -> x6, local copies, waits for them, and re-layouts: 1.59 us -> 2.64 us
    add x1, other arithmetic: 0.73 us -> 0.01 us  [per_device(): total = total + swap(scores[offset], 'dp', offset * CORES)]
    ppermute x12, starting transfers between devices: 13.6 us -> 13 us  [swap(): lax.ppermute(value, axis, [(i, i ^ offset) for i in range(lax.axis_size(a...]
  transfers between devices with their start and end apart: 12 -> 12, of which waited for: 6 -> 8; matrix products, arithmetic and copies ran while one was open for 0% -> 0% of each run, Pallas kernels for 20% -> 3%
where the time goes in v1:
time: 47 us; the launch traced here: 46.8 us
  waiting for transfers between devices  19.1 us (41%)
  starting transfers between devices  13 us (28%)
  Pallas kernels  11.3 us (24%)
  local copies, waits for them, and re-layouts  2.65 us (6%)
  other arithmetic  0.61 us (1%)
    ppermute x12, waiting for transfers between devices, swap(): lax.ppermute(value, axis, [(i, i ^ offset) for i in range(lax.axis_size(a...  19.1 us
    ppermute x12, starting transfers between devices, swap(): lax.ppermute(value, axis, [(i, i ^ offset) for i in range(lax.axis_size(a...  13 us
    pallas_call x1, Pallas kernels, solve(): pl.pallas_call(functools.partial(solve_kernel, sizes), out_shape=[near((t...  9.72 us
    unnamed x6, local copies, waits for them, and re-layouts  2.64 us
    pallas_call x2, Pallas kernels, gram(): pl.pallas_call(functools.partial(gram_kernel, len(blocks), rows), out_sha...  1.33 us
  transfers between devices with their start and end apart: 12, of which 8 were waited for; matrix products, arithmetic and copies ran while one was open for 0% of the time, Pallas kernels for 3%

profile of v1, /device:TPU:0, one launch (start us, length us, event | category | flops | bytes accessed | tf_op | source)
XLA Modules:
  0.0 46.8 jit_solution(809224654408247503)
XLA Ops:
  0.0 0.0 copy-start
  0.0 1.2 %copy-done = f32[128,4,512]{2,1,0:T(4,128)S(1)} copy-done((f32[128,4,512]{2,1,0:T(4,128)S(1)}, f32[128,4,512]{2,1,0:T(4,128)}, u32[]{:S(2)}) %copy-start) | copy-done | bytes 1048600
  1.2 0.0 copy-start.1
  1.2 0.8 %copy-done.1 = f32[4,4,512]{2,1,0:T(4,128)S(1)} copy-done((f32[4,4,512]{2,1,0:T(4,128)S(1)}, f32[4,4,512]{2,1,0:T(4,128)}, u32[]{:S(2)}) %copy-start.1) | copy-done | bytes 32792
  2.0 0.1 pack.5
  2.0 3.1 %collective-permute-start.1 = (f32[132,512]{1,0:T(8,128)S(1)}, f32[132,512]{1,0:T(8,128)S(1)}, u32[]{:S(2)}, u32[]{:S(2)}) collective-permute-start(f32[132,512]{1,0:T(8,128)S(1)} %pack.5), channel_id=1, source_target_pairs={{0,4},{1,5},{2,6},{3,7},{4,0},{5,1},{6,2},{7,3},{8,12},{9,13},{10,... | collective-permute-start | bytes 811016 | tf_op jit(solution)/shard_map/ppermute | solution.py:226
  5.1 0.1 pack.6
  5.2 1.6 %collective-permute-start.2 = (f32[132,512]{1,0:T(8,128)S(1)}, f32[132,512]{1,0:T(8,128)S(1)}, u32[]{:S(2)}, u32[]{:S(2)}) collective-permute-start(f32[132,512]{1,0:T(8,128)S(1)} %pack.6), channel_id=1, source_target_pairs={{0,2},{1,3},{2,0},{3,1},{4,6},{5,7},{6,4},{7,5},{8,10},{9,11},{10,... | collective-permute-start | bytes 811016 | tf_op jit(solution)/shard_map/ppermute | solution.py:226
  6.7 0.1 pack.4
  6.8 0.1 collective-permute-start
  6.9 0.1 pack.7.refs_0_.refs_3_
  6.9 0.1 collective-permute-start.3
  7.0 7.7 %collective-permute-done.2.refs_2_.refs_4_ = f32[132,512]{1,0:T(8,128)S(1)} collective-permute-done((f32[132,512]{1,0:T(8,128)S(1)}, f32[132,512]{1,0:T(8,128)S(1)}, u32[]{:S(2)}, u32[]{:S(2)}) %collective-permute-start.2) | collective-permute-done | bytes 270368 | tf_op jit(solution)/shard_map/ppermute | solution.py:226
  14.8 0.0 collective-permute-start.4
  14.8 0.0 collective-permute-done.1.refs_1_.refs_5_
  14.8 0.5 %collective-permute-start.5 = (f32[132,512]{1,0:T(8,128)S(1)}, f32[132,512]{1,0:T(8,128)S(1)}, u32[]{:S(2)}, u32[]{:S(2)}) collective-permute-start(f32[132,512]{1,0:T(8,128)S(1)} %collective-permute-done.1.refs_1_.refs_5_), channel_id=1, source_target_pairs={{0,1},{1,0},{2,3},{3,2},{4,5},{5,4},{6,7},{7,6},{8,9},{9,8},{10,11... | collective-permute-start | bytes 811016 | tf_op jit(solution)/shard_map/ppermute | solution.py:226
  15.3 3.8 %collective-permute-done.refs_0_.refs_6_ = f32[132,512]{1,0:T(8,128)S(1)} collective-permute-done((f32[132,512]{1,0:T(8,128)S(1)}, f32[132,512]{1,0:T(8,128)S(1)}, u32[]{:S(2)}, u32[]{:S(2)}) %collective-permute-start) | collective-permute-done | bytes 270368 | tf_op jit(solution)/shard_map/ppermute | solution.py:226
  19.1 0.0 collective-permute-start.6
  19.1 0.0 collective-permute-done.3.refs_1_.refs_7_
  19.1 0.5 %gram.2 = (f32[256,256]{1,0:T(8,128)S(1)}, f32[512,256]{1,0:T(8,128)S(1)}) custom-call(f32[132,512]{1,0:T(8,128)S(1)} %pack.7.refs_0_.refs_3_, f32[132,512]{1,0:T(8,128)S(1)} %collective-permute-done.3.refs_1_.refs_7_), custom_call_target="tpu_custom_call" | custom-call | flops 800000000 | tf_op jit(solution)/shard_map/gram/pallas_call | solution.py:101
  19.6 0.8 %gram.3 = (f32[256,256]{1,0:T(8,128)S(1)}, f32[512,256]{1,0:T(8,128)S(1)}) custom-call(f32[132,512]{1,0:T(8,128)S(1)} %collective-permute-done.refs_0_.refs_6_, f32[132,512]{1,0:T(8,128)S(1)} %collective-permute-done.1.refs_1_.refs_5_, f32[132,512]{1,0:T(8,128)S(1)} %collective-permute-done.2.refs_2_.refs_4_, f32[256,256]{1,0:T(8,128)S(1)} %get-tuple-element.13.refs_3_, ...), custom_call_target="tpu_custom_call" | custom-call | flops 1200000000 | tf_op jit(solution)/shard_map/gram/pallas_call | solution.py:101
  20.4 0.0 collective-permute-done.4.refs_8_
  20.4 0.0 collective-permute-done.5.refs_9_
  20.4 0.2 collective-permute-done.6.refs_10_
  20.6 0.0 copy-start.2
  20.6 0.7 %copy-done.2 = f32[4]{0:T(128)S(1)} copy-done((f32[4]{0:T(128)S(1)}, f32[4]{0:T(128)}, u32[]{:S(2)}) %copy-start.2) | copy-done | bytes 40
  21.3 9.7 %solve.1 = (f32[32,128]{1,0:T(8,128)S(1)}, f32[32,128]{1,0:T(8,128)S(1)}, f32[32,128]{1,0:T(8,128)S(1)}, f32[32,128]{1,0:T(8,128)S(1)}) custom-call(f32[4]{0:T(128)S(1)} %copy-done.2, f32[256,256]{1,0:T(8,128)S(1)} %get-tuple-element.15.refs_1_, f32[512,256]{1,0:T(8,128)S(1)} %get-tuple-element.16.refs_2_, f32[132,512]{1,0:T(8,128)S(1)} %pack.7.refs_0_.refs_3_, ...), custom_call_target="tpu_custom_call" | custom-call | flops 8999999488 | tf_op jit(solution)/shard_map/solve/pallas_call | solution.py:205
  31.0 2.7 %collective-permute-start.7 = (f32[32,128]{1,0:T(8,128)S(1)}, f32[32,128]{1,0:T(8,128)S(1)}, u32[]{:S(2)}, u32[]{:S(2)}) collective-permute-start(f32[32,128]{1,0:T(8,128)S(1)} %get-tuple-element.18), channel_id=1, source_target_pairs={{0,6},{1,7},{2,4},{3,5},{4,2},{5,3},{6,0},{7,1},{8,14},{9,15},{10,... | collective-permute-start | bytes 49160 | tf_op jit(solution)/shard_map/ppermute | solution.py:226
  33.7 0.5 %collective-permute-start.8 = (f32[32,128]{1,0:T(8,128)S(1)}, f32[32,128]{1,0:T(8,128)S(1)}, u32[]{:S(2)}, u32[]{:S(2)}) collective-permute-start(f32[32,128]{1,0:T(8,128)S(1)} %get-tuple-element.19), channel_id=1, source_target_pairs={{0,4},{1,5},{2,6},{3,7},{4,0},{5,1},{6,2},{7,3},{8,12},{9,13},{10,... | collective-permute-start | bytes 49160 | tf_op jit(solution)/shard_map/ppermute | solution.py:226
  34.2 0.3 collective-permute-start.9
  34.5 1.1 %collective-permute-done.7 = f32[32,128]{1,0:T(8,128)S(1)} collective-permute-done((f32[32,128]{1,0:T(8,128)S(1)}, f32[32,128]{1,0:T(8,128)S(1)}, u32[]{:S(2)}, u32[]{:S(2)}) %collective-permute-start.7) | collective-permute-done | bytes 16416 | tf_op jit(solution)/shard_map/ppermute | solution.py:226
  35.7 1.7 %collective-permute-done.8 = f32[32,128]{1,0:T(8,128)S(1)} collective-permute-done((f32[32,128]{1,0:T(8,128)S(1)}, f32[32,128]{1,0:T(8,128)S(1)}, u32[]{:S(2)}, u32[]{:S(2)}) %collective-permute-start.8) | collective-permute-done | bytes 16416 | tf_op jit(solution)/shard_map/ppermute | solution.py:226
  37.4 0.5 %collective-permute-done.9 = f32[32,128]{1,0:T(8,128)S(1)} collective-permute-done((f32[32,128]{1,0:T(8,128)S(1)}, f32[32,128]{1,0:T(8,128)S(1)}, u32[]{:S(2)}, u32[]{:S(2)}) %collective-permute-start.9) | collective-permute-done | bytes 16416 | tf_op jit(solution)/shard_map/ppermute | solution.py:226
  37.9 2.7 %collective-permute-start.10 = (f32[16,128]{1,0:T(8,128)S(1)}, f32[16,128]{1,0:T(8,128)S(1)}, u32[]{:S(2)}, u32[]{:S(2)}) collective-permute-start(f32[16,128]{1,0:T(8,128)S(1)} %slice.17), channel_id=1, source_target_pairs={{0,16},{8,24},{16,0},{24,8},{1,17},{9,25},{17,1},{25,9},{2,18},{10... | collective-permute-start | bytes 24584 | tf_op jit(solution)/shard_map/ppermute | solution.py:226
  40.6 2.0 %collective-permute-done.10 = f32[16,128]{1,0:T(8,128)S(1)} collective-permute-done((f32[16,128]{1,0:T(8,128)S(1)}, f32[16,128]{1,0:T(8,128)S(1)}, u32[]{:S(2)}, u32[]{:S(2)}) %collective-permute-start.10) | collective-permute-done | bytes 8224 | tf_op jit(solution)/shard_map/ppermute | solution.py:226
  42.6 1.6 %collective-permute-start.11 = (f32[8,128]{1,0:T(8,128)S(1)}, f32[8,128]{1,0:T(8,128)S(1)}, u32[]{:S(2)}, u32[]{:S(2)}) collective-permute-start(f32[8,128]{1,0:T(8,128)S(1)} %slice.19), channel_id=1, source_target_pairs={{0,8},{8,0},{16,24},{24,16},{1,9},{9,1},{17,25},{25,17},{2,10},{10... | collective-permute-start | bytes 12296 | tf_op jit(solution)/shard_map/ppermute | solution.py:226
  44.1 2.0 %collective-permute-done.11 = f32[8,128]{1,0:T(8,128)S(1)} collective-permute-done((f32[8,128]{1,0:T(8,128)S(1)}, f32[8,128]{1,0:T(8,128)S(1)}, u32[]{:S(2)}, u32[]{:S(2)}) %collective-permute-start.11) | collective-permute-done | bytes 4128 | tf_op jit(solution)/shard_map/ppermute | solution.py:226
  46.2 0.6 %fusion = f32[128,8]{0,1:T(8,128)} fusion(f32[8,128]{1,0:T(8,128)S(1)} %collective-permute-done.11, f32[16,128]{1,0:T(8,128)S(1)} %slice_add_fusion), kind=kLoop, calls=%fused_computation.3 | loop fusion | flops 1024 | bytes 12288 | tf_op jit(solution)/shard_map/transpose | solution.py:265
  (4 shorter events, 0.0 us)
Async XLA Ops:
  0.0 1.2 %copy-start = (f32[128,4,512]{2,1,0:T(4,128)S(1)}, f32[128,4,512]{2,1,0:T(4,128)}, u32[]{:S(2)}) copy-start(f32[128,4,512]{2,1,0:T(4,128)} %rows_ref.7) | copy-start | bytes 3145732
  1.2 0.8 %copy-start.1 = (f32[4,4,512]{2,1,0:T(4,128)S(1)}, f32[4,4,512]{2,1,0:T(4,128)}, u32[]{:S(2)}) copy-start(f32[4,4,512]{2,1,0:T(4,128)} %queries_ref.7) | copy-start | bytes 98308
  2.0 12.7 %collective-permute-start.1 = (f32[132,512]{1,0:T(8,128)S(1)}, f32[132,512]{1,0:T(8,128)S(1)}, u32[]{:S(2)}, u32[]{:S(2)}) collective-permute-start(f32[132,512]{1,0:T(8,128)S(1)} %pack.5), channel_id=1, source_target_pairs={{0,4},{1,5},{2,6},{3,7},{4,0},{5,1},{6,2},{7,3},{8,12},{9,13},{10,... | collective-permute-start | bytes 811016 | tf_op jit(solution)/shard_map/ppermute | solution.py:226
  5.2 9.6 %collective-permute-start.2 = (f32[132,512]{1,0:T(8,128)S(1)}, f32[132,512]{1,0:T(8,128)S(1)}, u32[]{:S(2)}, u32[]{:S(2)}) collective-permute-start(f32[132,512]{1,0:T(8,128)S(1)} %pack.6), channel_id=1, source_target_pairs={{0,2},{1,3},{2,0},{3,1},{4,6},{5,7},{6,4},{7,5},{8,10},{9,11},{10,... | collective-permute-start | bytes 811016 | tf_op jit(solution)/shard_map/ppermute | solution.py:226
  6.8 12.3 %collective-permute-start = (f32[132,512]{1,0:T(8,128)S(1)}, f32[132,512]{1,0:T(8,128)S(1)}, u32[]{:S(2)}, u32[]{:S(2)}) collective-permute-start(f32[132,512]{1,0:T(8,128)S(1)} %pack.4), channel_id=1, source_target_pairs={{0,6},{1,7},{2,4},{3,5},{4,2},{5,3},{6,0},{7,1},{8,14},{9,15},{10,... | collective-permute-start | bytes 811016 | tf_op jit(solution)/shard_map/ppermute | solution.py:226
  6.9 12.1 %collective-permute-start.3 = (f32[132,512]{1,0:T(8,128)S(1)}, f32[132,512]{1,0:T(8,128)S(1)}, u32[]{:S(2)}, u32[]{:S(2)}) collective-permute-start(f32[132,512]{1,0:T(8,128)S(1)} %pack.7.refs_0_.refs_3_), channel_id=1, source_target_pairs={{0,1},{1,0},{2,3},{3,2},{4,5},{5,4},{6,7},{7,6},{8,9},{9,8},{10,11... | collective-permute-start | bytes 811016 | tf_op jit(solution)/shard_map/ppermute | solution.py:226
  14.8 5.7 %collective-permute-start.4 = (f32[132,512]{1,0:T(8,128)S(1)}, f32[132,512]{1,0:T(8,128)S(1)}, u32[]{:S(2)}, u32[]{:S(2)}) collective-permute-start(f32[132,512]{1,0:T(8,128)S(1)} %collective-permute-done.2.refs_2_.refs_4_), channel_id=1, source_target_pairs={{0,1},{1,0},{2,3},{3,2},{4,5},{5,4},{6,7},{7,6},{8,9},{9,8},{10,11... | collective-permute-start | bytes 811016 | tf_op jit(solution)/shard_map/ppermute | solution.py:226
  14.8 5.7 %collective-permute-start.5 = (f32[132,512]{1,0:T(8,128)S(1)}, f32[132,512]{1,0:T(8,128)S(1)}, u32[]{:S(2)}, u32[]{:S(2)}) collective-permute-start(f32[132,512]{1,0:T(8,128)S(1)} %collective-permute-done.1.refs_1_.refs_5_), channel_id=1, source_target_pairs={{0,1},{1,0},{2,3},{3,2},{4,5},{5,4},{6,7},{7,6},{8,9},{9,8},{10,11... | collective-permute-start | bytes 811016 | tf_op jit(solution)/shard_map/ppermute | solution.py:226
  19.1 1.6 %collective-permute-start.6 = (f32[132,512]{1,0:T(8,128)S(1)}, f32[132,512]{1,0:T(8,128)S(1)}, u32[]{:S(2)}, u32[]{:S(2)}) collective-permute-start(f32[132,512]{1,0:T(8,128)S(1)} %collective-permute-done.refs_0_.refs_6_), channel_id=1, source_target_pairs={{0,1},{1,0},{2,3},{3,2},{4,5},{5,4},{6,7},{7,6},{8,9},{9,8},{10,11... | collective-permute-start | bytes 811016 | tf_op jit(solution)/shard_map/ppermute | solution.py:226
  20.6 0.7 %copy-start.2 = (f32[4]{0:T(128)S(1)}, f32[4]{0:T(128)}, u32[]{:S(2)}) copy-start(f32[4]{0:T(128)} %refs_0_.1) | copy-start | bytes 52
  31.0 4.7 %collective-permute-start.7 = (f32[32,128]{1,0:T(8,128)S(1)}, f32[32,128]{1,0:T(8,128)S(1)}, u32[]{:S(2)}, u32[]{:S(2)}) collective-permute-start(f32[32,128]{1,0:T(8,128)S(1)} %get-tuple-element.18), channel_id=1, source_target_pairs={{0,6},{1,7},{2,4},{3,5},{4,2},{5,3},{6,0},{7,1},{8,14},{9,15},{10,... | collective-permute-start | bytes 49160 | tf_op jit(solution)/shard_map/ppermute | solution.py:226
  33.7 3.7 %collective-permute-start.8 = (f32[32,128]{1,0:T(8,128)S(1)}, f32[32,128]{1,0:T(8,128)S(1)}, u32[]{:S(2)}, u32[]{:S(2)}) collective-permute-start(f32[32,128]{1,0:T(8,128)S(1)} %get-tuple-element.19), channel_id=1, source_target_pairs={{0,4},{1,5},{2,6},{3,7},{4,0},{5,1},{6,2},{7,3},{8,12},{9,13},{10,... | collective-permute-start | bytes 49160 | tf_op jit(solution)/shard_map/ppermute | solution.py:226
  34.2 3.7 %collective-permute-start.9 = (f32[32,128]{1,0:T(8,128)S(1)}, f32[32,128]{1,0:T(8,128)S(1)}, u32[]{:S(2)}, u32[]{:S(2)}) collective-permute-start(f32[32,128]{1,0:T(8,128)S(1)} %get-tuple-element.20), channel_id=1, source_target_pairs={{0,2},{1,3},{2,0},{3,1},{4,6},{5,7},{6,4},{7,5},{8,10},{9,11},{10,... | collective-permute-start | bytes 49160 | tf_op jit(solution)/shard_map/ppermute | solution.py:226
  37.9 4.6 %collective-permute-start.10 = (f32[16,128]{1,0:T(8,128)S(1)}, f32[16,128]{1,0:T(8,128)S(1)}, u32[]{:S(2)}, u32[]{:S(2)}) collective-permute-start(f32[16,128]{1,0:T(8,128)S(1)} %slice.17), channel_id=1, source_target_pairs={{0,16},{8,24},{16,0},{24,8},{1,17},{9,25},{17,1},{25,9},{2,18},{10... | collective-permute-start | bytes 24584 | tf_op jit(solution)/shard_map/ppermute | solution.py:226
  42.6 3.6 %collective-permute-start.11 = (f32[8,128]{1,0:T(8,128)S(1)}, f32[8,128]{1,0:T(8,128)S(1)}, u32[]{:S(2)}, u32[]{:S(2)}) collective-permute-start(f32[8,128]{1,0:T(8,128)S(1)} %slice.19), channel_id=1, source_target_pairs={{0,8},{8,0},{16,24},{24,16},{1,9},{9,1},{17,25},{25,17},{2,10},{10... | collective-permute-start | bytes 12296 | tf_op jit(solution)/shard_map/ppermute | solution.py:226

commit v2 on v1

v2 whole, which is shorter than its diff:
```python
import functools
import math

import jax
import jax.numpy as jnp
from jax import lax
from jax.experimental import pallas as pl
from jax.experimental.pallas import tpu as pltpu
from jax.sharding import PartitionSpec as P

NEWTON_STEPS = 8
CORES = 2
SOLVER = 1
PIECES = 4

epsilon = 1e-06

VMEM = pl.BlockSpec(memory_space=pltpu.VMEM)
SMEM = pl.BlockSpec(memory_space=pltpu.SMEM)
HBM = pl.BlockSpec(memory_space=pltpu.HBM)


def near(shape):
    return pltpu.VMEM(shape, jnp.float32)


def hold(*values):
    return [pltpu.with_memory_space_constraint(value, pltpu.VMEM) for value in values]


def grant(mebibytes):
    return pltpu.CompilerParams(vmem_limit_bytes=mebibytes << 20)


def cost(microseconds):
    return pl.CostEstimate(flops=int(microseconds * 1e9), bytes_accessed=0, transcendentals=0)


def halves(value):
    high = value.astype(jnp.bfloat16)
    return high, (value - high.astype(jnp.float32)).astype(jnp.bfloat16)


def product(left, right, dims=(((1,), (0,)), ((), ()))):
    return lax.dot_general(left, right, dims, preferred_element_type=jnp.float32)


def product_3(left_high, left_low, right_high, right_low, dims=(((1,), (0,)), ((), ()))):
    return (
        product(left_high, right_high, dims)
        + product(left_high, right_low, dims)
        + product(left_low, right_high, dims)
    )


def pack_kernel(rows_ref, queries_ref, *refs):
    rows, queries, row_sems, query_sem = refs[-4:]
    blocks = refs[:-4]
    chip = lax.axis_index("dp") // CORES
    total = rows_ref.shape[0]
    step = total // PIECES
    query_copy = pltpu.make_async_copy(queries_ref, queries, query_sem)
    copies = [
        pltpu.make_async_copy(
            rows_ref.at[pl.ds(piece * step, step)],
            rows.at[pl.ds(piece * step, step)],
            row_sems.at[piece],
        )
        for piece in range(PIECES)
    ]
    for copy in copies:
        copy.start()
    query_copy.start()
    modules = [lax.bitwise_xor(chip, jnp.int32(offset)) for offset in range(len(blocks))]
    for piece, copy in enumerate(copies):
        copy.wait()
        here = slice(piece * step, (piece + 1) * step)
        for module, block in zip(modules, blocks):
            block[here] = rows[here, module, :]
    query_copy.wait()
    for module, block in zip(modules, blocks):
        block[total:] = queries[:, module, :]


def pack(train_grads, queries):
    rows, modules, width = train_grads.shape
    return pl.pallas_call(
        pack_kernel,
        out_shape=[near((rows + queries.shape[0], width))] * modules,
        in_specs=[HBM, HBM],
        out_specs=[VMEM] * modules,
        scratch_shapes=[
            pltpu.VMEM(train_grads.shape, jnp.float32),
            pltpu.VMEM(queries.shape, jnp.float32),
            pltpu.SemaphoreType.DMA((PIECES,)),
            pltpu.SemaphoreType.DMA,
        ],
        compiler_params=grant(16),
        cost_estimate=cost(1.5),
        name="pack",
    )(*(pltpu.with_memory_space_constraint(value, pltpu.HBM) for value in (train_grads, queries)))


def add_gram(rows, blocks, left_ref, right_ref, stack):
    half = left_ref.shape[0]
    for place, block in enumerate(blocks):
        stack[place * rows : (place + 1) * rows] = block[0:rows]
    high, low = halves(stack[...])
    dims = (((0,), (0,)), ((), ()))
    left_ref[...] += product_3(high[:, :half], low[:, :half], high[:, :half], low[:, :half], dims)
    right_ref[...] += product_3(high, low, high[:, half:], low[:, half:], dims)


def first_gram_kernel(rows, damping_ref, one, two, left_ref, right_ref, damp_ref, stack):
    chip = lax.axis_index("dp") // CORES
    damp_ref[...] = jnp.full(damp_ref.shape, damping_ref[chip], jnp.float32)
    left_ref[...] = jnp.zeros_like(left_ref)
    right_ref[...] = jnp.zeros_like(right_ref)
    add_gram(rows, (one, two), left_ref, right_ref, stack)


def gram_kernel(rows, one, two, given_left, given_right, left_ref, right_ref, stack):
    left_ref[...] = given_left[...]
    right_ref[...] = given_right[...]
    add_gram(rows, (one, two), left_ref, right_ref, stack)


def gram(rows, pair, given=(), damping=None):
    width = pair[0].shape[1]
    half = width // 2
    shapes = [near((half, half)), near((width, half))]
    first = damping is not None
    return pl.pallas_call(
        functools.partial(first_gram_kernel if first else gram_kernel, rows),
        out_shape=shapes + [near((8, 128))] * first,
        in_specs=[SMEM] * first + [VMEM] * (2 + len(given)),
        out_specs=[VMEM] * (2 + first),
        scratch_shapes=[pltpu.VMEM((2 * rows, width), jnp.float32)],
        compiler_params=grant(16),
        cost_estimate=cost(0.6),
        name="gram",
    )(*([damping] * first), *hold(*pair, *given))


def solve_kernel(sizes, *refs):
    chips, rows, per_device, groups, total_rows, scale = sizes
    refs = list(refs)
    damp_ref, left_ref, right_ref = refs[:3]
    blocks = [refs[3 + CORES * offset : 3 + CORES * (offset + 1)] for offset in range(chips)]
    scores = refs[3 + CORES * chips : 3 + (CORES + 1) * chips]
    left, right, stack, state, high, low, asked = refs[3 + (CORES + 1) * chips :]
    half = left_ref.shape[0]
    width = 2 * half
    chip = lax.axis_index("dp") // CORES
    pair = CORES * per_device
    total_queries = chips * pair
    group = total_queries // groups
    group_here = lax.axis_index("mod")

    for offset in range(chips):
        source = lax.bitwise_xor(chip, jnp.int32(offset))
        asked[pl.ds(pl.multiple_of(source * pair, pair), pair)] = jnp.concatenate(
            [block[rows : rows + per_device] for block in blocks[offset]], 0
        )

    left[...] = left_ref[...]
    right[...] = right_ref[...]
    add_gram(rows, blocks[-1], left, right, stack)

    diagonal = lax.broadcasted_iota(jnp.int32, (half, half), 0) == lax.broadcasted_iota(
        jnp.int32, (half, half), 1
    )
    eye = diagonal.astype(jnp.float32)
    first, cross, last = left[...], right[0:half], right[half:]
    trace = jnp.sum((first + last) * eye, keepdims=True).reshape(1, 1) / total_rows
    shift = damp_ref[0:1, 0:1] * trace / width
    first = first / total_rows + shift * eye
    last = last / total_rows + shift * eye
    cross = cross / total_rows
    squares = first * first + last * last + 2.0 * (cross * cross)
    inverse_norm = lax.rsqrt(jnp.sum(squares, keepdims=True).reshape(1, 1) + epsilon)
    cross = cross * inverse_norm
    state[0:half, 0:half] = first * inverse_norm
    state[0:half, half:] = cross
    state[half:width, 0:half] = cross.T
    state[half:width, half:] = last * inverse_norm
    for offset in range(groups):
        source = lax.bitwise_xor(group_here, jnp.int32(offset))
        state[width + offset * group : width + (offset + 1) * group] = (
            asked[pl.ds(pl.multiple_of(source * group, group), group)] * inverse_norm
        )

    for _ in range(NEWTON_STEPS - 1):
        high[...], low[...] = halves(state[...])

        def part(start, stop, column):
            columns = slice(column, column + half)
            return product_3(
                high[start:stop],
                low[start:stop],
                high[0:width, columns],
                low[0:width, columns],
            )

        state[0:half, 0:half] = 2.0 * state[0:half, 0:half] - part(0, half, 0)
        new = 2.0 * state[0:width, half:] - part(0, width, half)
        state[0:width, half:] = new
        state[half:width, 0:half] = new[0:half].T
        state[width:, 0:half] = 2.0 * state[width:, 0:half] - part(width, width + total_queries, 0)
        state[width:, half:] = 2.0 * state[width:, half:] - part(width, width + total_queries, half)

    high[...], low[...] = halves(state[...])
    conditioned = 2.0 * state[width:] - product_3(
        high[width:], low[width:], high[0:width], low[0:width]
    )
    conditioned_high, conditioned_low = halves(conditioned * scale)
    for offset in range(chips):
        for place, block in enumerate(blocks[offset]):
            block_high, block_low = halves(block[0:rows])
            scores[offset][:, place * rows : (place + 1) * rows] = product_3(
                conditioned_high, conditioned_low, block_high, block_low, (((1,), (1,)), ((), ()))
            )


def solve(sizes, damp, given, blocks):
    chips, rows, per_device = sizes[:3]
    width = blocks[0].shape[1]
    half = width // 2
    total_queries = chips * CORES * per_device
    return pl.pallas_call(
        functools.partial(solve_kernel, sizes),
        out_shape=[near((total_queries, CORES * rows))] * chips,
        in_specs=[VMEM] * (3 + CORES * chips),
        out_specs=[VMEM] * chips,
        scratch_shapes=[
            pltpu.VMEM((half, half), jnp.float32),
            pltpu.VMEM((width, half), jnp.float32),
            pltpu.VMEM((CORES * rows, width), jnp.float32),
            pltpu.VMEM((width + total_queries, width), jnp.float32),
            pltpu.VMEM((width + total_queries, width), jnp.bfloat16),
            pltpu.VMEM((width + total_queries, width), jnp.bfloat16),
            pltpu.VMEM((total_queries, width), jnp.float32),
        ],
        compiler_params=grant(24),
        cost_estimate=cost(9.0),
        name="solve",
    )(*hold(damp, *given, *blocks))


def send(value, axis, offset, source=SOLVER, target=SOLVER):
    chips = lax.axis_size("dp") // CORES
    pairs = [
        (CORES * chip + source, CORES * (chip ^ offset) + target) for chip in range(chips)
    ]
    return lax.ppermute(value, axis, pairs)


def swap(value, offset):
    devices, groups = lax.axis_size("dp"), lax.axis_size("mod")
    pairs = [
        (group * devices + device, (group ^ offset) * devices + device)
        for group in range(groups)
        for device in range(SOLVER, devices, CORES)
    ]
    return lax.ppermute(value, ("mod", "dp"), pairs)


def per_device(train_grads, queries, damping):
    rows, modules, width = train_grads.shape
    devices = lax.axis_size("dp")
    groups = lax.axis_size("mod")
    chips = devices // CORES
    packed = pack(train_grads, queries)
    blocks = [[None] * CORES for _ in range(chips)]
    for offset in range(chips):
        for core in range(CORES):
            blocks[offset][core] = (
                packed[0]
                if (offset, core) == (0, SOLVER)
                else send(packed[offset], "dp", offset, source=core)
            )
    *given, damp = gram(rows, blocks[0], damping=damping)
    for offset in range(1, chips - 1):
        given = gram(rows, blocks[offset], given)
    sizes = (
        chips,
        rows,
        queries.shape[0],
        groups,
        rows * devices,
        1.0 / math.sqrt(modules * groups * width),
    )
    scores = solve(sizes, damp, given, sum(blocks, []))
    total = scores[0]
    for offset in range(chips - 1, 0, -1):
        total = total + send(scores[offset], "dp", offset)
    bit = groups // 2
    while bit:
        keep = total.shape[0] // 2
        total = total[:keep] + swap(total[keep:], bit)
        bit //= 2
    own = lax.axis_index("dp") % CORES == SOLVER
    result = jnp.where(
        own, total[:, SOLVER * rows :], send(total[:, :rows], "dp", 0, target=1 - SOLVER)
    )
    return result.T


def solution(mesh):
    return jax.shard_map(
        per_device,
        mesh=mesh,
        in_specs=(P("dp", "mod", None), P("dp", "mod", None), P("mod")),
        out_specs=P("dp", "mod"),
        check_vma=False,
    )
```

time: 47 us -> 58.4 us (1.24)
  waiting for transfers between devices: 19.1 us -> 26.1 us
  starting transfers between devices: 13 us -> 18.5 us
  local copies, waits for them, and re-layouts: 2.65 us -> 0.01 us
  Pallas kernels: 11.3 us -> 12.4 us
    ppermute x12 -> x13, waiting for transfers between devices: 19.1 us -> 26.1 us  [the longest x11 26.1 us: send(): return lax.ppermute(value, axis, pairs)]
    ppermute x12 -> x13, starting transfers between devices: 13 us -> 18.5 us  [the longest x11 17.2 us: send(): return lax.ppermute(value, axis, pairs)]
    unnamed x6 -> x2, local copies, waits for them, and re-layouts: 2.64 us -> 0.01 us
    pallas_call x6 -> x4, Pallas kernels: 1.57 us -> 3.38 us  [the longest x3 2.09 us: gram(): pl.pallas_call(functools.partial(first_gram_kernel if first else gram_ker...]
    pallas_call x1, Pallas kernels: 9.72 us -> 9.02 us  [solve(): pl.pallas_call(functools.partial(solve_kernel, sizes), out_shape=[near((t...]
  transfers between devices with their start and end apart: 12 -> 13, of which waited for: 8 -> 2; matrix products, arithmetic and copies ran while one was open for 0% -> 0% of each run, Pallas kernels for 3% -> 4%
where the time goes in v2:
time: 58.4 us; the launch traced here: 58 us
  waiting for transfers between devices  26.1 us (45%)
  starting transfers between devices  18.5 us (32%)
  Pallas kernels  12.4 us (21%)
  other arithmetic  0.62 us (1%)
    ppermute x11, waiting for transfers between devices, send(): return lax.ppermute(value, axis, pairs)  26.1 us
    ppermute x11, starting transfers between devices, send(): return lax.ppermute(value, axis, pairs)  17.2 us
    pallas_call x1, Pallas kernels, solve(): pl.pallas_call(functools.partial(solve_kernel, sizes), out_shape=[near((t...  9.02 us
    pallas_call x3, Pallas kernels, gram(): pl.pallas_call(functools.partial(first_gram_kernel if first else gram_ker...  2.09 us
    ppermute x2, starting transfers between devices, swap(): return lax.ppermute(value, ('mod', 'dp'), pairs)  1.32 us
    pallas_call x1, Pallas kernels, pack(): pl.pallas_call(pack_kernel, out_shape=[near((rows + queries.shape[0], wid...  1.29 us
  transfers between devices with their start and end apart: 13, of which 2 were waited for; matrix products, arithmetic and copies ran while one was open for 0% of the time, Pallas kernels for 4%

profile of v2, /device:TPU:0, one launch (start us, length us, event | category | flops | bytes accessed | tf_op | source)
XLA Modules:
  0.0 58.0 jit_solution(1176178446659714149)
XLA Ops:
  0.0 1.3 %pack.1 = (f32[132,512]{1,0:T(8,128)S(1)}, f32[132,512]{1,0:T(8,128)S(1)}, f32[132,512]{1,0:T(8,128)S(1)}, f32[132,512]{1,0:T(8,128)S(1)}) custom-call(f32[128,4,512]{2,1,0:T(4,128)} %rows_ref.1, f32[4,4,512]{2,1,0:T(4,128)} %queries_ref.1), custom_call_target="tpu_custom_call" | custom-call | flops 1500000000 | tf_op jit(solution)/shard_map/pack/pallas_call | solution.py:87
  1.3 2.4 %collective-permute-start = (f32[132,512]{1,0:T(8,128)S(1)}, f32[132,512]{1,0:T(8,128)S(1)}, u32[]{:S(2)}, u32[]{:S(2)}) collective-permute-start(f32[132,512]{1,0:T(8,128)S(1)} %get-tuple-element.20.two.refs_4_), channel_id=1, source_target_pairs={{0,1},{2,3},{4,5},{6,7},{8,9},{10,11},{12,13},{14,15},{16,17},{18,... | collective-permute-start | bytes 811016 | tf_op jit(solution)/shard_map/ppermute | solution.py:255
  3.7 3.2 %collective-permute-start.3 = (f32[132,512]{1,0:T(8,128)S(1)}, f32[132,512]{1,0:T(8,128)S(1)}, u32[]{:S(2)}, u32[]{:S(2)}) collective-permute-start(f32[132,512]{1,0:T(8,128)S(1)} %get-tuple-element.23), channel_id=1, source_target_pairs={{0,3},{2,1},{4,7},{6,5},{8,11},{10,9},{12,15},{14,13},{16,19},{18,... | collective-permute-start | bytes 811016 | tf_op jit(solution)/shard_map/ppermute | solution.py:255
  6.9 0.7 %collective-permute-start.4 = (f32[132,512]{1,0:T(8,128)S(1)}, f32[132,512]{1,0:T(8,128)S(1)}, u32[]{:S(2)}, u32[]{:S(2)}) collective-permute-start(f32[132,512]{1,0:T(8,128)S(1)} %get-tuple-element.23), channel_id=1, source_target_pairs={{1,3},{3,1},{5,7},{7,5},{9,11},{11,9},{13,15},{15,13},{17,19},{19,... | collective-permute-start | bytes 811016 | tf_op jit(solution)/shard_map/ppermute | solution.py:255
  7.6 0.0 copy-start
  7.6 3.8 %collective-permute-start.1 = (f32[132,512]{1,0:T(8,128)S(1)}, f32[132,512]{1,0:T(8,128)S(1)}, u32[]{:S(2)}, u32[]{:S(2)}) collective-permute-start(f32[132,512]{1,0:T(8,128)S(1)} %get-tuple-element.22), channel_id=1, source_target_pairs={{0,5},{2,7},{4,1},{6,3},{8,13},{10,15},{12,9},{14,11},{16,21},{18,... | collective-permute-start | bytes 811016 | tf_op jit(solution)/shard_map/ppermute | solution.py:255
  11.4 0.7 %collective-permute-start.2 = (f32[132,512]{1,0:T(8,128)S(1)}, f32[132,512]{1,0:T(8,128)S(1)}, u32[]{:S(2)}, u32[]{:S(2)}) collective-permute-start(f32[132,512]{1,0:T(8,128)S(1)} %get-tuple-element.22), channel_id=1, source_target_pairs={{1,5},{3,7},{5,1},{7,3},{9,13},{11,15},{13,9},{15,11},{17,21},{19,... | collective-permute-start | bytes 811016 | tf_op jit(solution)/shard_map/ppermute | solution.py:255
  12.1 0.0 collective-permute-done.one.refs_3_
  12.1 2.5 %collective-permute-start.5 = (f32[132,512]{1,0:T(8,128)S(1)}, f32[132,512]{1,0:T(8,128)S(1)}, u32[]{:S(2)}, u32[]{:S(2)}) collective-permute-start(f32[132,512]{1,0:T(8,128)S(1)} %get-tuple-element.30), channel_id=1, source_target_pairs={{0,7},{2,5},{4,3},{6,1},{8,15},{10,13},{12,11},{14,9},{16,23},{18,... | collective-permute-start | bytes 811016 | tf_op jit(solution)/shard_map/ppermute | solution.py:255
  14.6 0.0 collective-permute-done.3.one.refs_5_
  14.6 0.7 %collective-permute-start.6 = (f32[132,512]{1,0:T(8,128)S(1)}, f32[132,512]{1,0:T(8,128)S(1)}, u32[]{:S(2)}, u32[]{:S(2)}) collective-permute-start(f32[132,512]{1,0:T(8,128)S(1)} %get-tuple-element.30), channel_id=1, source_target_pairs={{1,7},{3,5},{5,3},{7,1},{9,15},{11,13},{13,11},{15,9},{17,23},{19,... | collective-permute-start | bytes 811016 | tf_op jit(solution)/shard_map/ppermute | solution.py:255
  15.3 0.0 copy-done
  15.3 1.1 %gram.3 = (f32[256,256]{1,0:T(8,128)S(1)}, f32[512,256]{1,0:T(8,128)S(1)}, f32[8,128]{1,0:T(8,128)S(1)}) custom-call(f32[4]{0:T(128)S(1)} %copy-done, f32[132,512]{1,0:T(8,128)S(1)} %collective-permute-done.one.refs_3_, f32[132,512]{1,0:T(8,128)S(1)} %get-tuple-element.20.two.refs_4_), custom_call_target="tpu_custom_call" | custom-call | flops 600000000 | tf_op jit(solution)/shard_map/gram/pallas_call | solution.py:133
  16.4 0.0 collective-permute-done.4.two.refs_6_
  16.4 0.5 gram.4
  16.9 6.6 %collective-permute-done.1.one.refs_7_ = f32[132,512]{1,0:T(8,128)S(1)} collective-permute-done((f32[132,512]{1,0:T(8,128)S(1)}, f32[132,512]{1,0:T(8,128)S(1)}, u32[]{:S(2)}, u32[]{:S(2)}) %collective-permute-start.1) | collective-permute-done | bytes 270368 | tf_op jit(solution)/shard_map/ppermute | solution.py:255
  23.5 0.0 collective-permute-done.2.two.refs_8_
  23.5 0.5 gram.5
  24.0 0.0 collective-permute-done.5.refs_9_
  24.1 0.0 collective-permute-done.6.refs_10_
  24.1 9.0 %solve.1 = (f32[32,256]{1,0:T(8,128)S(1)}, f32[32,256]{1,0:T(8,128)S(1)}, f32[32,256]{1,0:T(8,128)S(1)}, f32[32,256]{1,0:T(8,128)S(1)}) custom-call(f32[8,128]{1,0:T(8,128)S(1)} %get-tuple-element.21.refs_0_, f32[256,256]{1,0:T(8,128)S(1)} %get-tuple-element.28.refs_1_, f32[512,256]{1,0:T(8,128)S(1)} %get-tuple-element.29.refs_2_, ...), custom_call_target="tpu_custom_call" | custom-call | flops 8999999488 | tf_op jit(solution)/shard_map/solve/pallas_call | solution.py:230
  33.1 0.7 %collective-permute-start.9 = (f32[32,256]{1,0:T(8,128)S(1)}, f32[32,256]{1,0:T(8,128)S(1)}, u32[]{:S(2)}, u32[]{:S(2)}) collective-permute-start(f32[32,256]{1,0:T(8,128)S(1)} %get-tuple-element.34), channel_id=1, source_target_pairs={{1,3},{3,1},{5,7},{7,5},{9,11},{11,9},{13,15},{15,13},{17,19},{19,... | collective-permute-start | bytes 98312 | tf_op jit(solution)/shard_map/ppermute | solution.py:255
  33.8 0.7 %collective-permute-start.8 = (f32[32,256]{1,0:T(8,128)S(1)}, f32[32,256]{1,0:T(8,128)S(1)}, u32[]{:S(2)}, u32[]{:S(2)}) collective-permute-start(f32[32,256]{1,0:T(8,128)S(1)} %get-tuple-element.33), channel_id=1, source_target_pairs={{1,5},{3,7},{5,1},{7,3},{9,13},{11,15},{13,9},{15,11},{17,21},{19,... | collective-permute-start | bytes 98312 | tf_op jit(solution)/shard_map/ppermute | solution.py:255
  34.4 0.7 %collective-permute-start.7 = (f32[32,256]{1,0:T(8,128)S(1)}, f32[32,256]{1,0:T(8,128)S(1)}, u32[]{:S(2)}, u32[]{:S(2)}) collective-permute-start(f32[32,256]{1,0:T(8,128)S(1)} %get-tuple-element.32), channel_id=1, source_target_pairs={{1,7},{3,5},{5,3},{7,1},{9,15},{11,13},{13,11},{15,9},{17,23},{19,... | collective-permute-start | bytes 98312 | tf_op jit(solution)/shard_map/ppermute | solution.py:255
  35.1 0.0 collective-permute-done.9
  35.1 0.0 collective-permute-done.8
  35.1 0.0 collective-permute-done.7
  35.2 0.7 %collective-permute-start.10 = (f32[16,256]{1,0:T(8,128)S(1)}, f32[16,256]{1,0:T(8,128)S(1)}, u32[]{:S(2)}, u32[]{:S(2)}) collective-permute-start(f32[16,256]{1,0:T(8,128)S(1)} %slice.25), channel_id=1, source_target_pairs={{1,17},{3,19},{5,21},{7,23},{9,25},{11,27},{13,29},{15,31},{17,1},... | collective-permute-start | bytes 49160 | tf_op jit(solution)/shard_map/ppermute | solution.py:265
  35.8 0.0 collective-permute-done.10
  35.9 0.7 %collective-permute-start.11 = (f32[8,256]{1,0:T(8,128)S(1)}, f32[8,256]{1,0:T(8,128)S(1)}, u32[]{:S(2)}, u32[]{:S(2)}) collective-permute-start(f32[8,256]{1,0:T(8,128)S(1)} %slice.27), channel_id=1, source_target_pairs={{1,9},{3,11},{5,13},{7,15},{9,1},{11,3},{13,5},{15,7},{17,25},{19,... | collective-permute-start | bytes 24584 | tf_op jit(solution)/shard_map/ppermute | solution.py:265
  36.6 0.0 collective-permute-done.11
  36.6 1.3 %collective-permute-start.12 = (f32[8,128]{1,0:T(8,128)S(1)}, f32[8,128]{1,0:T(8,128)S(1)}, u32[]{:S(2)}, u32[]{:S(2)}) collective-permute-start(f32[8,128]{1,0:T(8,128)S(1)} %slice.29), channel_id=1, source_target_pairs={{1,0},{3,2},{5,4},{7,6},{9,8},{11,10},{13,12},{15,14},{17,16},{19,... | collective-permute-start | bytes 12296 | tf_op jit(solution)/shard_map/ppermute | solution.py:255
  37.9 19.5 %collective-permute-done.12 = f32[8,128]{1,0:T(8,128)S(1)} collective-permute-done((f32[8,128]{1,0:T(8,128)S(1)}, f32[8,128]{1,0:T(8,128)S(1)}, u32[]{:S(2)}, u32[]{:S(2)}) %collective-permute-start.12) | collective-permute-done | bytes 4128 | tf_op jit(solution)/shard_map/ppermute | solution.py:255
  57.4 0.6 %fusion = f32[128,8]{0,1:T(8,128)} fusion(f32[8,128]{1,0:T(8,128)S(1)} %collective-permute-done.12, f32[8,256]{1,0:T(8,128)S(1)} %slice_add_fusion.1, pred[]{:T(512)S(6)} %eq.5), kind=kLoop, calls=%fused_computation.4 | loop fusion | flops 1024 | bytes 12289 | tf_op jit(solution)/shard_map/transpose | solution.py:306
  (6 shorter events, 0.0 us)
Async XLA Ops:
  1.3 10.8 %collective-permute-start = (f32[132,512]{1,0:T(8,128)S(1)}, f32[132,512]{1,0:T(8,128)S(1)}, u32[]{:S(2)}, u32[]{:S(2)}) collective-permute-start(f32[132,512]{1,0:T(8,128)S(1)} %get-tuple-element.20.two.refs_4_), channel_id=1, source_target_pairs={{0,1},{2,3},{4,5},{6,7},{8,9},{10,11},{12,13},{14,15},{16,17},{18,... | collective-permute-start | bytes 811016 | tf_op jit(solution)/shard_map/ppermute | solution.py:255
  3.7 10.9 %collective-permute-start.3 = (f32[132,512]{1,0:T(8,128)S(1)}, f32[132,512]{1,0:T(8,128)S(1)}, u32[]{:S(2)}, u32[]{:S(2)}) collective-permute-start(f32[132,512]{1,0:T(8,128)S(1)} %get-tuple-element.23), channel_id=1, source_target_pairs={{0,3},{2,1},{4,7},{6,5},{8,11},{10,9},{12,15},{14,13},{16,19},{18,... | collective-permute-start | bytes 811016 | tf_op jit(solution)/shard_map/ppermute | solution.py:255
  6.9 9.4 %collective-permute-start.4 = (f32[132,512]{1,0:T(8,128)S(1)}, f32[132,512]{1,0:T(8,128)S(1)}, u32[]{:S(2)}, u32[]{:S(2)}) collective-permute-start(f32[132,512]{1,0:T(8,128)S(1)} %get-tuple-element.23), channel_id=1, source_target_pairs={{1,3},{3,1},{5,7},{7,5},{9,11},{11,9},{13,15},{15,13},{17,19},{19,... | collective-permute-start | bytes 811016 | tf_op jit(solution)/shard_map/ppermute | solution.py:255
  7.6 7.7 %copy-start = (f32[4]{0:T(128)S(1)}, f32[4]{0:T(128)}, u32[]{:S(2)}) copy-start(f32[4]{0:T(128)} %damping_ref.1) | copy-start | bytes 52
  7.6 15.9 %collective-permute-start.1 = (f32[132,512]{1,0:T(8,128)S(1)}, f32[132,512]{1,0:T(8,128)S(1)}, u32[]{:S(2)}, u32[]{:S(2)}) collective-permute-start(f32[132,512]{1,0:T(8,128)S(1)} %get-tuple-element.22), channel_id=1, source_target_pairs={{0,5},{2,7},{4,1},{6,3},{8,13},{10,15},{12,9},{14,11},{16,21},{18,... | collective-permute-start | bytes 811016 | tf_op jit(solution)/shard_map/ppermute | solution.py:255
  11.4 12.1 %collective-permute-start.2 = (f32[132,512]{1,0:T(8,128)S(1)}, f32[132,512]{1,0:T(8,128)S(1)}, u32[]{:S(2)}, u32[]{:S(2)}) collective-permute-start(f32[132,512]{1,0:T(8,128)S(1)} %get-tuple-element.22), channel_id=1, source_target_pairs={{1,5},{3,7},{5,1},{7,3},{9,13},{11,15},{13,9},{15,11},{17,21},{19,... | collective-permute-start | bytes 811016 | tf_op jit(solution)/shard_map/ppermute | solution.py:255
  12.1 11.9 %collective-permute-start.5 = (f32[132,512]{1,0:T(8,128)S(1)}, f32[132,512]{1,0:T(8,128)S(1)}, u32[]{:S(2)}, u32[]{:S(2)}) collective-permute-start(f32[132,512]{1,0:T(8,128)S(1)} %get-tuple-element.30), channel_id=1, source_target_pairs={{0,7},{2,5},{4,3},{6,1},{8,15},{10,13},{12,11},{14,9},{16,23},{18,... | collective-permute-start | bytes 811016 | tf_op jit(solution)/shard_map/ppermute | solution.py:255
  14.6 9.4 %collective-permute-start.6 = (f32[132,512]{1,0:T(8,128)S(1)}, f32[132,512]{1,0:T(8,128)S(1)}, u32[]{:S(2)}, u32[]{:S(2)}) collective-permute-start(f32[132,512]{1,0:T(8,128)S(1)} %get-tuple-element.30), channel_id=1, source_target_pairs={{1,7},{3,5},{5,3},{7,1},{9,15},{11,13},{13,11},{15,9},{17,23},{19,... | collective-permute-start | bytes 811016 | tf_op jit(solution)/shard_map/ppermute | solution.py:255
  33.1 2.0 %collective-permute-start.9 = (f32[32,256]{1,0:T(8,128)S(1)}, f32[32,256]{1,0:T(8,128)S(1)}, u32[]{:S(2)}, u32[]{:S(2)}) collective-permute-start(f32[32,256]{1,0:T(8,128)S(1)} %get-tuple-element.34), channel_id=1, source_target_pairs={{1,3},{3,1},{5,7},{7,5},{9,11},{11,9},{13,15},{15,13},{17,19},{19,... | collective-permute-start | bytes 98312 | tf_op jit(solution)/shard_map/ppermute | solution.py:255
  33.8 1.4 %collective-permute-start.8 = (f32[32,256]{1,0:T(8,128)S(1)}, f32[32,256]{1,0:T(8,128)S(1)}, u32[]{:S(2)}, u32[]{:S(2)}) collective-permute-start(f32[32,256]{1,0:T(8,128)S(1)} %get-tuple-element.33), channel_id=1, source_target_pairs={{1,5},{3,7},{5,1},{7,3},{9,13},{11,15},{13,9},{15,11},{17,21},{19,... | collective-permute-start | bytes 98312 | tf_op jit(solution)/shard_map/ppermute | solution.py:255
  34.4 0.7 %collective-permute-start.7 = (f32[32,256]{1,0:T(8,128)S(1)}, f32[32,256]{1,0:T(8,128)S(1)}, u32[]{:S(2)}, u32[]{:S(2)}) collective-permute-start(f32[32,256]{1,0:T(8,128)S(1)} %get-tuple-element.32), channel_id=1, source_target_pairs={{1,7},{3,5},{5,3},{7,1},{9,15},{11,13},{13,11},{15,9},{17,23},{19,... | collective-permute-start | bytes 98312 | tf_op jit(solution)/shard_map/ppermute | solution.py:255
  35.2 0.7 %collective-permute-start.10 = (f32[16,256]{1,0:T(8,128)S(1)}, f32[16,256]{1,0:T(8,128)S(1)}, u32[]{:S(2)}, u32[]{:S(2)}) collective-permute-start(f32[16,256]{1,0:T(8,128)S(1)} %slice.25), channel_id=1, source_target_pairs={{1,17},{3,19},{5,21},{7,23},{9,25},{11,27},{13,29},{15,31},{17,1},... | collective-permute-start | bytes 49160 | tf_op jit(solution)/shard_map/ppermute | solution.py:265
  35.9 0.7 %collective-permute-start.11 = (f32[8,256]{1,0:T(8,128)S(1)}, f32[8,256]{1,0:T(8,128)S(1)}, u32[]{:S(2)}, u32[]{:S(2)}) collective-permute-start(f32[8,256]{1,0:T(8,128)S(1)} %slice.27), channel_id=1, source_target_pairs={{1,9},{3,11},{5,13},{7,15},{9,1},{11,3},{13,5},{15,7},{17,25},{19,... | collective-permute-start | bytes 24584 | tf_op jit(solution)/shard_map/ppermute | solution.py:265
  36.6 20.8 %collective-permute-start.12 = (f32[8,128]{1,0:T(8,128)S(1)}, f32[8,128]{1,0:T(8,128)S(1)}, u32[]{:S(2)}, u32[]{:S(2)}) collective-permute-start(f32[8,128]{1,0:T(8,128)S(1)} %slice.29), channel_id=1, source_target_pairs={{1,0},{3,2},{5,4},{7,6},{9,8},{11,10},{13,12},{15,14},{17,16},{19,... | collective-permute-start | bytes 12296 | tf_op jit(solution)/shard_map/ppermute | solution.py:255

commit v3 on v2

--- a/solution.py
+++ b/solution.py
@@ -111,18 +111,27 @@
     right_ref[...] += product_3(high, low, high[:, half:], low[:, half:], dims)
 
 
+def on_solver(body):
+    pl.when(lax.axis_index("dp") % CORES == SOLVER)(body)
+
+
 def first_gram_kernel(rows, damping_ref, one, two, left_ref, right_ref, damp_ref, stack):
     chip = lax.axis_index("dp") // CORES
     damp_ref[...] = jnp.full(damp_ref.shape, damping_ref[chip], jnp.float32)
-    left_ref[...] = jnp.zeros_like(left_ref)
-    right_ref[...] = jnp.zeros_like(right_ref)
-    add_gram(rows, (one, two), left_ref, right_ref, stack)
+
+    @on_solver
+    def _():
+        left_ref[...] = jnp.zeros_like(left_ref)
+        right_ref[...] = jnp.zeros_like(right_ref)
+        add_gram(rows, (one, two), left_ref, right_ref, stack)
 
 
 def gram_kernel(rows, one, two, given_left, given_right, left_ref, right_ref, stack):
-    left_ref[...] = given_left[...]
-    right_ref[...] = given_right[...]
-    add_gram(rows, (one, two), left_ref, right_ref, stack)
+    @on_solver
+    def _():
+        left_ref[...] = given_left[...]
+        right_ref[...] = given_right[...]
+        add_gram(rows, (one, two), left_ref, right_ref, stack)
 
 
 def gram(rows, pair, given=(), damping=None):
@@ -143,6 +152,18 @@
 
 
 def solve_kernel(sizes, *refs):
+    chips = sizes[0]
+    scores = refs[3 + CORES * chips : 3 + (CORES + 1) * chips]
+
+    @pl.when(lax.axis_index("dp") % CORES != SOLVER)
+    def _():
+        for score in scores:
+            score[...] = jnp.zeros_like(score)
+
+    on_solver(functools.partial(solve_module, sizes, *refs))
+
+
+def solve_module(sizes, *refs):
     chips, rows, per_device, groups, total_rows, scale = sizes
     refs = list(refs)
     damp_ref, left_ref, right_ref = refs[:3]
@@ -247,22 +268,8 @@
     )(*hold(damp, *given, *blocks))
 
 
-def send(value, axis, offset, source=SOLVER, target=SOLVER):
-    chips = lax.axis_size("dp") // CORES
-    pairs = [
-        (CORES * chip + source, CORES * (chip ^ offset) + target) for chip in range(chips)
-    ]
-    return lax.ppermute(value, axis, pairs)
-
-
-def swap(value, offset):
-    devices, groups = lax.axis_size("dp"), lax.axis_size("mod")
-    pairs = [
-        (group * devices + device, (group ^ offset) * devices + device)
-        for group in range(groups)
-        for device in range(SOLVER, devices, CORES)
-    ]
-    return lax.ppermute(value, ("mod", "dp"), pairs)
+def swap(value, axis, offset):
+    return lax.ppermute(value, axis, [(i, i ^ offset) for i in range(lax.axis_size(axis))])
 
 
 def per_device(train_grads, queries, damping):
@@ -271,14 +278,10 @@
     groups = lax.axis_size("mod")
     chips = devices // CORES
     packed = pack(train_grads, queries)
-    blocks = [[None] * CORES for _ in range(chips)]
-    for offset in range(chips):
-        for core in range(CORES):
-            blocks[offset][core] = (
-                packed[0]
-                if (offset, core) == (0, SOLVER)
-                else send(packed[offset], "dp", offset, source=core)
-            )
+    arrived = [packed[0]]
+    for offset in range(1, chips):
+        arrived.append(swap(packed[offset], "dp", CORES * offset))
+    blocks = [[swap(block, "dp", 1), block] for block in arrived]
     *given, damp = gram(rows, blocks[0], damping=damping)
     for offset in range(1, chips - 1):
         given = gram(rows, blocks[offset], given)
@@ -293,16 +296,14 @@
     scores = solve(sizes, damp, given, sum(blocks, []))
     total = scores[0]
     for offset in range(chips - 1, 0, -1):
-        total = total + send(scores[offset], "dp", offset)
+        total = total + swap(scores[offset], "dp", CORES * offset)
     bit = groups // 2
     while bit:
         keep = total.shape[0] // 2
-        total = total[:keep] + swap(total[keep:], bit)
+        total = total[:keep] + swap(total[keep:], "mod", bit)
         bit //= 2
-    own = lax.axis_index("dp") % CORES == SOLVER
-    result = jnp.where(
-        own, total[:, SOLVER * rows :], send(total[:, :rows], "dp", 0, target=1 - SOLVER)
-    )
+    solver = lax.axis_index("dp") % CORES == SOLVER
+    result = jnp.where(solver, total[:, SOLVER * rows :], swap(total[:, :rows], "dp", 1))
     return result.T
 
 

time: 58.4 us -> 43 us (0.74)
  Pallas kernels: 12.4 us -> 1.88 us
  waiting for transfers between devices: 26.1 us -> 21.7 us
    pallas_call x1, Pallas kernels: 9.02 us -> 0.01 us  [solve(): pl.pallas_call(functools.partial(solve_kernel, sizes), out_shape=[near((t...]
    ppermute x13, waiting for transfers between devices: 26.1 us -> 21.7 us  [swap(): lax.ppermute(value, axis, [(i, i ^ offset) for i in range(lax.axis_size(a...]
    pallas_call x3, Pallas kernels: 2.09 us -> 0.58 us  [gram(): pl.pallas_call(functools.partial(first_gram_kernel if first else gram_ker...]
  transfers between devices with their start and end apart: 13 -> 13, of which waited for: 2 -> 10; matrix products, arithmetic and copies ran while one was open for 0% -> 0% of each run, Pallas kernels for 4% -> 1%
where the time goes in v3:
time: 43 us; the launch traced here: 42.9 us
  waiting for transfers between devices  21.7 us (50%)
  starting transfers between devices  18.6 us (43%)
  Pallas kernels  1.88 us (4%)
  other arithmetic  0.61 us (1%)
    ppermute x13, waiting for transfers between devices, swap(): lax.ppermute(value, axis, [(i, i ^ offset) for i in range(lax.axis_size(a...  21.7 us
    ppermute x13, starting transfers between devices, swap(): lax.ppermute(value, axis, [(i, i ^ offset) for i in range(lax.axis_size(a...  18.6 us
    pallas_call x1, Pallas kernels, pack(): pl.pallas_call(pack_kernel, out_shape=[near((rows + queries.shape[0], wid...  1.29 us
  transfers between devices with their start and end apart: 13, of which 10 were waited for; matrix products, arithmetic and copies ran while one was open for 0% of the time, Pallas kernels for 1%

profile of v3, /device:TPU:0, one launch (start us, length us, event | category | flops | bytes accessed | tf_op | source)
XLA Modules:
  0.0 42.9 jit_solution(12511651970161813411)
XLA Ops:
  0.0 1.3 %pack.1 = (f32[132,512]{1,0:T(8,128)S(1)}, f32[132,512]{1,0:T(8,128)S(1)}, f32[132,512]{1,0:T(8,128)S(1)}, f32[132,512]{1,0:T(8,128)S(1)}) custom-call(f32[128,4,512]{2,1,0:T(4,128)} %rows_ref.1, f32[4,4,512]{2,1,0:T(4,128)} %queries_ref.1), custom_call_target="tpu_custom_call" | custom-call | flops 1500000000 | tf_op jit(solution)/shard_map/pack/pallas_call | solution.py:87
  1.3 3.0 %collective-permute-start.3 = (f32[132,512]{1,0:T(8,128)S(1)}, f32[132,512]{1,0:T(8,128)S(1)}, u32[]{:S(2)}, u32[]{:S(2)}) collective-permute-start(f32[132,512]{1,0:T(8,128)S(1)} %get-tuple-element.23), channel_id=1, source_target_pairs={{0,2},{1,3},{2,0},{3,1},{4,6},{5,7},{6,4},{7,5},{8,10},{9,11},{10,... | collective-permute-start | bytes 811016 | tf_op jit(solution)/shard_map/ppermute | solution.py:272
  4.3 1.5 %collective-permute-start.1 = (f32[132,512]{1,0:T(8,128)S(1)}, f32[132,512]{1,0:T(8,128)S(1)}, u32[]{:S(2)}, u32[]{:S(2)}) collective-permute-start(f32[132,512]{1,0:T(8,128)S(1)} %get-tuple-element.22), channel_id=1, source_target_pairs={{0,4},{1,5},{2,6},{3,7},{4,0},{5,1},{6,2},{7,3},{8,12},{9,13},{10,... | collective-permute-start | bytes 811016 | tf_op jit(solution)/shard_map/ppermute | solution.py:272
  5.9 0.0 copy-start
  5.9 0.0 collective-permute-start.5
  5.9 0.0 collective-permute-start
  5.9 6.0 %collective-permute-done.3.two.refs_6_ = f32[132,512]{1,0:T(8,128)S(1)} collective-permute-done((f32[132,512]{1,0:T(8,128)S(1)}, f32[132,512]{1,0:T(8,128)S(1)}, u32[]{:S(2)}, u32[]{:S(2)}) %collective-permute-start.3) | collective-permute-done | bytes 270368 | tf_op jit(solution)/shard_map/ppermute | solution.py:272
  11.8 0.0 collective-permute-start.4
  11.8 6.6 %collective-permute-done.1.two.refs_8_ = f32[132,512]{1,0:T(8,128)S(1)} collective-permute-done((f32[132,512]{1,0:T(8,128)S(1)}, f32[132,512]{1,0:T(8,128)S(1)}, u32[]{:S(2)}, u32[]{:S(2)}) %collective-permute-start.1) | collective-permute-done | bytes 270368 | tf_op jit(solution)/shard_map/ppermute | solution.py:272
  18.4 0.0 collective-permute-start.2
  18.4 0.0 collective-permute-done.5.refs_10_
  18.4 0.5 %collective-permute-start.6 = (f32[132,512]{1,0:T(8,128)S(1)}, f32[132,512]{1,0:T(8,128)S(1)}, u32[]{:S(2)}, u32[]{:S(2)}) collective-permute-start(f32[132,512]{1,0:T(8,128)S(1)} %collective-permute-done.5.refs_10_), channel_id=1, source_target_pairs={{0,1},{1,0},{2,3},{3,2},{4,5},{5,4},{6,7},{7,6},{8,9},{9,8},{10,11... | collective-permute-start | bytes 811016 | tf_op jit(solution)/shard_map/ppermute | solution.py:272
  18.9 0.0 collective-permute-done.one.refs_3_
  18.9 0.0 copy-done
  18.9 0.6 %gram.3 = (f32[256,256]{1,0:T(8,128)S(1)}, f32[512,256]{1,0:T(8,128)S(1)}, f32[8,128]{1,0:T(8,128)S(1)}) custom-call(f32[4]{0:T(128)S(1)} %copy-done, f32[132,512]{1,0:T(8,128)S(1)} %collective-permute-done.one.refs_3_, f32[132,512]{1,0:T(8,128)S(1)} %get-tuple-element.20.two.refs_4_), custom_call_target="tpu_custom_call" | custom-call | flops 600000000 | tf_op jit(solution)/shard_map/gram/pallas_call | solution.py:142
  19.5 0.0 collective-permute-done.4.one.refs_5_
  19.5 0.4 %collective-permute-done.2.one.refs_7_ = f32[132,512]{1,0:T(8,128)S(1)} collective-permute-done((f32[132,512]{1,0:T(8,128)S(1)}, f32[132,512]{1,0:T(8,128)S(1)}, u32[]{:S(2)}, u32[]{:S(2)}) %collective-permute-start.2) | collective-permute-done | bytes 270368 | tf_op jit(solution)/shard_map/ppermute | solution.py:272
  20.0 0.4 collective-permute-done.6.refs_9_
  20.4 0.9 %collective-permute-start.9 = (f32[32,256]{1,0:T(8,128)S(1)}, f32[32,256]{1,0:T(8,128)S(1)}, u32[]{:S(2)}, u32[]{:S(2)}) collective-permute-start(f32[32,256]{1,0:T(8,128)S(1)} %get-tuple-element.34), channel_id=1, source_target_pairs={{0,2},{1,3},{2,0},{3,1},{4,6},{5,7},{6,4},{7,5},{8,10},{9,11},{10,... | collective-permute-start | bytes 98312 | tf_op jit(solution)/shard_map/ppermute | solution.py:272
  21.3 1.2 %collective-permute-start.8 = (f32[32,256]{1,0:T(8,128)S(1)}, f32[32,256]{1,0:T(8,128)S(1)}, u32[]{:S(2)}, u32[]{:S(2)}) collective-permute-start(f32[32,256]{1,0:T(8,128)S(1)} %get-tuple-element.33), channel_id=1, source_target_pairs={{0,4},{1,5},{2,6},{3,7},{4,0},{5,1},{6,2},{7,3},{8,12},{9,13},{10,... | collective-permute-start | bytes 98312 | tf_op jit(solution)/shard_map/ppermute | solution.py:272
  22.5 1.4 %collective-permute-start.7 = (f32[32,256]{1,0:T(8,128)S(1)}, f32[32,256]{1,0:T(8,128)S(1)}, u32[]{:S(2)}, u32[]{:S(2)}) collective-permute-start(f32[32,256]{1,0:T(8,128)S(1)} %get-tuple-element.32), channel_id=1, source_target_pairs={{0,6},{1,7},{2,4},{3,5},{4,2},{5,3},{6,0},{7,1},{8,14},{9,15},{10,... | collective-permute-start | bytes 98312 | tf_op jit(solution)/shard_map/ppermute | solution.py:272
  24.0 0.4 collective-permute-done.9
  24.4 0.8 %collective-permute-done.8 = f32[32,256]{1,0:T(8,128)S(1)} collective-permute-done((f32[32,256]{1,0:T(8,128)S(1)}, f32[32,256]{1,0:T(8,128)S(1)}, u32[]{:S(2)}, u32[]{:S(2)}) %collective-permute-start.8) | collective-permute-done | bytes 32800 | tf_op jit(solution)/shard_map/ppermute | solution.py:272
  25.2 2.1 %collective-permute-done.7 = f32[32,256]{1,0:T(8,128)S(1)} collective-permute-done((f32[32,256]{1,0:T(8,128)S(1)}, f32[32,256]{1,0:T(8,128)S(1)}, u32[]{:S(2)}, u32[]{:S(2)}) %collective-permute-start.7) | collective-permute-done | bytes 32800 | tf_op jit(solution)/shard_map/ppermute | solution.py:272
  27.4 2.7 %collective-permute-start.10 = (f32[16,256]{1,0:T(8,128)S(1)}, f32[16,256]{1,0:T(8,128)S(1)}, u32[]{:S(2)}, u32[]{:S(2)}) collective-permute-start(f32[16,256]{1,0:T(8,128)S(1)} %slice.25), channel_id=1, source_target_pairs={{0,16},{8,24},{16,0},{24,8},{1,17},{9,25},{17,1},{25,9},{2,18},{10... | collective-permute-start | bytes 49160 | tf_op jit(solution)/shard_map/ppermute | solution.py:272
  30.0 2.0 %collective-permute-done.10 = f32[16,256]{1,0:T(8,128)S(1)} collective-permute-done((f32[16,256]{1,0:T(8,128)S(1)}, f32[16,256]{1,0:T(8,128)S(1)}, u32[]{:S(2)}, u32[]{:S(2)}) %collective-permute-start.10) | collective-permute-done | bytes 16416 | tf_op jit(solution)/shard_map/ppermute | solution.py:272
  32.1 1.6 %collective-permute-start.11 = (f32[8,256]{1,0:T(8,128)S(1)}, f32[8,256]{1,0:T(8,128)S(1)}, u32[]{:S(2)}, u32[]{:S(2)}) collective-permute-start(f32[8,256]{1,0:T(8,128)S(1)} %slice.27), channel_id=1, source_target_pairs={{0,8},{8,0},{16,24},{24,16},{1,9},{9,1},{17,25},{25,17},{2,10},{10... | collective-permute-start | bytes 24584 | tf_op jit(solution)/shard_map/ppermute | solution.py:272
  33.6 2.1 %collective-permute-done.11 = f32[8,256]{1,0:T(8,128)S(1)} collective-permute-done((f32[8,256]{1,0:T(8,128)S(1)}, f32[8,256]{1,0:T(8,128)S(1)}, u32[]{:S(2)}, u32[]{:S(2)}) %collective-permute-start.11) | collective-permute-done | bytes 8224 | tf_op jit(solution)/shard_map/ppermute | solution.py:272
  35.7 5.7 %collective-permute-start.12 = (f32[8,128]{1,0:T(8,128)S(1)}, f32[8,128]{1,0:T(8,128)S(1)}, u32[]{:S(2)}, u32[]{:S(2)}) collective-permute-start(f32[8,128]{1,0:T(8,128)S(1)} %slice.29), channel_id=1, source_target_pairs={{0,1},{1,0},{2,3},{3,2},{4,5},{5,4},{6,7},{7,6},{8,9},{9,8},{10,11... | collective-permute-start | bytes 12296 | tf_op jit(solution)/shard_map/ppermute | solution.py:272
  41.5 0.8 %collective-permute-done.12 = f32[8,128]{1,0:T(8,128)S(1)} collective-permute-done((f32[8,128]{1,0:T(8,128)S(1)}, f32[8,128]{1,0:T(8,128)S(1)}, u32[]{:S(2)}, u32[]{:S(2)}) %collective-permute-start.12) | collective-permute-done | bytes 4128 | tf_op jit(solution)/shard_map/ppermute | solution.py:272
  42.3 0.6 %fusion = f32[128,8]{0,1:T(8,128)} fusion(f32[8,128]{1,0:T(8,128)S(1)} %collective-permute-done.12, f32[8,256]{1,0:T(8,128)S(1)} %slice_add_fusion.1, pred[]{:T(512)S(6)} %eq.5), kind=kLoop, calls=%fused_computation.4 | loop fusion | flops 1024 | bytes 12289 | tf_op jit(solution)/shard_map/transpose | solution.py:307
  (9 shorter events, 0.1 us)
Async XLA Ops:
  1.3 10.5 %collective-permute-start.3 = (f32[132,512]{1,0:T(8,128)S(1)}, f32[132,512]{1,0:T(8,128)S(1)}, u32[]{:S(2)}, u32[]{:S(2)}) collective-permute-start(f32[132,512]{1,0:T(8,128)S(1)} %get-tuple-element.23), channel_id=1, source_target_pairs={{0,2},{1,3},{2,0},{3,1},{4,6},{5,7},{6,4},{7,5},{8,10},{9,11},{10,... | collective-permute-start | bytes 811016 | tf_op jit(solution)/shard_map/ppermute | solution.py:272
  4.3 14.1 %collective-permute-start.1 = (f32[132,512]{1,0:T(8,128)S(1)}, f32[132,512]{1,0:T(8,128)S(1)}, u32[]{:S(2)}, u32[]{:S(2)}) collective-permute-start(f32[132,512]{1,0:T(8,128)S(1)} %get-tuple-element.22), channel_id=1, source_target_pairs={{0,4},{1,5},{2,6},{3,7},{4,0},{5,1},{6,2},{7,3},{8,12},{9,13},{10,... | collective-permute-start | bytes 811016 | tf_op jit(solution)/shard_map/ppermute | solution.py:272
  5.9 13.1 %copy-start = (f32[4]{0:T(128)S(1)}, f32[4]{0:T(128)}, u32[]{:S(2)}) copy-start(f32[4]{0:T(128)} %damping_ref.1) | copy-start | bytes 52
  5.9 12.6 %collective-permute-start.5 = (f32[132,512]{1,0:T(8,128)S(1)}, f32[132,512]{1,0:T(8,128)S(1)}, u32[]{:S(2)}, u32[]{:S(2)}) collective-permute-start(f32[132,512]{1,0:T(8,128)S(1)} %get-tuple-element.30), channel_id=1, source_target_pairs={{0,6},{1,7},{2,4},{3,5},{4,2},{5,3},{6,0},{7,1},{8,14},{9,15},{10,... | collective-permute-start | bytes 811016 | tf_op jit(solution)/shard_map/ppermute | solution.py:272
  5.9 13.1 %collective-permute-start = (f32[132,512]{1,0:T(8,128)S(1)}, f32[132,512]{1,0:T(8,128)S(1)}, u32[]{:S(2)}, u32[]{:S(2)}) collective-permute-start(f32[132,512]{1,0:T(8,128)S(1)} %get-tuple-element.20.two.refs_4_), channel_id=1, source_target_pairs={{0,1},{1,0},{2,3},{3,2},{4,5},{5,4},{6,7},{7,6},{8,9},{9,8},{10,11... | collective-permute-start | bytes 811016 | tf_op jit(solution)/shard_map/ppermute | solution.py:272
  11.8 7.7 %collective-permute-start.4 = (f32[132,512]{1,0:T(8,128)S(1)}, f32[132,512]{1,0:T(8,128)S(1)}, u32[]{:S(2)}, u32[]{:S(2)}) collective-permute-start(f32[132,512]{1,0:T(8,128)S(1)} %collective-permute-done.3.two.refs_6_), channel_id=1, source_target_pairs={{0,1},{1,0},{2,3},{3,2},{4,5},{5,4},{6,7},{7,6},{8,9},{9,8},{10,11... | collective-permute-start | bytes 811016 | tf_op jit(solution)/shard_map/ppermute | solution.py:272
  18.4 1.6 %collective-permute-start.2 = (f32[132,512]{1,0:T(8,128)S(1)}, f32[132,512]{1,0:T(8,128)S(1)}, u32[]{:S(2)}, u32[]{:S(2)}) collective-permute-start(f32[132,512]{1,0:T(8,128)S(1)} %collective-permute-done.1.two.refs_8_), channel_id=1, source_target_pairs={{0,1},{1,0},{2,3},{3,2},{4,5},{5,4},{6,7},{7,6},{8,9},{9,8},{10,11... | collective-permute-start | bytes 811016 | tf_op jit(solution)/shard_map/ppermute | solution.py:272
  18.4 2.0 %collective-permute-start.6 = (f32[132,512]{1,0:T(8,128)S(1)}, f32[132,512]{1,0:T(8,128)S(1)}, u32[]{:S(2)}, u32[]{:S(2)}) collective-permute-start(f32[132,512]{1,0:T(8,128)S(1)} %collective-permute-done.5.refs_10_), channel_id=1, source_target_pairs={{0,1},{1,0},{2,3},{3,2},{4,5},{5,4},{6,7},{7,6},{8,9},{9,8},{10,11... | collective-permute-start | bytes 811016 | tf_op jit(solution)/shard_map/ppermute | solution.py:272
  20.4 4.0 %collective-permute-start.9 = (f32[32,256]{1,0:T(8,128)S(1)}, f32[32,256]{1,0:T(8,128)S(1)}, u32[]{:S(2)}, u32[]{:S(2)}) collective-permute-start(f32[32,256]{1,0:T(8,128)S(1)} %get-tuple-element.34), channel_id=1, source_target_pairs={{0,2},{1,3},{2,0},{3,1},{4,6},{5,7},{6,4},{7,5},{8,10},{9,11},{10,... | collective-permute-start | bytes 98312 | tf_op jit(solution)/shard_map/ppermute | solution.py:272
  21.3 3.9 %collective-permute-start.8 = (f32[32,256]{1,0:T(8,128)S(1)}, f32[32,256]{1,0:T(8,128)S(1)}, u32[]{:S(2)}, u32[]{:S(2)}) collective-permute-start(f32[32,256]{1,0:T(8,128)S(1)} %get-tuple-element.33), channel_id=1, source_target_pairs={{0,4},{1,5},{2,6},{3,7},{4,0},{5,1},{6,2},{7,3},{8,12},{9,13},{10,... | collective-permute-start | bytes 98312 | tf_op jit(solution)/shard_map/ppermute | solution.py:272
  22.5 4.8 %collective-permute-start.7 = (f32[32,256]{1,0:T(8,128)S(1)}, f32[32,256]{1,0:T(8,128)S(1)}, u32[]{:S(2)}, u32[]{:S(2)}) collective-permute-start(f32[32,256]{1,0:T(8,128)S(1)} %get-tuple-element.32), channel_id=1, source_target_pairs={{0,6},{1,7},{2,4},{3,5},{4,2},{5,3},{6,0},{7,1},{8,14},{9,15},{10,... | collective-permute-start | bytes 98312 | tf_op jit(solution)/shard_map/ppermute | solution.py:272
  27.4 4.7 %collective-permute-start.10 = (f32[16,256]{1,0:T(8,128)S(1)}, f32[16,256]{1,0:T(8,128)S(1)}, u32[]{:S(2)}, u32[]{:S(2)}) collective-permute-start(f32[16,256]{1,0:T(8,128)S(1)} %slice.25), channel_id=1, source_target_pairs={{0,16},{8,24},{16,0},{24,8},{1,17},{9,25},{17,1},{25,9},{2,18},{10... | collective-permute-start | bytes 49160 | tf_op jit(solution)/shard_map/ppermute | solution.py:272
  32.1 3.7 %collective-permute-start.11 = (f32[8,256]{1,0:T(8,128)S(1)}, f32[8,256]{1,0:T(8,128)S(1)}, u32[]{:S(2)}, u32[]{:S(2)}) collective-permute-start(f32[8,256]{1,0:T(8,128)S(1)} %slice.27), channel_id=1, source_target_pairs={{0,8},{8,0},{16,24},{24,16},{1,9},{9,1},{17,25},{25,17},{2,10},{10... | collective-permute-start | bytes 24584 | tf_op jit(solution)/shard_map/ppermute | solution.py:272
  35.7 6.5 %collective-permute-start.12 = (f32[8,128]{1,0:T(8,128)S(1)}, f32[8,128]{1,0:T(8,128)S(1)}, u32[]{:S(2)}, u32[]{:S(2)}) collective-permute-start(f32[8,128]{1,0:T(8,128)S(1)} %slice.29), channel_id=1, source_target_pairs={{0,1},{1,0},{2,3},{3,2},{4,5},{5,4},{6,7},{7,6},{8,9},{9,8},{10,11... | collective-permute-start | bytes 12296 | tf_op jit(solution)/shard_map/ppermute | solution.py:272

commit v4 on v3

--- a/solution.py
+++ b/solution.py
@@ -8,7 +8,9 @@
 from jax.experimental.pallas import tpu as pltpu
 from jax.sharding import PartitionSpec as P
 
+
 NEWTON_STEPS = 8
+SQUARINGS = 6
 CORES = 2
 SOLVER = 1
 PIECES = 4
@@ -51,6 +53,13 @@
         + product(left_high, right_low, dims)
         + product(left_low, right_high, dims)
     )
+
+
+def narrow_product(left, right_high, right_low, dims=(((1,), (0,)), ((), ()))):
+    high, low = halves(left)
+    count = left.shape[0]
+    both = product(jnp.concatenate([high, low], 0), right_high, dims)
+    return both[:count] + both[count:] + product(high, right_low, dims)
 
 
 def pack_kernel(rows_ref, queries_ref, *refs):
@@ -211,7 +220,7 @@
             asked[pl.ds(pl.multiple_of(source * group, group), group)] * inverse_norm
         )
 
-    for _ in range(NEWTON_STEPS - 1):
+    for _ in range(SQUARINGS):
         high[...], low[...] = halves(state[...])
 
         def part(start, stop, column):
@@ -231,16 +240,19 @@
         state[width:, half:] = 2.0 * state[width:, half:] - part(width, width + total_queries, half)
 
     high[...], low[...] = halves(state[...])
-    conditioned = 2.0 * state[width:] - product_3(
-        high[width:], low[width:], high[0:width], low[0:width]
-    )
-    conditioned_high, conditioned_low = halves(conditioned * scale)
+    asked_last = state[width:]
+    conditioned = asked_last
+    for _ in range(2 ** (NEWTON_STEPS - SQUARINGS) - 1):
+        moved = narrow_product(conditioned, high[0:width], low[0:width])
+        conditioned = asked_last + (conditioned - moved)
+    conditioned = conditioned * scale
     for offset in range(chips):
         for place, block in enumerate(blocks[offset]):
-            block_high, block_low = halves(block[0:rows])
-            scores[offset][:, place * rows : (place + 1) * rows] = product_3(
-                conditioned_high, conditioned_low, block_high, block_low, (((1,), (1,)), ((), ()))
-            )
+            stack[place * rows : (place + 1) * rows] = block[0:rows]
+        rows_high, rows_low = halves(stack[...])
+        scores[offset][...] = narrow_product(
+            conditioned, rows_high, rows_low, (((1,), (1,)), ((), ()))
+        )
 
 
 def solve(sizes, damp, given, blocks):
@@ -272,16 +284,56 @@
     return lax.ppermute(value, axis, [(i, i ^ offset) for i in range(lax.axis_size(axis))])
 
 
-def per_device(train_grads, queries, damping):
+def route(value, to_solver, others):
+    devices, groups = lax.axis_size("dp"), lax.axis_size("mod")
+    pairs = []
+    for group in range(groups):
+        for device in range(devices):
+            goal = to_solver(group, device)
+            if goal is None:
+                goal = others(group, device)
+            pairs.append((group * devices + device, goal[0] * devices + goal[1]))
+    return lax.ppermute(value, ("mod", "dp"), pairs)
+
+
+def same_core(value, offset):
+    return route(
+        value,
+        lambda group, device: (group, device ^ (CORES * offset)) if device % CORES == SOLVER else None,
+        lambda group, device: (group ^ 1, device),
+    )
+
+
+def cross_core(value, offset):
+    return route(
+        value,
+        lambda group, device: None
+        if device % CORES == SOLVER
+        else (group, (device ^ (CORES * offset)) ^ 1),
+        lambda group, device: (group, device ^ 1),
+    )
+
+
+def sequence(chips):
+    steps = []
+    for first in range(1, chips, 2):
+        offsets = range(first, min(first + 2, chips))
+        steps += [("same", offset) for offset in offsets]
+        steps += [("cross", offset) for offset in offsets]
+    return steps + [("cross", 0)]
+
+
+def influence(train_grads, queries, damping):
     rows, modules, width = train_grads.shape
     devices = lax.axis_size("dp")
     groups = lax.axis_size("mod")
     chips = devices // CORES
     packed = pack(train_grads, queries)
-    arrived = [packed[0]]
-    for offset in range(1, chips):
-        arrived.append(swap(packed[offset], "dp", CORES * offset))
-    blocks = [[swap(block, "dp", 1), block] for block in arrived]
+    arrived = {("same", 0): packed[0]}
+    for kind, offset in sequence(chips):
+        mover = same_core if kind == "same" else cross_core
+        arrived[kind, offset] = mover(packed[offset], offset)
+    blocks = [[arrived["cross", offset], arrived["same", offset]] for offset in range(chips)]
     *given, damp = gram(rows, blocks[0], damping=damping)
     for offset in range(1, chips - 1):
         given = gram(rows, blocks[offset], given)
@@ -309,7 +361,7 @@
 
 def solution(mesh):
     return jax.shard_map(
-        per_device,
+        influence,
         mesh=mesh,
         in_specs=(P("dp", "mod", None), P("dp", "mod", None), P("mod")),
         out_specs=P("dp", "mod"),

time: 43 us -> 41.3 us (0.960)
  waiting for transfers between devices: 21.7 us -> 17.8 us
  starting transfers between devices: 18.6 us -> 20.8 us
    ppermute x13 -> x6, waiting for transfers between devices: 21.7 us -> 10.3 us  [swap(): lax.ppermute(value, axis, [(i, i ^ offset) for i in range(lax.axis_size(a...]
    ppermute x0 -> x7, starting transfers between devices: none -> 8.13 us  [route(): return lax.ppermute(value, ('mod', 'dp'), pairs)]
    ppermute x0 -> x7, waiting for transfers between devices: none -> 7.49 us  [route(): return lax.ppermute(value, ('mod', 'dp'), pairs)]
    ppermute x13 -> x6, starting transfers between devices: 18.6 us -> 12.7 us  [swap(): lax.ppermute(value, axis, [(i, i ^ offset) for i in range(lax.axis_size(a...]
  transfers between devices with their start and end apart: 13 -> 13, of which waited for: 10 -> 8; matrix products, arithmetic and copies ran while one was open for 0% -> 0% of each run, Pallas kernels for 1% -> 1%
where the time goes in v4:
time: 41.3 us; the launch traced here: 41.2 us
  starting transfers between devices  20.8 us (50%)
  waiting for transfers between devices  17.8 us (43%)
  Pallas kernels  1.88 us (5%)
  other arithmetic  0.61 us (1%)
    ppermute x6, starting transfers between devices, swap(): lax.ppermute(value, axis, [(i, i ^ offset) for i in range(lax.axis_size(a...  12.7 us
    ppermute x6, waiting for transfers between devices, swap(): lax.ppermute(value, axis, [(i, i ^ offset) for i in range(lax.axis_size(a...  10.3 us
    ppermute x7, starting transfers between devices, route(): return lax.ppermute(value, ('mod', 'dp'), pairs)  8.13 us
    ppermute x7, waiting for transfers between devices, route(): return lax.ppermute(value, ('mod', 'dp'), pairs)  7.49 us
    pallas_call x1, Pallas kernels, pack(): pl.pallas_call(pack_kernel, out_shape=[near((rows + queries.shape[0], wid...  1.29 us
  transfers between devices with their start and end apart: 13, of which 8 were waited for; matrix products, arithmetic and copies ran while one was open for 0% of the time, Pallas kernels for 1%

profile of v4, /device:TPU:0, one launch (start us, length us, event | category | flops | bytes accessed | tf_op | source)
XLA Modules:
  0.0 41.2 jit_solution(6324364647381774062)
XLA Ops:
  0.0 1.3 %pack.1 = (f32[132,512]{1,0:T(8,128)S(1)}, f32[132,512]{1,0:T(8,128)S(1)}, f32[132,512]{1,0:T(8,128)S(1)}, f32[132,512]{1,0:T(8,128)S(1)}) custom-call(f32[128,4,512]{2,1,0:T(4,128)} %rows_ref.1, f32[4,4,512]{2,1,0:T(4,128)} %queries_ref.1), custom_call_target="tpu_custom_call" | custom-call | flops 1500000000 | tf_op jit(solution)/shard_map/pack/pallas_call | solution.py:96
  1.3 0.6 %collective-permute-start = (f32[132,512]{1,0:T(8,128)S(1)}, f32[132,512]{1,0:T(8,128)S(1)}, u32[]{:S(2)}, u32[]{:S(2)}) collective-permute-start(f32[132,512]{1,0:T(8,128)S(1)} %get-tuple-element.20.two.refs_4_), channel_id=1, source_target_pairs={{0,1},{1,0},{2,3},{3,2},{4,5},{5,4},{6,7},{7,6},{8,9},{9,8},{10,11... | collective-permute-start | bytes 811016 | tf_op jit(solution)/shard_map/ppermute | solution.py:296
  1.9 2.6 %collective-permute-start.3 = (f32[132,512]{1,0:T(8,128)S(1)}, f32[132,512]{1,0:T(8,128)S(1)}, u32[]{:S(2)}, u32[]{:S(2)}) collective-permute-start(f32[132,512]{1,0:T(8,128)S(1)} %get-tuple-element.23), channel_id=1, source_target_pairs={{0,3},{1,0},{2,1},{3,2},{4,7},{5,4},{6,5},{7,6},{8,11},{9,8},{10,9... | collective-permute-start | bytes 811016 | tf_op jit(solution)/shard_map/ppermute | solution.py:296
  4.4 1.6 %collective-permute-start.4 = (f32[132,512]{1,0:T(8,128)S(1)}, f32[132,512]{1,0:T(8,128)S(1)}, u32[]{:S(2)}, u32[]{:S(2)}) collective-permute-start(f32[132,512]{1,0:T(8,128)S(1)} %get-tuple-element.23), channel_id=1, source_target_pairs={{0,8},{1,3},{2,10},{3,1},{4,12},{5,7},{6,14},{7,5},{8,0},{9,11},{1... | collective-permute-start | bytes 811016 | tf_op jit(solution)/shard_map/ppermute | solution.py:296
  6.0 0.0 copy-start
  6.0 0.0 collective-permute-start.1
  6.0 1.3 %collective-permute-start.2 = (f32[132,512]{1,0:T(8,128)S(1)}, f32[132,512]{1,0:T(8,128)S(1)}, u32[]{:S(2)}, u32[]{:S(2)}) collective-permute-start(f32[132,512]{1,0:T(8,128)S(1)} %get-tuple-element.22), channel_id=1, source_target_pairs={{0,8},{1,5},{2,10},{3,7},{4,12},{5,1},{6,14},{7,3},{8,0},{9,13},{1... | collective-permute-start | bytes 811016 | tf_op jit(solution)/shard_map/ppermute | solution.py:296
  7.3 0.0 collective-permute-done.one.refs_3_
  7.3 0.5 %collective-permute-start.5 = (f32[132,512]{1,0:T(8,128)S(1)}, f32[132,512]{1,0:T(8,128)S(1)}, u32[]{:S(2)}, u32[]{:S(2)}) collective-permute-start(f32[132,512]{1,0:T(8,128)S(1)} %get-tuple-element.30), channel_id=1, source_target_pairs={{0,7},{1,0},{2,5},{3,2},{4,3},{5,4},{6,1},{7,6},{8,15},{9,8},{10,1... | collective-permute-start | bytes 811016 | tf_op jit(solution)/shard_map/ppermute | solution.py:296
  7.9 3.1 %collective-permute-done.3.one.refs_5_ = f32[132,512]{1,0:T(8,128)S(1)} collective-permute-done((f32[132,512]{1,0:T(8,128)S(1)}, f32[132,512]{1,0:T(8,128)S(1)}, u32[]{:S(2)}, u32[]{:S(2)}) %collective-permute-start.3) | collective-permute-done | bytes 270368 | tf_op jit(solution)/shard_map/ppermute | solution.py:296
  11.0 1.6 %collective-permute-start.6 = (f32[132,512]{1,0:T(8,128)S(1)}, f32[132,512]{1,0:T(8,128)S(1)}, u32[]{:S(2)}, u32[]{:S(2)}) collective-permute-start(f32[132,512]{1,0:T(8,128)S(1)} %get-tuple-element.30), channel_id=1, source_target_pairs={{0,8},{1,7},{2,10},{3,5},{4,12},{5,3},{6,14},{7,1},{8,0},{9,15},{1... | collective-permute-start | bytes 811016 | tf_op jit(solution)/shard_map/ppermute | solution.py:296
  12.6 0.0 copy-done
  12.6 0.6 %gram.3 = (f32[256,256]{1,0:T(8,128)S(1)}, f32[512,256]{1,0:T(8,128)S(1)}, f32[8,128]{1,0:T(8,128)S(1)}) custom-call(f32[4]{0:T(128)S(1)} %copy-done, f32[132,512]{1,0:T(8,128)S(1)} %collective-permute-done.one.refs_3_, f32[132,512]{1,0:T(8,128)S(1)} %get-tuple-element.20.two.refs_4_), custom_call_target="tpu_custom_call" | custom-call | flops 600000000 | tf_op jit(solution)/shard_map/gram/pallas_call | solution.py:151
  13.1 0.0 collective-permute-done.4.two.refs_6_
  13.2 1.7 %collective-permute-done.1.one.refs_7_ = f32[132,512]{1,0:T(8,128)S(1)} collective-permute-done((f32[132,512]{1,0:T(8,128)S(1)}, f32[132,512]{1,0:T(8,128)S(1)}, u32[]{:S(2)}, u32[]{:S(2)}) %collective-permute-start.1) | collective-permute-done | bytes 270368 | tf_op jit(solution)/shard_map/ppermute | solution.py:296
  14.9 0.0 collective-permute-done.2.two.refs_8_
  14.9 0.0 collective-permute-done.5.refs_9_
  14.9 2.7 %collective-permute-done.6.refs_10_ = f32[132,512]{1,0:T(8,128)S(1)} collective-permute-done((f32[132,512]{1,0:T(8,128)S(1)}, f32[132,512]{1,0:T(8,128)S(1)}, u32[]{:S(2)}, u32[]{:S(2)}) %collective-permute-start.6) | collective-permute-done | bytes 270368 | tf_op jit(solution)/shard_map/ppermute | solution.py:296
  17.6 0.3 collective-permute-start.9
  17.9 3.3 %collective-permute-start.8 = (f32[32,256]{1,0:T(8,128)S(1)}, f32[32,256]{1,0:T(8,128)S(1)}, u32[]{:S(2)}, u32[]{:S(2)}) collective-permute-start(f32[32,256]{1,0:T(8,128)S(1)} %get-tuple-element.33), channel_id=1, source_target_pairs={{0,4},{1,5},{2,6},{3,7},{4,0},{5,1},{6,2},{7,3},{8,12},{9,13},{10,... | collective-permute-start | bytes 98312 | tf_op jit(solution)/shard_map/ppermute | solution.py:284
  21.2 0.9 %collective-permute-start.7 = (f32[32,256]{1,0:T(8,128)S(1)}, f32[32,256]{1,0:T(8,128)S(1)}, u32[]{:S(2)}, u32[]{:S(2)}) collective-permute-start(f32[32,256]{1,0:T(8,128)S(1)} %get-tuple-element.32), channel_id=1, source_target_pairs={{0,6},{1,7},{2,4},{3,5},{4,2},{5,3},{6,0},{7,1},{8,14},{9,15},{10,... | collective-permute-start | bytes 98312 | tf_op jit(solution)/shard_map/ppermute | solution.py:284
  22.1 0.0 collective-permute-done.9
  22.1 1.0 %collective-permute-done.8 = f32[32,256]{1,0:T(8,128)S(1)} collective-permute-done((f32[32,256]{1,0:T(8,128)S(1)}, f32[32,256]{1,0:T(8,128)S(1)}, u32[]{:S(2)}, u32[]{:S(2)}) %collective-permute-start.8) | collective-permute-done | bytes 32800 | tf_op jit(solution)/shard_map/ppermute | solution.py:284
  23.1 2.9 %collective-permute-done.7 = f32[32,256]{1,0:T(8,128)S(1)} collective-permute-done((f32[32,256]{1,0:T(8,128)S(1)}, f32[32,256]{1,0:T(8,128)S(1)}, u32[]{:S(2)}, u32[]{:S(2)}) %collective-permute-start.7) | collective-permute-done | bytes 32800 | tf_op jit(solution)/shard_map/ppermute | solution.py:284
  26.0 2.7 %collective-permute-start.10 = (f32[16,256]{1,0:T(8,128)S(1)}, f32[16,256]{1,0:T(8,128)S(1)}, u32[]{:S(2)}, u32[]{:S(2)}) collective-permute-start(f32[16,256]{1,0:T(8,128)S(1)} %slice.25), channel_id=1, source_target_pairs={{0,16},{8,24},{16,0},{24,8},{1,17},{9,25},{17,1},{25,9},{2,18},{10... | collective-permute-start | bytes 49160 | tf_op jit(solution)/shard_map/ppermute | solution.py:284
  28.7 2.0 %collective-permute-done.10 = f32[16,256]{1,0:T(8,128)S(1)} collective-permute-done((f32[16,256]{1,0:T(8,128)S(1)}, f32[16,256]{1,0:T(8,128)S(1)}, u32[]{:S(2)}, u32[]{:S(2)}) %collective-permute-start.10) | collective-permute-done | bytes 16416 | tf_op jit(solution)/shard_map/ppermute | solution.py:284
  30.7 0.1 collective-permute-start.11
  30.8 3.6 %collective-permute-done.11 = f32[8,256]{1,0:T(8,128)S(1)} collective-permute-done((f32[8,256]{1,0:T(8,128)S(1)}, f32[8,256]{1,0:T(8,128)S(1)}, u32[]{:S(2)}, u32[]{:S(2)}) %collective-permute-start.11) | collective-permute-done | bytes 8224 | tf_op jit(solution)/shard_map/ppermute | solution.py:284
  34.4 5.4 %collective-permute-start.12 = (f32[8,128]{1,0:T(8,128)S(1)}, f32[8,128]{1,0:T(8,128)S(1)}, u32[]{:S(2)}, u32[]{:S(2)}) collective-permute-start(f32[8,128]{1,0:T(8,128)S(1)} %slice.29), channel_id=1, source_target_pairs={{0,1},{1,0},{2,3},{3,2},{4,5},{5,4},{6,7},{7,6},{8,9},{9,8},{10,11... | collective-permute-start | bytes 12296 | tf_op jit(solution)/shard_map/ppermute | solution.py:284
  39.8 0.8 %collective-permute-done.12 = f32[8,128]{1,0:T(8,128)S(1)} collective-permute-done((f32[8,128]{1,0:T(8,128)S(1)}, f32[8,128]{1,0:T(8,128)S(1)}, u32[]{:S(2)}, u32[]{:S(2)}) %collective-permute-start.12) | collective-permute-done | bytes 4128 | tf_op jit(solution)/shard_map/ppermute | solution.py:284
  40.6 0.6 %fusion = f32[128,8]{0,1:T(8,128)} fusion(f32[8,128]{1,0:T(8,128)S(1)} %collective-permute-done.12, f32[8,256]{1,0:T(8,128)S(1)} %slice_add_fusion.1, pred[]{:T(512)S(6)} %eq.5), kind=kLoop, calls=%fused_computation.4 | loop fusion | flops 1024 | bytes 12289 | tf_op jit(solution)/shard_map/transpose | solution.py:359
  (9 shorter events, 0.1 us)
Async XLA Ops:
  1.3 6.0 %collective-permute-start = (f32[132,512]{1,0:T(8,128)S(1)}, f32[132,512]{1,0:T(8,128)S(1)}, u32[]{:S(2)}, u32[]{:S(2)}) collective-permute-start(f32[132,512]{1,0:T(8,128)S(1)} %get-tuple-element.20.two.refs_4_), channel_id=1, source_target_pairs={{0,1},{1,0},{2,3},{3,2},{4,5},{5,4},{6,7},{7,6},{8,9},{9,8},{10,11... | collective-permute-start | bytes 811016 | tf_op jit(solution)/shard_map/ppermute | solution.py:296
  1.9 9.1 %collective-permute-start.3 = (f32[132,512]{1,0:T(8,128)S(1)}, f32[132,512]{1,0:T(8,128)S(1)}, u32[]{:S(2)}, u32[]{:S(2)}) collective-permute-start(f32[132,512]{1,0:T(8,128)S(1)} %get-tuple-element.23), channel_id=1, source_target_pairs={{0,3},{1,0},{2,1},{3,2},{4,7},{5,4},{6,5},{7,6},{8,11},{9,8},{10,9... | collective-permute-start | bytes 811016 | tf_op jit(solution)/shard_map/ppermute | solution.py:296
  4.4 8.7 %collective-permute-start.4 = (f32[132,512]{1,0:T(8,128)S(1)}, f32[132,512]{1,0:T(8,128)S(1)}, u32[]{:S(2)}, u32[]{:S(2)}) collective-permute-start(f32[132,512]{1,0:T(8,128)S(1)} %get-tuple-element.23), channel_id=1, source_target_pairs={{0,8},{1,3},{2,10},{3,1},{4,12},{5,7},{6,14},{7,5},{8,0},{9,11},{1... | collective-permute-start | bytes 811016 | tf_op jit(solution)/shard_map/ppermute | solution.py:296
  6.0 6.5 %copy-start = (f32[4]{0:T(128)S(1)}, f32[4]{0:T(128)}, u32[]{:S(2)}) copy-start(f32[4]{0:T(128)} %damping_ref.1) | copy-start | bytes 52
  6.0 8.8 %collective-permute-start.1 = (f32[132,512]{1,0:T(8,128)S(1)}, f32[132,512]{1,0:T(8,128)S(1)}, u32[]{:S(2)}, u32[]{:S(2)}) collective-permute-start(f32[132,512]{1,0:T(8,128)S(1)} %get-tuple-element.22), channel_id=1, source_target_pairs={{0,5},{1,0},{2,7},{3,2},{4,1},{5,4},{6,3},{7,6},{8,13},{9,8},{10,1... | collective-permute-start | bytes 811016 | tf_op jit(solution)/shard_map/ppermute | solution.py:296
  6.0 8.8 %collective-permute-start.2 = (f32[132,512]{1,0:T(8,128)S(1)}, f32[132,512]{1,0:T(8,128)S(1)}, u32[]{:S(2)}, u32[]{:S(2)}) collective-permute-start(f32[132,512]{1,0:T(8,128)S(1)} %get-tuple-element.22), channel_id=1, source_target_pairs={{0,8},{1,5},{2,10},{3,7},{4,12},{5,1},{6,14},{7,3},{8,0},{9,13},{1... | collective-permute-start | bytes 811016 | tf_op jit(solution)/shard_map/ppermute | solution.py:296
  7.3 7.5 %collective-permute-start.5 = (f32[132,512]{1,0:T(8,128)S(1)}, f32[132,512]{1,0:T(8,128)S(1)}, u32[]{:S(2)}, u32[]{:S(2)}) collective-permute-start(f32[132,512]{1,0:T(8,128)S(1)} %get-tuple-element.30), channel_id=1, source_target_pairs={{0,7},{1,0},{2,5},{3,2},{4,3},{5,4},{6,1},{7,6},{8,15},{9,8},{10,1... | collective-permute-start | bytes 811016 | tf_op jit(solution)/shard_map/ppermute | solution.py:296
  11.0 6.5 %collective-permute-start.6 = (f32[132,512]{1,0:T(8,128)S(1)}, f32[132,512]{1,0:T(8,128)S(1)}, u32[]{:S(2)}, u32[]{:S(2)}) collective-permute-start(f32[132,512]{1,0:T(8,128)S(1)} %get-tuple-element.30), channel_id=1, source_target_pairs={{0,8},{1,7},{2,10},{3,5},{4,12},{5,3},{6,14},{7,1},{8,0},{9,15},{1... | collective-permute-start | bytes 811016 | tf_op jit(solution)/shard_map/ppermute | solution.py:296
  17.6 4.5 %collective-permute-start.9 = (f32[32,256]{1,0:T(8,128)S(1)}, f32[32,256]{1,0:T(8,128)S(1)}, u32[]{:S(2)}, u32[]{:S(2)}) collective-permute-start(f32[32,256]{1,0:T(8,128)S(1)} %get-tuple-element.34), channel_id=1, source_target_pairs={{0,2},{1,3},{2,0},{3,1},{4,6},{5,7},{6,4},{7,5},{8,10},{9,11},{10,... | collective-permute-start | bytes 98312 | tf_op jit(solution)/shard_map/ppermute | solution.py:284
  17.9 5.2 %collective-permute-start.8 = (f32[32,256]{1,0:T(8,128)S(1)}, f32[32,256]{1,0:T(8,128)S(1)}, u32[]{:S(2)}, u32[]{:S(2)}) collective-permute-start(f32[32,256]{1,0:T(8,128)S(1)} %get-tuple-element.33), channel_id=1, source_target_pairs={{0,4},{1,5},{2,6},{3,7},{4,0},{5,1},{6,2},{7,3},{8,12},{9,13},{10,... | collective-permute-start | bytes 98312 | tf_op jit(solution)/shard_map/ppermute | solution.py:284
  21.2 4.8 %collective-permute-start.7 = (f32[32,256]{1,0:T(8,128)S(1)}, f32[32,256]{1,0:T(8,128)S(1)}, u32[]{:S(2)}, u32[]{:S(2)}) collective-permute-start(f32[32,256]{1,0:T(8,128)S(1)} %get-tuple-element.32), channel_id=1, source_target_pairs={{0,6},{1,7},{2,4},{3,5},{4,2},{5,3},{6,0},{7,1},{8,14},{9,15},{10,... | collective-permute-start | bytes 98312 | tf_op jit(solution)/shard_map/ppermute | solution.py:284
  26.0 4.7 %collective-permute-start.10 = (f32[16,256]{1,0:T(8,128)S(1)}, f32[16,256]{1,0:T(8,128)S(1)}, u32[]{:S(2)}, u32[]{:S(2)}) collective-permute-start(f32[16,256]{1,0:T(8,128)S(1)} %slice.25), channel_id=1, source_target_pairs={{0,16},{8,24},{16,0},{24,8},{1,17},{9,25},{17,1},{25,9},{2,18},{10... | collective-permute-start | bytes 49160 | tf_op jit(solution)/shard_map/ppermute | solution.py:284
  30.7 3.7 %collective-permute-start.11 = (f32[8,256]{1,0:T(8,128)S(1)}, f32[8,256]{1,0:T(8,128)S(1)}, u32[]{:S(2)}, u32[]{:S(2)}) collective-permute-start(f32[8,256]{1,0:T(8,128)S(1)} %slice.27), channel_id=1, source_target_pairs={{0,8},{8,0},{16,24},{24,16},{1,9},{9,1},{17,25},{25,17},{2,10},{10... | collective-permute-start | bytes 24584 | tf_op jit(solution)/shard_map/ppermute | solution.py:284
  34.4 6.2 %collective-permute-start.12 = (f32[8,128]{1,0:T(8,128)S(1)}, f32[8,128]{1,0:T(8,128)S(1)}, u32[]{:S(2)}, u32[]{:S(2)}) collective-permute-start(f32[8,128]{1,0:T(8,128)S(1)} %slice.29), channel_id=1, source_target_pairs={{0,1},{1,0},{2,3},{3,2},{4,5},{5,4},{6,7},{7,6},{8,9},{9,8},{10,11... | collective-permute-start | bytes 12296 | tf_op jit(solution)/shard_map/ppermute | solution.py:284

commit v5 on v4

--- a/solution.py
+++ b/solution.py
@@ -161,13 +161,11 @@
 
 
 def solve_kernel(sizes, *refs):
-    chips = sizes[0]
-    scores = refs[3 + CORES * chips : 3 + (CORES + 1) * chips]
+    scores = refs[3 + CORES * sizes[0]]
 
     @pl.when(lax.axis_index("dp") % CORES != SOLVER)
     def _():
-        for score in scores:
-            score[...] = jnp.zeros_like(score)
+        scores[...] = jnp.zeros_like(scores)
 
     on_solver(functools.partial(solve_module, sizes, *refs))
 
@@ -177,8 +175,7 @@
     refs = list(refs)
     damp_ref, left_ref, right_ref = refs[:3]
     blocks = [refs[3 + CORES * offset : 3 + CORES * (offset + 1)] for offset in range(chips)]
-    scores = refs[3 + CORES * chips : 3 + (CORES + 1) * chips]
-    left, right, stack, state, high, low, asked = refs[3 + (CORES + 1) * chips :]
+    scores, left, right, stack, state, high, low, asked = refs[3 + CORES * chips :]
     half = left_ref.shape[0]
     width = 2 * half
     chip = lax.axis_index("dp") // CORES
@@ -195,25 +192,26 @@
 
     left[...] = left_ref[...]
     right[...] = right_ref[...]
-    add_gram(rows, blocks[-1], left, right, stack)
+    add_gram(rows, [block[1 - SOLVER] for block in blocks[-2:]], left, right, stack)
 
     diagonal = lax.broadcasted_iota(jnp.int32, (half, half), 0) == lax.broadcasted_iota(
         jnp.int32, (half, half), 1
     )
     eye = diagonal.astype(jnp.float32)
     first, cross, last = left[...], right[0:half], right[half:]
-    trace = jnp.sum((first + last) * eye, keepdims=True).reshape(1, 1) / total_rows
-    shift = damp_ref[0:1, 0:1] * trace / width
-    first = first / total_rows + shift * eye
-    last = last / total_rows + shift * eye
-    cross = cross / total_rows
+    trace = jnp.sum((first + last) * eye, keepdims=True).reshape(1, 1)
+    shift = (damp_ref[0:1, 0:1] * trace * (1.0 / width)) * eye
+    first = first + shift
+    last = last + shift
     squares = first * first + last * last + 2.0 * (cross * cross)
-    inverse_norm = lax.rsqrt(jnp.sum(squares, keepdims=True).reshape(1, 1) + epsilon)
-    cross = cross * inverse_norm
-    state[0:half, 0:half] = first * inverse_norm
+    squares = jnp.sum(squares, keepdims=True).reshape(1, 1) * (1.0 / total_rows**2)
+    inverse_norm = lax.rsqrt(squares + epsilon)
+    per_row = inverse_norm * (1.0 / total_rows)
+    cross = cross * per_row
+    state[0:half, 0:half] = first * per_row
     state[0:half, half:] = cross
     state[half:width, 0:half] = cross.T
-    state[half:width, half:] = last * inverse_norm
+    state[half:width, half:] = last * per_row
     for offset in range(groups):
         source = lax.bitwise_xor(group_here, jnp.int32(offset))
         state[width + offset * group : width + (offset + 1) * group] = (
@@ -250,7 +248,7 @@
         for place, block in enumerate(blocks[offset]):
             stack[place * rows : (place + 1) * rows] = block[0:rows]
         rows_high, rows_low = halves(stack[...])
-        scores[offset][...] = narrow_product(
+        scores[offset * total_queries : (offset + 1) * total_queries] = narrow_product(
             conditioned, rows_high, rows_low, (((1,), (1,)), ((), ()))
         )
 
@@ -262,9 +260,9 @@
     total_queries = chips * CORES * per_device
     return pl.pallas_call(
         functools.partial(solve_kernel, sizes),
-        out_shape=[near((total_queries, CORES * rows))] * chips,
+        out_shape=near((chips * total_queries, CORES * rows)),
         in_specs=[VMEM] * (3 + CORES * chips),
-        out_specs=[VMEM] * chips,
+        out_specs=VMEM,
         scratch_shapes=[
             pltpu.VMEM((half, half), jnp.float32),
             pltpu.VMEM((width, half), jnp.float32),
@@ -280,8 +278,8 @@
     )(*hold(damp, *given, *blocks))
 
 
-def swap(value, axis, offset):
-    return lax.ppermute(value, axis, [(i, i ^ offset) for i in range(lax.axis_size(axis))])
+def swap(value):
+    return lax.ppermute(value, "dp", [(i, i ^ 1) for i in range(lax.axis_size("dp"))])
 
 
 def route(value, to_solver, others):
@@ -312,6 +310,26 @@
         else (group, (device ^ (CORES * offset)) ^ 1),
         lambda group, device: (group, device ^ 1),
     )
+
+
+def hand_over(value, active, axis, offset):
+    move = CORES * offset
+
+    def goal(group, device):
+        if device % CORES != active:
+            return None
+        return (group ^ offset, device ^ 1) if axis == "mod" else (group, device ^ move ^ 1)
+
+    return route(value, goal, lambda group, device: (group, device ^ 1))
+
+
+def halvings(chips, groups):
+    steps = []
+    for axis, count in (("dp", chips), ("mod", groups)):
+        while count > 1:
+            count //= 2
+            steps.append((axis, count))
+    return steps
 
 
 def sequence(chips):
@@ -335,8 +353,9 @@
         arrived[kind, offset] = mover(packed[offset], offset)
     blocks = [[arrived["cross", offset], arrived["same", offset]] for offset in range(chips)]
     *given, damp = gram(rows, blocks[0], damping=damping)
-    for offset in range(1, chips - 1):
+    for offset in range(1, chips - 2):
         given = gram(rows, blocks[offset], given)
+    given = gram(rows, [block[SOLVER] for block in blocks[-2:]], given)
     sizes = (
         chips,
         rows,
@@ -346,17 +365,15 @@
         1.0 / math.sqrt(modules * groups * width),
     )
     scores = solve(sizes, damp, given, sum(blocks, []))
-    total = scores[0]
-    for offset in range(chips - 1, 0, -1):
-        total = total + swap(scores[offset], "dp", CORES * offset)
-    bit = groups // 2
-    while bit:
+    total, active = scores, SOLVER
+    for axis, offset in halvings(chips, groups):
         keep = total.shape[0] // 2
-        total = total[:keep] + swap(total[keep:], "mod", bit)
-        bit //= 2
-    solver = lax.axis_index("dp") % CORES == SOLVER
-    result = jnp.where(solver, total[:, SOLVER * rows :], swap(total[:, :rows], "dp", 1))
-    return result.T
+        theirs = hand_over(total[keep:], active, axis, offset)
+        total = swap(total[:keep]) + theirs
+        active = 1 - active
+    lanes = [total[:, core * rows : (core + 1) * rows] for core in range(CORES)]
+    handed = swap(lanes[1 - active])
+    return jnp.where(lax.axis_index("dp") % CORES == active, lanes[active], handed).T
 
 
 def solution(mesh):

time: 41.3 us -> 45 us (1.090)
  starting transfers between devices: 20.8 us -> 23.9 us
  waiting for transfers between devices: 17.8 us -> 18.3 us
    ppermute x7 -> x11, waiting for transfers between devices: 7.49 us -> 15.8 us  [route(): return lax.ppermute(value, ('mod', 'dp'), pairs)]
    ppermute x6 -> x5, waiting for transfers between devices: 10.3 us -> 2.47 us  [swap(): lax.ppermute(value, 'dp', [(i, i ^ 1) for i in range(lax.axis_size('dp'))])]
    ppermute x7 -> x11, starting transfers between devices: 8.13 us -> 12.4 us  [route(): return lax.ppermute(value, ('mod', 'dp'), pairs)]
    ppermute x6 -> x5, starting transfers between devices: 12.7 us -> 11.5 us  [swap(): lax.ppermute(value, 'dp', [(i, i ^ 1) for i in range(lax.axis_size('dp'))])]
  transfers between devices with their start and end apart: 13 -> 16, of which waited for: 8 -> 10; matrix products, arithmetic and copies ran while one was open for 0% -> 0% of each run, Pallas kernels for 1% -> 1%
where the time goes in v5:
time: 45 us; the launch traced here: 44.9 us
  starting transfers between devices  23.9 us (53%)
  waiting for transfers between devices  18.3 us (41%)
  Pallas kernels  1.88 us (4%)
  other arithmetic  0.62 us (1%)
    ppermute x11, waiting for transfers between devices, route(): return lax.ppermute(value, ('mod', 'dp'), pairs)  15.8 us
    ppermute x11, starting transfers between devices, route(): return lax.ppermute(value, ('mod', 'dp'), pairs)  12.4 us
    ppermute x5, starting transfers between devices, swap(): lax.ppermute(value, 'dp', [(i, i ^ 1) for i in range(lax.axis_size('dp'))])  11.5 us
    ppermute x5, waiting for transfers between devices, swap(): lax.ppermute(value, 'dp', [(i, i ^ 1) for i in range(lax.axis_size('dp'))])  2.47 us
    pallas_call x1, Pallas kernels, pack(): pl.pallas_call(pack_kernel, out_shape=[near((rows + queries.shape[0], wid...  1.29 us
  transfers between devices with their start and end apart: 16, of which 10 were waited for; matrix products, arithmetic and copies ran while one was open for 0% of the time, Pallas kernels for 1%

profile of v5, /device:TPU:0, one launch (start us, length us, event | category | flops | bytes accessed | tf_op | source)
XLA Modules:
  0.0 44.9 jit_solution(14079832581504382563)
XLA Ops:
  0.0 1.3 %pack.1 = (f32[132,512]{1,0:T(8,128)S(1)}, f32[132,512]{1,0:T(8,128)S(1)}, f32[132,512]{1,0:T(8,128)S(1)}, f32[132,512]{1,0:T(8,128)S(1)}) custom-call(f32[128,4,512]{2,1,0:T(4,128)} %rows_ref.1, f32[4,4,512]{2,1,0:T(4,128)} %queries_ref.1), custom_call_target="tpu_custom_call" | custom-call | flops 1500000000 | tf_op jit(solution)/shard_map/pack/pallas_call | solution.py:96
  1.3 0.6 %collective-permute-start = (f32[132,512]{1,0:T(8,128)S(1)}, f32[132,512]{1,0:T(8,128)S(1)}, u32[]{:S(2)}, u32[]{:S(2)}) collective-permute-start(f32[132,512]{1,0:T(8,128)S(1)} %get-tuple-element.16.two.refs_4_), channel_id=1, source_target_pairs={{0,1},{1,0},{2,3},{3,2},{4,5},{5,4},{6,7},{7,6},{8,9},{9,8},{10,11... | collective-permute-start | bytes 811016 | tf_op jit(solution)/shard_map/ppermute | solution.py:294
  1.9 2.6 %collective-permute-start.3 = (f32[132,512]{1,0:T(8,128)S(1)}, f32[132,512]{1,0:T(8,128)S(1)}, u32[]{:S(2)}, u32[]{:S(2)}) collective-permute-start(f32[132,512]{1,0:T(8,128)S(1)} %get-tuple-element.20), channel_id=1, source_target_pairs={{0,3},{1,0},{2,1},{3,2},{4,7},{5,4},{6,5},{7,6},{8,11},{9,8},{10,9... | collective-permute-start | bytes 811016 | tf_op jit(solution)/shard_map/ppermute | solution.py:294
  4.4 1.6 %collective-permute-start.4 = (f32[132,512]{1,0:T(8,128)S(1)}, f32[132,512]{1,0:T(8,128)S(1)}, u32[]{:S(2)}, u32[]{:S(2)}) collective-permute-start(f32[132,512]{1,0:T(8,128)S(1)} %get-tuple-element.20), channel_id=1, source_target_pairs={{0,8},{1,3},{2,10},{3,1},{4,12},{5,7},{6,14},{7,5},{8,0},{9,11},{1... | collective-permute-start | bytes 811016 | tf_op jit(solution)/shard_map/ppermute | solution.py:294
  6.0 0.0 copy-start
  6.0 0.4 %collective-permute-start.1 = (f32[132,512]{1,0:T(8,128)S(1)}, f32[132,512]{1,0:T(8,128)S(1)}, u32[]{:S(2)}, u32[]{:S(2)}) collective-permute-start(f32[132,512]{1,0:T(8,128)S(1)} %get-tuple-element.18), channel_id=1, source_target_pairs={{0,8},{1,5},{2,10},{3,7},{4,12},{5,1},{6,14},{7,3},{8,0},{9,13},{1... | collective-permute-start | bytes 811016 | tf_op jit(solution)/shard_map/ppermute | solution.py:294
  6.5 1.6 %collective-permute-start.2 = (f32[132,512]{1,0:T(8,128)S(1)}, f32[132,512]{1,0:T(8,128)S(1)}, u32[]{:S(2)}, u32[]{:S(2)}) collective-permute-start(f32[132,512]{1,0:T(8,128)S(1)} %get-tuple-element.19), channel_id=1, source_target_pairs={{0,8},{1,7},{2,10},{3,5},{4,12},{5,3},{6,14},{7,1},{8,0},{9,15},{1... | collective-permute-start | bytes 811016 | tf_op jit(solution)/shard_map/ppermute | solution.py:294
  8.1 0.0 collective-permute-done.one.refs_3_
  8.1 0.0 collective-permute-start.5
  8.1 3.4 %collective-permute-done.3.one.refs_5_ = f32[132,512]{1,0:T(8,128)S(1)} collective-permute-done((f32[132,512]{1,0:T(8,128)S(1)}, f32[132,512]{1,0:T(8,128)S(1)}, u32[]{:S(2)}, u32[]{:S(2)}) %collective-permute-start.3) | collective-permute-done | bytes 270368 | tf_op jit(solution)/shard_map/ppermute | solution.py:294
  11.5 3.2 %collective-permute-start.6 = (f32[132,512]{1,0:T(8,128)S(1)}, f32[132,512]{1,0:T(8,128)S(1)}, u32[]{:S(2)}, u32[]{:S(2)}) collective-permute-start(f32[132,512]{1,0:T(8,128)S(1)} %get-tuple-element.19), channel_id=1, source_target_pairs={{0,7},{1,0},{2,5},{3,2},{4,3},{5,4},{6,1},{7,6},{8,15},{9,8},{10,1... | collective-permute-start | bytes 811016 | tf_op jit(solution)/shard_map/ppermute | solution.py:294
  14.7 0.0 copy-done
  14.7 0.6 %gram.3 = (f32[256,256]{1,0:T(8,128)S(1)}, f32[512,256]{1,0:T(8,128)S(1)}, f32[8,128]{1,0:T(8,128)S(1)}) custom-call(f32[4]{0:T(128)S(1)} %copy-done, f32[132,512]{1,0:T(8,128)S(1)} %collective-permute-done.one.refs_3_, f32[132,512]{1,0:T(8,128)S(1)} %get-tuple-element.16.two.refs_4_), custom_call_target="tpu_custom_call" | custom-call | flops 600000000 | tf_op jit(solution)/shard_map/gram/pallas_call | solution.py:151
  15.2 0.0 collective-permute-done.4.two.refs_6_
  15.3 0.0 collective-permute-done.1.one.refs_8_
  15.3 1.7 %collective-permute-done.2.two.refs_10_ = f32[132,512]{1,0:T(8,128)S(1)} collective-permute-done((f32[132,512]{1,0:T(8,128)S(1)}, f32[132,512]{1,0:T(8,128)S(1)}, u32[]{:S(2)}, u32[]{:S(2)}) %collective-permute-start.2) | collective-permute-done | bytes 270368 | tf_op jit(solution)/shard_map/ppermute | solution.py:294
  17.0 0.0 collective-permute-done.5.refs_7_
  17.0 1.7 %collective-permute-done.6.refs_9_ = f32[132,512]{1,0:T(8,128)S(1)} collective-permute-done((f32[132,512]{1,0:T(8,128)S(1)}, f32[132,512]{1,0:T(8,128)S(1)}, u32[]{:S(2)}, u32[]{:S(2)}) %collective-permute-start.6) | collective-permute-done | bytes 270368 | tf_op jit(solution)/shard_map/ppermute | solution.py:294
  18.8 9.3 %collective-permute-start.7 = (f32[64,256]{1,0:T(8,128)S(1)}, f32[64,256]{1,0:T(8,128)S(1)}, u32[]{:S(2)}, u32[]{:S(2)}) collective-permute-start(f32[64,256]{1,0:T(8,128)S(1)} %get-tuple-element.28), channel_id=1, source_target_pairs={{0,1},{1,0},{2,3},{3,2},{4,5},{5,4},{6,7},{7,6},{8,9},{9,8},{10,11... | collective-permute-start | bytes 196616 | tf_op jit(solution)/shard_map/ppermute | solution.py:282
  28.0 0.1 collective-permute-start.8
  28.1 0.8 %collective-permute-done.7 = f32[64,256]{1,0:T(8,128)S(1)} collective-permute-done((f32[64,256]{1,0:T(8,128)S(1)}, f32[64,256]{1,0:T(8,128)S(1)}, u32[]{:S(2)}, u32[]{:S(2)}) %collective-permute-start.7) | collective-permute-done | bytes 65568 | tf_op jit(solution)/shard_map/ppermute | solution.py:282
  28.9 2.8 %collective-permute-done.8 = f32[64,256]{1,0:T(8,128)S(1)} collective-permute-done((f32[64,256]{1,0:T(8,128)S(1)}, f32[64,256]{1,0:T(8,128)S(1)}, u32[]{:S(2)}, u32[]{:S(2)}) %collective-permute-start.8) | collective-permute-done | bytes 65568 | tf_op jit(solution)/shard_map/ppermute | solution.py:294
  31.7 0.1 collective-permute-start.9
  31.8 1.2 %collective-permute-start.10 = (f32[32,256]{1,0:T(8,128)S(1)}, f32[32,256]{1,0:T(8,128)S(1)}, u32[]{:S(2)}, u32[]{:S(2)}) collective-permute-start(f32[32,256]{1,0:T(8,128)S(1)} %get-tuple-element.29), channel_id=1, source_target_pairs={{0,3},{1,0},{2,1},{3,2},{4,7},{5,4},{6,5},{7,6},{8,11},{9,8},{10,9... | collective-permute-start | bytes 98312 | tf_op jit(solution)/shard_map/ppermute | solution.py:294
  33.0 0.0 collective-permute-done.9
  33.0 1.6 %collective-permute-done.10 = f32[32,256]{1,0:T(8,128)S(1)} collective-permute-done((f32[32,256]{1,0:T(8,128)S(1)}, f32[32,256]{1,0:T(8,128)S(1)}, u32[]{:S(2)}, u32[]{:S(2)}) %collective-permute-start.10) | collective-permute-done | bytes 32800 | tf_op jit(solution)/shard_map/ppermute | solution.py:294
  34.6 1.1 %collective-permute-start.11 = (f32[16,256]{1,0:T(8,128)S(1)}, f32[16,256]{1,0:T(8,128)S(1)}, u32[]{:S(2)}, u32[]{:S(2)}) collective-permute-start(f32[16,256]{1,0:T(8,128)S(1)} %get-tuple-element.32), channel_id=1, source_target_pairs={{0,1},{1,0},{2,3},{3,2},{4,5},{5,4},{6,7},{7,6},{8,9},{9,8},{10,11... | collective-permute-start | bytes 49160 | tf_op jit(solution)/shard_map/ppermute | solution.py:282
  35.7 0.1 collective-permute-start.12
  35.8 0.8 %collective-permute-done.11 = f32[16,256]{1,0:T(8,128)S(1)} collective-permute-done((f32[16,256]{1,0:T(8,128)S(1)}, f32[16,256]{1,0:T(8,128)S(1)}, u32[]{:S(2)}, u32[]{:S(2)}) %collective-permute-start.11) | collective-permute-done | bytes 16416 | tf_op jit(solution)/shard_map/ppermute | solution.py:282
  36.6 3.2 %collective-permute-done.12 = f32[16,256]{1,0:T(8,128)S(1)} collective-permute-done((f32[16,256]{1,0:T(8,128)S(1)}, f32[16,256]{1,0:T(8,128)S(1)}, u32[]{:S(2)}, u32[]{:S(2)}) %collective-permute-start.12) | collective-permute-done | bytes 16416 | tf_op jit(solution)/shard_map/ppermute | solution.py:294
  39.8 0.1 collective-permute-start.13
  39.9 1.2 %collective-permute-start.14 = (f32[8,256]{1,0:T(8,128)S(1)}, f32[8,256]{1,0:T(8,128)S(1)}, u32[]{:S(2)}, u32[]{:S(2)}) collective-permute-start(f32[8,256]{1,0:T(8,128)S(1)} %get-tuple-element.33), channel_id=1, source_target_pairs={{0,9},{1,0},{2,11},{3,2},{4,13},{5,4},{6,15},{7,6},{8,1},{9,8},{10... | collective-permute-start | bytes 24584 | tf_op jit(solution)/shard_map/ppermute | solution.py:294
  41.1 0.0 collective-permute-done.13
  41.1 1.4 %collective-permute-done.14 = f32[8,256]{1,0:T(8,128)S(1)} collective-permute-done((f32[8,256]{1,0:T(8,128)S(1)}, f32[8,256]{1,0:T(8,128)S(1)}, u32[]{:S(2)}, u32[]{:S(2)}) %collective-permute-start.14) | collective-permute-done | bytes 8224 | tf_op jit(solution)/shard_map/ppermute | solution.py:294
  42.5 1.0 %collective-permute-start.15 = (f32[8,128]{1,0:T(8,128)S(1)}, f32[8,128]{1,0:T(8,128)S(1)}, u32[]{:S(2)}, u32[]{:S(2)}) collective-permute-start(f32[8,128]{1,0:T(8,128)S(1)} %slice.49), channel_id=1, source_target_pairs={{0,1},{1,0},{2,3},{3,2},{4,5},{5,4},{6,7},{7,6},{8,9},{9,8},{10,11... | collective-permute-start | bytes 12296 | tf_op jit(solution)/shard_map/ppermute | solution.py:282
  43.5 0.8 %collective-permute-done.15 = f32[8,128]{1,0:T(8,128)S(1)} collective-permute-done((f32[8,128]{1,0:T(8,128)S(1)}, f32[8,128]{1,0:T(8,128)S(1)}, u32[]{:S(2)}, u32[]{:S(2)}) %collective-permute-start.15) | collective-permute-done | bytes 4128 | tf_op jit(solution)/shard_map/ppermute | solution.py:282
  44.3 0.6 %fusion = f32[128,8]{0,1:T(8,128)} fusion(f32[8,128]{1,0:T(8,128)S(1)} %collective-permute-done.15, f32[8,256]{1,0:T(8,128)S(1)} %add.20, pred[]{:T(512)S(6)} %eq.5), kind=kLoop, calls=%fused_computation.1 | loop fusion | flops 1024 | bytes 12289 | tf_op jit(solution)/shard_map/transpose | solution.py:376
  (12 shorter events, 0.1 us)
Async XLA Ops:
  1.3 6.8 %collective-permute-start = (f32[132,512]{1,0:T(8,128)S(1)}, f32[132,512]{1,0:T(8,128)S(1)}, u32[]{:S(2)}, u32[]{:S(2)}) collective-permute-start(f32[132,512]{1,0:T(8,128)S(1)} %get-tuple-element.16.two.refs_4_), channel_id=1, source_target_pairs={{0,1},{1,0},{2,3},{3,2},{4,5},{5,4},{6,7},{7,6},{8,9},{9,8},{10,11... | collective-permute-start | bytes 811016 | tf_op jit(solution)/shard_map/ppermute | solution.py:294
  1.9 9.6 %collective-permute-start.3 = (f32[132,512]{1,0:T(8,128)S(1)}, f32[132,512]{1,0:T(8,128)S(1)}, u32[]{:S(2)}, u32[]{:S(2)}) collective-permute-start(f32[132,512]{1,0:T(8,128)S(1)} %get-tuple-element.20), channel_id=1, source_target_pairs={{0,3},{1,0},{2,1},{3,2},{4,7},{5,4},{6,5},{7,6},{8,11},{9,8},{10,9... | collective-permute-start | bytes 811016 | tf_op jit(solution)/shard_map/ppermute | solution.py:294
  4.4 10.8 %collective-permute-start.4 = (f32[132,512]{1,0:T(8,128)S(1)}, f32[132,512]{1,0:T(8,128)S(1)}, u32[]{:S(2)}, u32[]{:S(2)}) collective-permute-start(f32[132,512]{1,0:T(8,128)S(1)} %get-tuple-element.20), channel_id=1, source_target_pairs={{0,8},{1,3},{2,10},{3,1},{4,12},{5,7},{6,14},{7,5},{8,0},{9,11},{1... | collective-permute-start | bytes 811016 | tf_op jit(solution)/shard_map/ppermute | solution.py:294
  6.0 8.6 %copy-start = (f32[4]{0:T(128)S(1)}, f32[4]{0:T(128)}, u32[]{:S(2)}) copy-start(f32[4]{0:T(128)} %damping_ref.1) | copy-start | bytes 52
  6.0 9.2 %collective-permute-start.1 = (f32[132,512]{1,0:T(8,128)S(1)}, f32[132,512]{1,0:T(8,128)S(1)}, u32[]{:S(2)}, u32[]{:S(2)}) collective-permute-start(f32[132,512]{1,0:T(8,128)S(1)} %get-tuple-element.18), channel_id=1, source_target_pairs={{0,8},{1,5},{2,10},{3,7},{4,12},{5,1},{6,14},{7,3},{8,0},{9,13},{1... | collective-permute-start | bytes 811016 | tf_op jit(solution)/shard_map/ppermute | solution.py:294
  6.5 10.5 %collective-permute-start.2 = (f32[132,512]{1,0:T(8,128)S(1)}, f32[132,512]{1,0:T(8,128)S(1)}, u32[]{:S(2)}, u32[]{:S(2)}) collective-permute-start(f32[132,512]{1,0:T(8,128)S(1)} %get-tuple-element.19), channel_id=1, source_target_pairs={{0,8},{1,7},{2,10},{3,5},{4,12},{5,3},{6,14},{7,1},{8,0},{9,15},{1... | collective-permute-start | bytes 811016 | tf_op jit(solution)/shard_map/ppermute | solution.py:294
  8.1 8.9 %collective-permute-start.5 = (f32[132,512]{1,0:T(8,128)S(1)}, f32[132,512]{1,0:T(8,128)S(1)}, u32[]{:S(2)}, u32[]{:S(2)}) collective-permute-start(f32[132,512]{1,0:T(8,128)S(1)} %get-tuple-element.18), channel_id=1, source_target_pairs={{0,5},{1,0},{2,7},{3,2},{4,1},{5,4},{6,3},{7,6},{8,13},{9,8},{10,1... | collective-permute-start | bytes 811016 | tf_op jit(solution)/shard_map/ppermute | solution.py:294
  11.5 7.2 %collective-permute-start.6 = (f32[132,512]{1,0:T(8,128)S(1)}, f32[132,512]{1,0:T(8,128)S(1)}, u32[]{:S(2)}, u32[]{:S(2)}) collective-permute-start(f32[132,512]{1,0:T(8,128)S(1)} %get-tuple-element.19), channel_id=1, source_target_pairs={{0,7},{1,0},{2,5},{3,2},{4,3},{5,4},{6,1},{7,6},{8,15},{9,8},{10,1... | collective-permute-start | bytes 811016 | tf_op jit(solution)/shard_map/ppermute | solution.py:294
  18.8 10.2 %collective-permute-start.7 = (f32[64,256]{1,0:T(8,128)S(1)}, f32[64,256]{1,0:T(8,128)S(1)}, u32[]{:S(2)}, u32[]{:S(2)}) collective-permute-start(f32[64,256]{1,0:T(8,128)S(1)} %get-tuple-element.28), channel_id=1, source_target_pairs={{0,1},{1,0},{2,3},{3,2},{4,5},{5,4},{6,7},{7,6},{8,9},{9,8},{10,11... | collective-permute-start | bytes 196616 | tf_op jit(solution)/shard_map/ppermute | solution.py:282
  28.0 3.7 %collective-permute-start.8 = (f32[64,256]{1,0:T(8,128)S(1)}, f32[64,256]{1,0:T(8,128)S(1)}, u32[]{:S(2)}, u32[]{:S(2)}) collective-permute-start(f32[64,256]{1,0:T(8,128)S(1)} %get-tuple-element.27), channel_id=1, source_target_pairs={{0,1},{1,4},{2,3},{3,6},{4,5},{5,0},{6,7},{7,2},{8,9},{9,12},{10,1... | collective-permute-start | bytes 196616 | tf_op jit(solution)/shard_map/ppermute | solution.py:294
  31.7 1.3 %collective-permute-start.9 = (f32[32,256]{1,0:T(8,128)S(1)}, f32[32,256]{1,0:T(8,128)S(1)}, u32[]{:S(2)}, u32[]{:S(2)}) collective-permute-start(f32[32,256]{1,0:T(8,128)S(1)} %get-tuple-element.30), channel_id=1, source_target_pairs={{0,1},{1,0},{2,3},{3,2},{4,5},{5,4},{6,7},{7,6},{8,9},{9,8},{10,11... | collective-permute-start | bytes 98312 | tf_op jit(solution)/shard_map/ppermute | solution.py:282
  31.8 2.8 %collective-permute-start.10 = (f32[32,256]{1,0:T(8,128)S(1)}, f32[32,256]{1,0:T(8,128)S(1)}, u32[]{:S(2)}, u32[]{:S(2)}) collective-permute-start(f32[32,256]{1,0:T(8,128)S(1)} %get-tuple-element.29), channel_id=1, source_target_pairs={{0,3},{1,0},{2,1},{3,2},{4,7},{5,4},{6,5},{7,6},{8,11},{9,8},{10,9... | collective-permute-start | bytes 98312 | tf_op jit(solution)/shard_map/ppermute | solution.py:294
  34.6 2.0 %collective-permute-start.11 = (f32[16,256]{1,0:T(8,128)S(1)}, f32[16,256]{1,0:T(8,128)S(1)}, u32[]{:S(2)}, u32[]{:S(2)}) collective-permute-start(f32[16,256]{1,0:T(8,128)S(1)} %get-tuple-element.32), channel_id=1, source_target_pairs={{0,1},{1,0},{2,3},{3,2},{4,5},{5,4},{6,7},{7,6},{8,9},{9,8},{10,11... | collective-permute-start | bytes 49160 | tf_op jit(solution)/shard_map/ppermute | solution.py:282
  35.7 4.1 %collective-permute-start.12 = (f32[16,256]{1,0:T(8,128)S(1)}, f32[16,256]{1,0:T(8,128)S(1)}, u32[]{:S(2)}, u32[]{:S(2)}) collective-permute-start(f32[16,256]{1,0:T(8,128)S(1)} %get-tuple-element.31), channel_id=1, source_target_pairs={{0,1},{1,16},{2,3},{3,18},{4,5},{5,20},{6,7},{7,22},{8,9},{9,24},{... | collective-permute-start | bytes 49160 | tf_op jit(solution)/shard_map/ppermute | solution.py:294
  39.8 1.3 %collective-permute-start.13 = (f32[8,256]{1,0:T(8,128)S(1)}, f32[8,256]{1,0:T(8,128)S(1)}, u32[]{:S(2)}, u32[]{:S(2)}) collective-permute-start(f32[8,256]{1,0:T(8,128)S(1)} %get-tuple-element.34), channel_id=1, source_target_pairs={{0,1},{1,0},{2,3},{3,2},{4,5},{5,4},{6,7},{7,6},{8,9},{9,8},{10,11... | collective-permute-start | bytes 24584 | tf_op jit(solution)/shard_map/ppermute | solution.py:282
  39.9 2.6 %collective-permute-start.14 = (f32[8,256]{1,0:T(8,128)S(1)}, f32[8,256]{1,0:T(8,128)S(1)}, u32[]{:S(2)}, u32[]{:S(2)}) collective-permute-start(f32[8,256]{1,0:T(8,128)S(1)} %get-tuple-element.33), channel_id=1, source_target_pairs={{0,9},{1,0},{2,11},{3,2},{4,13},{5,4},{6,15},{7,6},{8,1},{9,8},{10... | collective-permute-start | bytes 24584 | tf_op jit(solution)/shard_map/ppermute | solution.py:294
  42.5 1.8 %collective-permute-start.15 = (f32[8,128]{1,0:T(8,128)S(1)}, f32[8,128]{1,0:T(8,128)S(1)}, u32[]{:S(2)}, u32[]{:S(2)}) collective-permute-start(f32[8,128]{1,0:T(8,128)S(1)} %slice.49), channel_id=1, source_target_pairs={{0,1},{1,0},{2,3},{3,2},{4,5},{5,4},{6,7},{7,6},{8,9},{9,8},{10,11... | collective-permute-start | bytes 12296 | tf_op jit(solution)/shard_map/ppermute | solution.py:282

commit v6 on v4

--- a/solution.py
+++ b/solution.py
@@ -195,25 +195,26 @@
 
     left[...] = left_ref[...]
     right[...] = right_ref[...]
-    add_gram(rows, blocks[-1], left, right, stack)
+    add_gram(rows, [block[1 - SOLVER] for block in blocks[-2:]], left, right, stack)
 
     diagonal = lax.broadcasted_iota(jnp.int32, (half, half), 0) == lax.broadcasted_iota(
         jnp.int32, (half, half), 1
     )
     eye = diagonal.astype(jnp.float32)
     first, cross, last = left[...], right[0:half], right[half:]
-    trace = jnp.sum((first + last) * eye, keepdims=True).reshape(1, 1) / total_rows
-    shift = damp_ref[0:1, 0:1] * trace / width
-    first = first / total_rows + shift * eye
-    last = last / total_rows + shift * eye
-    cross = cross / total_rows
+    trace = jnp.sum((first + last) * eye, keepdims=True).reshape(1, 1)
+    shift = (damp_ref[0:1, 0:1] * trace * (1.0 / width)) * eye
+    first = first + shift
+    last = last + shift
     squares = first * first + last * last + 2.0 * (cross * cross)
-    inverse_norm = lax.rsqrt(jnp.sum(squares, keepdims=True).reshape(1, 1) + epsilon)
-    cross = cross * inverse_norm
-    state[0:half, 0:half] = first * inverse_norm
+    squares = jnp.sum(squares, keepdims=True).reshape(1, 1) * (1.0 / total_rows**2)
+    inverse_norm = lax.rsqrt(squares + epsilon)
+    per_row = inverse_norm * (1.0 / total_rows)
+    cross = cross * per_row
+    state[0:half, 0:half] = first * per_row
     state[0:half, half:] = cross
     state[half:width, 0:half] = cross.T
-    state[half:width, half:] = last * inverse_norm
+    state[half:width, half:] = last * per_row
     for offset in range(groups):
         source = lax.bitwise_xor(group_here, jnp.int32(offset))
         state[width + offset * group : width + (offset + 1) * group] = (
@@ -335,8 +336,9 @@
         arrived[kind, offset] = mover(packed[offset], offset)
     blocks = [[arrived["cross", offset], arrived["same", offset]] for offset in range(chips)]
     *given, damp = gram(rows, blocks[0], damping=damping)
-    for offset in range(1, chips - 1):
+    for offset in range(1, chips - 2):
         given = gram(rows, blocks[offset], given)
+    given = gram(rows, [block[SOLVER] for block in blocks[-2:]], given)
     sizes = (
         chips,
         rows,

time: 41.3 us -> 41.3 us (level)
  starting transfers between devices: 20.8 us -> 24.6 us
  waiting for transfers between devices: 17.8 us -> 14 us
    ppermute x6, waiting for transfers between devices: 10.3 us -> 7.08 us  [swap(): lax.ppermute(value, axis, [(i, i ^ offset) for i in range(lax.axis_size(a...]
    ppermute x6, starting transfers between devices: 12.7 us -> 14.7 us  [swap(): lax.ppermute(value, axis, [(i, i ^ offset) for i in range(lax.axis_size(a...]
    ppermute x7, starting transfers between devices: 8.13 us -> 9.91 us  [route(): return lax.ppermute(value, ('mod', 'dp'), pairs)]
    ppermute x7, waiting for transfers between devices: 7.49 us -> 6.89 us  [route(): return lax.ppermute(value, ('mod', 'dp'), pairs)]
  transfers between devices with their start and end apart: 13 -> 13, of which waited for: 8 -> 9; matrix products, arithmetic and copies ran while one was open for 0% -> 0% of each run, Pallas kernels for 1% -> 1%
where the time goes in v6:
time: 41.3 us; the launch traced here: 41.1 us
  starting transfers between devices  24.6 us (60%)
  waiting for transfers between devices  14 us (34%)
  Pallas kernels  1.88 us (5%)
  other arithmetic  0.61 us (1%)
    ppermute x6, starting transfers between devices, swap(): lax.ppermute(value, axis, [(i, i ^ offset) for i in range(lax.axis_size(a...  14.7 us
    ppermute x7, starting transfers between devices, route(): return lax.ppermute(value, ('mod', 'dp'), pairs)  9.91 us
    ppermute x6, waiting for transfers between devices, swap(): lax.ppermute(value, axis, [(i, i ^ offset) for i in range(lax.axis_size(a...  7.08 us
    ppermute x7, waiting for transfers between devices, route(): return lax.ppermute(value, ('mod', 'dp'), pairs)  6.89 us
    pallas_call x1, Pallas kernels, pack(): pl.pallas_call(pack_kernel, out_shape=[near((rows + queries.shape[0], wid...  1.29 us
  transfers between devices with their start and end apart: 13, of which 9 were waited for; matrix products, arithmetic and copies ran while one was open for 0% of the time, Pallas kernels for 1%

profile of v6, /device:TPU:0, one launch (start us, length us, event | category | flops | bytes accessed | tf_op | source)
XLA Modules:
  0.0 41.1 jit_solution(6754375547396378286)
XLA Ops:
  0.0 1.3 %pack.1 = (f32[132,512]{1,0:T(8,128)S(1)}, f32[132,512]{1,0:T(8,128)S(1)}, f32[132,512]{1,0:T(8,128)S(1)}, f32[132,512]{1,0:T(8,128)S(1)}) custom-call(f32[128,4,512]{2,1,0:T(4,128)} %rows_ref.1, f32[4,4,512]{2,1,0:T(4,128)} %queries_ref.1), custom_call_target="tpu_custom_call" | custom-call | flops 1500000000 | tf_op jit(solution)/shard_map/pack/pallas_call | solution.py:96
  1.3 0.6 %collective-permute-start = (f32[132,512]{1,0:T(8,128)S(1)}, f32[132,512]{1,0:T(8,128)S(1)}, u32[]{:S(2)}, u32[]{:S(2)}) collective-permute-start(f32[132,512]{1,0:T(8,128)S(1)} %get-tuple-element.20.two.refs_4_), channel_id=1, source_target_pairs={{0,1},{1,0},{2,3},{3,2},{4,5},{5,4},{6,7},{7,6},{8,9},{9,8},{10,11... | collective-permute-start | bytes 811016 | tf_op jit(solution)/shard_map/ppermute | solution.py:297
  1.9 2.6 %collective-permute-start.3 = (f32[132,512]{1,0:T(8,128)S(1)}, f32[132,512]{1,0:T(8,128)S(1)}, u32[]{:S(2)}, u32[]{:S(2)}) collective-permute-start(f32[132,512]{1,0:T(8,128)S(1)} %get-tuple-element.24), channel_id=1, source_target_pairs={{0,3},{1,0},{2,1},{3,2},{4,7},{5,4},{6,5},{7,6},{8,11},{9,8},{10,9... | collective-permute-start | bytes 811016 | tf_op jit(solution)/shard_map/ppermute | solution.py:297
  4.4 1.6 %collective-permute-start.4 = (f32[132,512]{1,0:T(8,128)S(1)}, f32[132,512]{1,0:T(8,128)S(1)}, u32[]{:S(2)}, u32[]{:S(2)}) collective-permute-start(f32[132,512]{1,0:T(8,128)S(1)} %get-tuple-element.24), channel_id=1, source_target_pairs={{0,8},{1,3},{2,10},{3,1},{4,12},{5,7},{6,14},{7,5},{8,0},{9,11},{1... | collective-permute-start | bytes 811016 | tf_op jit(solution)/shard_map/ppermute | solution.py:297
  6.0 0.0 copy-start
  6.0 0.4 %collective-permute-start.1 = (f32[132,512]{1,0:T(8,128)S(1)}, f32[132,512]{1,0:T(8,128)S(1)}, u32[]{:S(2)}, u32[]{:S(2)}) collective-permute-start(f32[132,512]{1,0:T(8,128)S(1)} %get-tuple-element.22), channel_id=1, source_target_pairs={{0,8},{1,5},{2,10},{3,7},{4,12},{5,1},{6,14},{7,3},{8,0},{9,13},{1... | collective-permute-start | bytes 811016 | tf_op jit(solution)/shard_map/ppermute | solution.py:297
  6.5 1.6 %collective-permute-start.2 = (f32[132,512]{1,0:T(8,128)S(1)}, f32[132,512]{1,0:T(8,128)S(1)}, u32[]{:S(2)}, u32[]{:S(2)}) collective-permute-start(f32[132,512]{1,0:T(8,128)S(1)} %get-tuple-element.23), channel_id=1, source_target_pairs={{0,8},{1,7},{2,10},{3,5},{4,12},{5,3},{6,14},{7,1},{8,0},{9,15},{1... | collective-permute-start | bytes 811016 | tf_op jit(solution)/shard_map/ppermute | solution.py:297
  8.1 0.0 collective-permute-done.one.refs_3_
  8.1 0.0 collective-permute-start.5
  8.1 3.4 %collective-permute-done.3.one.refs_5_ = f32[132,512]{1,0:T(8,128)S(1)} collective-permute-done((f32[132,512]{1,0:T(8,128)S(1)}, f32[132,512]{1,0:T(8,128)S(1)}, u32[]{:S(2)}, u32[]{:S(2)}) %collective-permute-start.3) | collective-permute-done | bytes 270368 | tf_op jit(solution)/shard_map/ppermute | solution.py:297
  11.5 3.2 %collective-permute-start.6 = (f32[132,512]{1,0:T(8,128)S(1)}, f32[132,512]{1,0:T(8,128)S(1)}, u32[]{:S(2)}, u32[]{:S(2)}) collective-permute-start(f32[132,512]{1,0:T(8,128)S(1)} %get-tuple-element.23), channel_id=1, source_target_pairs={{0,7},{1,0},{2,5},{3,2},{4,3},{5,4},{6,1},{7,6},{8,15},{9,8},{10,1... | collective-permute-start | bytes 811016 | tf_op jit(solution)/shard_map/ppermute | solution.py:297
  14.7 0.0 copy-done
  14.7 0.6 %gram.3 = (f32[256,256]{1,0:T(8,128)S(1)}, f32[512,256]{1,0:T(8,128)S(1)}, f32[8,128]{1,0:T(8,128)S(1)}) custom-call(f32[4]{0:T(128)S(1)} %copy-done, f32[132,512]{1,0:T(8,128)S(1)} %collective-permute-done.one.refs_3_, f32[132,512]{1,0:T(8,128)S(1)} %get-tuple-element.20.two.refs_4_), custom_call_target="tpu_custom_call" | custom-call | flops 600000000 | tf_op jit(solution)/shard_map/gram/pallas_call | solution.py:151
  15.2 0.0 collective-permute-done.4.two.refs_6_
  15.3 0.0 collective-permute-done.1.one.refs_8_
  15.3 1.7 %collective-permute-done.2.two.refs_10_ = f32[132,512]{1,0:T(8,128)S(1)} collective-permute-done((f32[132,512]{1,0:T(8,128)S(1)}, f32[132,512]{1,0:T(8,128)S(1)}, u32[]{:S(2)}, u32[]{:S(2)}) %collective-permute-start.2) | collective-permute-done | bytes 270368 | tf_op jit(solution)/shard_map/ppermute | solution.py:297
  17.0 0.0 collective-permute-done.5.refs_7_
  17.0 1.7 %collective-permute-done.6.refs_9_ = f32[132,512]{1,0:T(8,128)S(1)} collective-permute-done((f32[132,512]{1,0:T(8,128)S(1)}, f32[132,512]{1,0:T(8,128)S(1)}, u32[]{:S(2)}, u32[]{:S(2)}) %collective-permute-start.6) | collective-permute-done | bytes 270368 | tf_op jit(solution)/shard_map/ppermute | solution.py:297
  18.7 0.6 %collective-permute-start.9 = (f32[32,256]{1,0:T(8,128)S(1)}, f32[32,256]{1,0:T(8,128)S(1)}, u32[]{:S(2)}, u32[]{:S(2)}) collective-permute-start(f32[32,256]{1,0:T(8,128)S(1)} %get-tuple-element.34), channel_id=1, source_target_pairs={{0,2},{1,3},{2,0},{3,1},{4,6},{5,7},{6,4},{7,5},{8,10},{9,11},{10,... | collective-permute-start | bytes 98312 | tf_op jit(solution)/shard_map/ppermute | solution.py:285
  19.3 0.4 %collective-permute-start.8 = (f32[32,256]{1,0:T(8,128)S(1)}, f32[32,256]{1,0:T(8,128)S(1)}, u32[]{:S(2)}, u32[]{:S(2)}) collective-permute-start(f32[32,256]{1,0:T(8,128)S(1)} %get-tuple-element.33), channel_id=1, source_target_pairs={{0,4},{1,5},{2,6},{3,7},{4,0},{5,1},{6,2},{7,3},{8,12},{9,13},{10,... | collective-permute-start | bytes 98312 | tf_op jit(solution)/shard_map/ppermute | solution.py:285
  19.8 2.5 %collective-permute-start.7 = (f32[32,256]{1,0:T(8,128)S(1)}, f32[32,256]{1,0:T(8,128)S(1)}, u32[]{:S(2)}, u32[]{:S(2)}) collective-permute-start(f32[32,256]{1,0:T(8,128)S(1)} %get-tuple-element.32), channel_id=1, source_target_pairs={{0,6},{1,7},{2,4},{3,5},{4,2},{5,3},{6,0},{7,1},{8,14},{9,15},{10,... | collective-permute-start | bytes 98312 | tf_op jit(solution)/shard_map/ppermute | solution.py:285
  22.3 0.4 %collective-permute-done.9 = f32[32,256]{1,0:T(8,128)S(1)} collective-permute-done((f32[32,256]{1,0:T(8,128)S(1)}, f32[32,256]{1,0:T(8,128)S(1)}, u32[]{:S(2)}, u32[]{:S(2)}) %collective-permute-start.9) | collective-permute-done | bytes 32800 | tf_op jit(solution)/shard_map/ppermute | solution.py:285
  22.7 0.5 %collective-permute-done.8 = f32[32,256]{1,0:T(8,128)S(1)} collective-permute-done((f32[32,256]{1,0:T(8,128)S(1)}, f32[32,256]{1,0:T(8,128)S(1)}, u32[]{:S(2)}, u32[]{:S(2)}) %collective-permute-start.8) | collective-permute-done | bytes 32800 | tf_op jit(solution)/shard_map/ppermute | solution.py:285
  23.3 1.3 %collective-permute-done.7 = f32[32,256]{1,0:T(8,128)S(1)} collective-permute-done((f32[32,256]{1,0:T(8,128)S(1)}, f32[32,256]{1,0:T(8,128)S(1)}, u32[]{:S(2)}, u32[]{:S(2)}) %collective-permute-start.7) | collective-permute-done | bytes 32800 | tf_op jit(solution)/shard_map/ppermute | solution.py:285
  24.6 2.8 %collective-permute-start.10 = (f32[16,256]{1,0:T(8,128)S(1)}, f32[16,256]{1,0:T(8,128)S(1)}, u32[]{:S(2)}, u32[]{:S(2)}) collective-permute-start(f32[16,256]{1,0:T(8,128)S(1)} %slice.25), channel_id=1, source_target_pairs={{0,16},{8,24},{16,0},{24,8},{1,17},{9,25},{17,1},{25,9},{2,18},{10... | collective-permute-start | bytes 49160 | tf_op jit(solution)/shard_map/ppermute | solution.py:285
  27.4 1.9 %collective-permute-done.10 = f32[16,256]{1,0:T(8,128)S(1)} collective-permute-done((f32[16,256]{1,0:T(8,128)S(1)}, f32[16,256]{1,0:T(8,128)S(1)}, u32[]{:S(2)}, u32[]{:S(2)}) %collective-permute-start.10) | collective-permute-done | bytes 16416 | tf_op jit(solution)/shard_map/ppermute | solution.py:285
  29.3 1.6 %collective-permute-start.11 = (f32[8,256]{1,0:T(8,128)S(1)}, f32[8,256]{1,0:T(8,128)S(1)}, u32[]{:S(2)}, u32[]{:S(2)}) collective-permute-start(f32[8,256]{1,0:T(8,128)S(1)} %slice.27), channel_id=1, source_target_pairs={{0,8},{8,0},{16,24},{24,16},{1,9},{9,1},{17,25},{25,17},{2,10},{10... | collective-permute-start | bytes 24584 | tf_op jit(solution)/shard_map/ppermute | solution.py:285
  31.0 2.0 %collective-permute-done.11 = f32[8,256]{1,0:T(8,128)S(1)} collective-permute-done((f32[8,256]{1,0:T(8,128)S(1)}, f32[8,256]{1,0:T(8,128)S(1)}, u32[]{:S(2)}, u32[]{:S(2)}) %collective-permute-start.11) | collective-permute-done | bytes 8224 | tf_op jit(solution)/shard_map/ppermute | solution.py:285
  33.0 6.7 %collective-permute-start.12 = (f32[8,128]{1,0:T(8,128)S(1)}, f32[8,128]{1,0:T(8,128)S(1)}, u32[]{:S(2)}, u32[]{:S(2)}) collective-permute-start(f32[8,128]{1,0:T(8,128)S(1)} %slice.29), channel_id=1, source_target_pairs={{0,1},{1,0},{2,3},{3,2},{4,5},{5,4},{6,7},{7,6},{8,9},{9,8},{10,11... | collective-permute-start | bytes 12296 | tf_op jit(solution)/shard_map/ppermute | solution.py:285
  39.7 0.8 %collective-permute-done.12 = f32[8,128]{1,0:T(8,128)S(1)} collective-permute-done((f32[8,128]{1,0:T(8,128)S(1)}, f32[8,128]{1,0:T(8,128)S(1)}, u32[]{:S(2)}, u32[]{:S(2)}) %collective-permute-start.12) | collective-permute-done | bytes 4128 | tf_op jit(solution)/shard_map/ppermute | solution.py:285
  40.5 0.6 %fusion = f32[128,8]{0,1:T(8,128)} fusion(f32[8,128]{1,0:T(8,128)S(1)} %collective-permute-done.12, f32[8,256]{1,0:T(8,128)S(1)} %slice_add_fusion.1, pred[]{:T(512)S(6)} %eq.5), kind=kLoop, calls=%fused_computation.4 | loop fusion | flops 1024 | bytes 12289 | tf_op jit(solution)/shard_map/transpose | solution.py:361
  (9 shorter events, 0.1 us)
Async XLA Ops:
  1.3 6.8 %collective-permute-start = (f32[132,512]{1,0:T(8,128)S(1)}, f32[132,512]{1,0:T(8,128)S(1)}, u32[]{:S(2)}, u32[]{:S(2)}) collective-permute-start(f32[132,512]{1,0:T(8,128)S(1)} %get-tuple-element.20.two.refs_4_), channel_id=1, source_target_pairs={{0,1},{1,0},{2,3},{3,2},{4,5},{5,4},{6,7},{7,6},{8,9},{9,8},{10,11... | collective-permute-start | bytes 811016 | tf_op jit(solution)/shard_map/ppermute | solution.py:297
  1.9 9.6 %collective-permute-start.3 = (f32[132,512]{1,0:T(8,128)S(1)}, f32[132,512]{1,0:T(8,128)S(1)}, u32[]{:S(2)}, u32[]{:S(2)}) collective-permute-start(f32[132,512]{1,0:T(8,128)S(1)} %get-tuple-element.24), channel_id=1, source_target_pairs={{0,3},{1,0},{2,1},{3,2},{4,7},{5,4},{6,5},{7,6},{8,11},{9,8},{10,9... | collective-permute-start | bytes 811016 | tf_op jit(solution)/shard_map/ppermute | solution.py:297
  4.4 10.8 %collective-permute-start.4 = (f32[132,512]{1,0:T(8,128)S(1)}, f32[132,512]{1,0:T(8,128)S(1)}, u32[]{:S(2)}, u32[]{:S(2)}) collective-permute-start(f32[132,512]{1,0:T(8,128)S(1)} %get-tuple-element.24), channel_id=1, source_target_pairs={{0,8},{1,3},{2,10},{3,1},{4,12},{5,7},{6,14},{7,5},{8,0},{9,11},{1... | collective-permute-start | bytes 811016 | tf_op jit(solution)/shard_map/ppermute | solution.py:297
  6.0 8.6 %copy-start = (f32[4]{0:T(128)S(1)}, f32[4]{0:T(128)}, u32[]{:S(2)}) copy-start(f32[4]{0:T(128)} %damping_ref.1) | copy-start | bytes 52
  6.0 9.2 %collective-permute-start.1 = (f32[132,512]{1,0:T(8,128)S(1)}, f32[132,512]{1,0:T(8,128)S(1)}, u32[]{:S(2)}, u32[]{:S(2)}) collective-permute-start(f32[132,512]{1,0:T(8,128)S(1)} %get-tuple-element.22), channel_id=1, source_target_pairs={{0,8},{1,5},{2,10},{3,7},{4,12},{5,1},{6,14},{7,3},{8,0},{9,13},{1... | collective-permute-start | bytes 811016 | tf_op jit(solution)/shard_map/ppermute | solution.py:297
  6.5 10.5 %collective-permute-start.2 = (f32[132,512]{1,0:T(8,128)S(1)}, f32[132,512]{1,0:T(8,128)S(1)}, u32[]{:S(2)}, u32[]{:S(2)}) collective-permute-start(f32[132,512]{1,0:T(8,128)S(1)} %get-tuple-element.23), channel_id=1, source_target_pairs={{0,8},{1,7},{2,10},{3,5},{4,12},{5,3},{6,14},{7,1},{8,0},{9,15},{1... | collective-permute-start | bytes 811016 | tf_op jit(solution)/shard_map/ppermute | solution.py:297
  8.1 8.9 %collective-permute-start.5 = (f32[132,512]{1,0:T(8,128)S(1)}, f32[132,512]{1,0:T(8,128)S(1)}, u32[]{:S(2)}, u32[]{:S(2)}) collective-permute-start(f32[132,512]{1,0:T(8,128)S(1)} %get-tuple-element.22), channel_id=1, source_target_pairs={{0,5},{1,0},{2,7},{3,2},{4,1},{5,4},{6,3},{7,6},{8,13},{9,8},{10,1... | collective-permute-start | bytes 811016 | tf_op jit(solution)/shard_map/ppermute | solution.py:297
  11.5 7.2 %collective-permute-start.6 = (f32[132,512]{1,0:T(8,128)S(1)}, f32[132,512]{1,0:T(8,128)S(1)}, u32[]{:S(2)}, u32[]{:S(2)}) collective-permute-start(f32[132,512]{1,0:T(8,128)S(1)} %get-tuple-element.23), channel_id=1, source_target_pairs={{0,7},{1,0},{2,5},{3,2},{4,3},{5,4},{6,1},{7,6},{8,15},{9,8},{10,1... | collective-permute-start | bytes 811016 | tf_op jit(solution)/shard_map/ppermute | solution.py:297
  18.7 4.0 %collective-permute-start.9 = (f32[32,256]{1,0:T(8,128)S(1)}, f32[32,256]{1,0:T(8,128)S(1)}, u32[]{:S(2)}, u32[]{:S(2)}) collective-permute-start(f32[32,256]{1,0:T(8,128)S(1)} %get-tuple-element.34), channel_id=1, source_target_pairs={{0,2},{1,3},{2,0},{3,1},{4,6},{5,7},{6,4},{7,5},{8,10},{9,11},{10,... | collective-permute-start | bytes 98312 | tf_op jit(solution)/shard_map/ppermute | solution.py:285
  19.3 3.9 %collective-permute-start.8 = (f32[32,256]{1,0:T(8,128)S(1)}, f32[32,256]{1,0:T(8,128)S(1)}, u32[]{:S(2)}, u32[]{:S(2)}) collective-permute-start(f32[32,256]{1,0:T(8,128)S(1)} %get-tuple-element.33), channel_id=1, source_target_pairs={{0,4},{1,5},{2,6},{3,7},{4,0},{5,1},{6,2},{7,3},{8,12},{9,13},{10,... | collective-permute-start | bytes 98312 | tf_op jit(solution)/shard_map/ppermute | solution.py:285
  19.8 4.8 %collective-permute-start.7 = (f32[32,256]{1,0:T(8,128)S(1)}, f32[32,256]{1,0:T(8,128)S(1)}, u32[]{:S(2)}, u32[]{:S(2)}) collective-permute-start(f32[32,256]{1,0:T(8,128)S(1)} %get-tuple-element.32), channel_id=1, source_target_pairs={{0,6},{1,7},{2,4},{3,5},{4,2},{5,3},{6,0},{7,1},{8,14},{9,15},{10,... | collective-permute-start | bytes 98312 | tf_op jit(solution)/shard_map/ppermute | solution.py:285
  24.6 4.7 %collective-permute-start.10 = (f32[16,256]{1,0:T(8,128)S(1)}, f32[16,256]{1,0:T(8,128)S(1)}, u32[]{:S(2)}, u32[]{:S(2)}) collective-permute-start(f32[16,256]{1,0:T(8,128)S(1)} %slice.25), channel_id=1, source_target_pairs={{0,16},{8,24},{16,0},{24,8},{1,17},{9,25},{17,1},{25,9},{2,18},{10... | collective-permute-start | bytes 49160 | tf_op jit(solution)/shard_map/ppermute | solution.py:285
  29.3 3.7 %collective-permute-start.11 = (f32[8,256]{1,0:T(8,128)S(1)}, f32[8,256]{1,0:T(8,128)S(1)}, u32[]{:S(2)}, u32[]{:S(2)}) collective-permute-start(f32[8,256]{1,0:T(8,128)S(1)} %slice.27), channel_id=1, source_target_pairs={{0,8},{8,0},{16,24},{24,16},{1,9},{9,1},{17,25},{25,17},{2,10},{10... | collective-permute-start | bytes 24584 | tf_op jit(solution)/shard_map/ppermute | solution.py:285
  33.0 7.5 %collective-permute-start.12 = (f32[8,128]{1,0:T(8,128)S(1)}, f32[8,128]{1,0:T(8,128)S(1)}, u32[]{:S(2)}, u32[]{:S(2)}) collective-permute-start(f32[8,128]{1,0:T(8,128)S(1)} %slice.29), channel_id=1, source_target_pairs={{0,1},{1,0},{2,3},{3,2},{4,5},{5,4},{6,7},{7,6},{8,9},{9,8},{10,11... | collective-permute-start | bytes 12296 | tf_op jit(solution)/shard_map/ppermute | solution.py:285

commit v7 on v6

--- a/solution.py
+++ b/solution.py
@@ -316,12 +316,8 @@
 
 
 def sequence(chips):
-    steps = []
-    for first in range(1, chips, 2):
-        offsets = range(first, min(first + 2, chips))
-        steps += [("same", offset) for offset in offsets]
-        steps += [("cross", offset) for offset in offsets]
-    return steps + [("cross", 0)]
+    same = [("same", offset) for offset in [chips - 1, *range(1, chips - 1)]]
+    return same + [("cross", offset) for offset in range(1, chips)]
 
 
 def influence(train_grads, queries, damping):
@@ -331,14 +327,15 @@
     chips = devices // CORES
     packed = pack(train_grads, queries)
     arrived = {("same", 0): packed[0]}
-    for kind, offset in sequence(chips):
+    steps = sequence(chips)
+    for kind, offset in steps + [("cross", 0)]:
         mover = same_core if kind == "same" else cross_core
         arrived[kind, offset] = mover(packed[offset], offset)
     blocks = [[arrived["cross", offset], arrived["same", offset]] for offset in range(chips)]
     *given, damp = gram(rows, blocks[0], damping=damping)
-    for offset in range(1, chips - 2):
-        given = gram(rows, blocks[offset], given)
-    given = gram(rows, [block[SOLVER] for block in blocks[-2:]], given)
+    for place in range(1, chips - 1):
+        pair = [arrived[step] for step in steps[2 * place - 2 : 2 * place]]
+        given = gram(rows, pair, given)
     sizes = (
         chips,
         rows,

time: 41.3 us -> 40.4 us (0.978)
  waiting for transfers between devices: 14 us -> 12.4 us
  starting transfers between devices: 24.6 us -> 25.4 us
    ppermute x7, waiting for transfers between devices: 6.89 us -> 5.67 us  [route(): return lax.ppermute(value, ('mod', 'dp'), pairs)]
where the time goes in v7:
time: 40.4 us; the launch traced here: 40.3 us
  starting transfers between devices  25.4 us (63%)
  waiting for transfers between devices  12.4 us (31%)
  Pallas kernels  1.88 us (5%)
  other arithmetic  0.61 us (2%)
    ppermute x6, starting transfers between devices, swap(): lax.ppermute(value, axis, [(i, i ^ offset) for i in range(lax.axis_size(a...  15.1 us
    ppermute x7, starting transfers between devices, route(): return lax.ppermute(value, ('mod', 'dp'), pairs)  10.3 us
    ppermute x6, waiting for transfers between devices, swap(): lax.ppermute(value, axis, [(i, i ^ offset) for i in range(lax.axis_size(a...  6.7 us
    ppermute x7, waiting for transfers between devices, route(): return lax.ppermute(value, ('mod', 'dp'), pairs)  5.67 us
    pallas_call x1, Pallas kernels, pack(): pl.pallas_call(pack_kernel, out_shape=[near((rows + queries.shape[0], wid...  1.29 us
  transfers between devices with their start and end apart: 13, of which 9 were waited for; matrix products, arithmetic and copies ran while one was open for 0% of the time, Pallas kernels for 1%

profile of v7, /device:TPU:0, one launch (start us, length us, event | category | flops | bytes accessed | tf_op | source)
XLA Modules:
  0.0 40.3 jit_solution(15490256301374787599)
XLA Ops:
  0.0 1.3 %pack.1 = (f32[132,512]{1,0:T(8,128)S(1)}, f32[132,512]{1,0:T(8,128)S(1)}, f32[132,512]{1,0:T(8,128)S(1)}, f32[132,512]{1,0:T(8,128)S(1)}) custom-call(f32[128,4,512]{2,1,0:T(4,128)} %rows_ref.1, f32[4,4,512]{2,1,0:T(4,128)} %queries_ref.1), custom_call_target="tpu_custom_call" | custom-call | flops 1500000000 | tf_op jit(solution)/shard_map/pack/pallas_call | solution.py:96
  1.3 0.6 %collective-permute-start = (f32[132,512]{1,0:T(8,128)S(1)}, f32[132,512]{1,0:T(8,128)S(1)}, u32[]{:S(2)}, u32[]{:S(2)}) collective-permute-start(f32[132,512]{1,0:T(8,128)S(1)} %get-tuple-element.20.two.refs_4_), channel_id=1, source_target_pairs={{0,1},{1,0},{2,3},{3,2},{4,5},{5,4},{6,7},{7,6},{8,9},{9,8},{10,11... | collective-permute-start | bytes 811016 | tf_op jit(solution)/shard_map/ppermute | solution.py:297
  1.9 2.6 %collective-permute-start.3 = (f32[132,512]{1,0:T(8,128)S(1)}, f32[132,512]{1,0:T(8,128)S(1)}, u32[]{:S(2)}, u32[]{:S(2)}) collective-permute-start(f32[132,512]{1,0:T(8,128)S(1)} %get-tuple-element.24), channel_id=1, source_target_pairs={{0,8},{1,7},{2,10},{3,5},{4,12},{5,3},{6,14},{7,1},{8,0},{9,15},{1... | collective-permute-start | bytes 811016 | tf_op jit(solution)/shard_map/ppermute | solution.py:297
  4.5 0.0 copy-start
  4.5 0.1 collective-permute-start.4
  4.6 1.9 %collective-permute-start.1 = (f32[132,512]{1,0:T(8,128)S(1)}, f32[132,512]{1,0:T(8,128)S(1)}, u32[]{:S(2)}, u32[]{:S(2)}) collective-permute-start(f32[132,512]{1,0:T(8,128)S(1)} %get-tuple-element.22), channel_id=1, source_target_pairs={{0,8},{1,5},{2,10},{3,7},{4,12},{5,1},{6,14},{7,3},{8,0},{9,13},{1... | collective-permute-start | bytes 811016 | tf_op jit(solution)/shard_map/ppermute | solution.py:297
  6.5 0.6 %collective-permute-start.2 = (f32[132,512]{1,0:T(8,128)S(1)}, f32[132,512]{1,0:T(8,128)S(1)}, u32[]{:S(2)}, u32[]{:S(2)}) collective-permute-start(f32[132,512]{1,0:T(8,128)S(1)} %get-tuple-element.23), channel_id=1, source_target_pairs={{0,3},{1,0},{2,1},{3,2},{4,7},{5,4},{6,5},{7,6},{8,11},{9,8},{10,9... | collective-permute-start | bytes 811016 | tf_op jit(solution)/shard_map/ppermute | solution.py:297
  7.1 0.0 collective-permute-done.one.refs_3_
  7.1 1.1 %collective-permute-start.5 = (f32[132,512]{1,0:T(8,128)S(1)}, f32[132,512]{1,0:T(8,128)S(1)}, u32[]{:S(2)}, u32[]{:S(2)}) collective-permute-start(f32[132,512]{1,0:T(8,128)S(1)} %get-tuple-element.22), channel_id=1, source_target_pairs={{0,5},{1,0},{2,7},{3,2},{4,1},{5,4},{6,3},{7,6},{8,13},{9,8},{10,1... | collective-permute-start | bytes 811016 | tf_op jit(solution)/shard_map/ppermute | solution.py:297
  8.2 0.9 %collective-permute-done.3.one.refs_10_ = f32[132,512]{1,0:T(8,128)S(1)} collective-permute-done((f32[132,512]{1,0:T(8,128)S(1)}, f32[132,512]{1,0:T(8,128)S(1)}, u32[]{:S(2)}, u32[]{:S(2)}) %collective-permute-start.3) | collective-permute-done | bytes 270368 | tf_op jit(solution)/shard_map/ppermute | solution.py:297
  9.0 3.4 %collective-permute-start.6 = (f32[132,512]{1,0:T(8,128)S(1)}, f32[132,512]{1,0:T(8,128)S(1)}, u32[]{:S(2)}, u32[]{:S(2)}) collective-permute-start(f32[132,512]{1,0:T(8,128)S(1)} %get-tuple-element.24), channel_id=1, source_target_pairs={{0,7},{1,0},{2,5},{3,2},{4,3},{5,4},{6,1},{7,6},{8,15},{9,8},{10,1... | collective-permute-start | bytes 811016 | tf_op jit(solution)/shard_map/ppermute | solution.py:297
  12.5 0.0 copy-done
  12.5 0.6 %gram.3 = (f32[256,256]{1,0:T(8,128)S(1)}, f32[512,256]{1,0:T(8,128)S(1)}, f32[8,128]{1,0:T(8,128)S(1)}) custom-call(f32[4]{0:T(128)S(1)} %copy-done, f32[132,512]{1,0:T(8,128)S(1)} %collective-permute-done.one.refs_3_, f32[132,512]{1,0:T(8,128)S(1)} %get-tuple-element.20.two.refs_4_), custom_call_target="tpu_custom_call" | custom-call | flops 600000000 | tf_op jit(solution)/shard_map/gram/pallas_call | solution.py:151
  13.0 0.0 collective-permute-done.4.two.refs_6_
  13.1 1.9 %collective-permute-done.1.one.refs_8_ = f32[132,512]{1,0:T(8,128)S(1)} collective-permute-done((f32[132,512]{1,0:T(8,128)S(1)}, f32[132,512]{1,0:T(8,128)S(1)}, u32[]{:S(2)}, u32[]{:S(2)}) %collective-permute-start.1) | collective-permute-done | bytes 270368 | tf_op jit(solution)/shard_map/ppermute | solution.py:297
  15.0 0.0 collective-permute-done.2.two.refs_5_
  15.0 0.0 collective-permute-done.5.refs_7_
  15.0 2.9 %collective-permute-done.6.refs_9_ = f32[132,512]{1,0:T(8,128)S(1)} collective-permute-done((f32[132,512]{1,0:T(8,128)S(1)}, f32[132,512]{1,0:T(8,128)S(1)}, u32[]{:S(2)}, u32[]{:S(2)}) %collective-permute-start.6) | collective-permute-done | bytes 270368 | tf_op jit(solution)/shard_map/ppermute | solution.py:297
  17.9 0.6 %collective-permute-start.9 = (f32[32,256]{1,0:T(8,128)S(1)}, f32[32,256]{1,0:T(8,128)S(1)}, u32[]{:S(2)}, u32[]{:S(2)}) collective-permute-start(f32[32,256]{1,0:T(8,128)S(1)} %get-tuple-element.34), channel_id=1, source_target_pairs={{0,2},{1,3},{2,0},{3,1},{4,6},{5,7},{6,4},{7,5},{8,10},{9,11},{10,... | collective-permute-start | bytes 98312 | tf_op jit(solution)/shard_map/ppermute | solution.py:285
  18.5 0.3 collective-permute-start.8
  18.8 2.7 %collective-permute-start.7 = (f32[32,256]{1,0:T(8,128)S(1)}, f32[32,256]{1,0:T(8,128)S(1)}, u32[]{:S(2)}, u32[]{:S(2)}) collective-permute-start(f32[32,256]{1,0:T(8,128)S(1)} %get-tuple-element.32), channel_id=1, source_target_pairs={{0,6},{1,7},{2,4},{3,5},{4,2},{5,3},{6,0},{7,1},{8,14},{9,15},{10,... | collective-permute-start | bytes 98312 | tf_op jit(solution)/shard_map/ppermute | solution.py:285
  21.4 0.4 %collective-permute-done.9 = f32[32,256]{1,0:T(8,128)S(1)} collective-permute-done((f32[32,256]{1,0:T(8,128)S(1)}, f32[32,256]{1,0:T(8,128)S(1)}, u32[]{:S(2)}, u32[]{:S(2)}) %collective-permute-start.9) | collective-permute-done | bytes 32800 | tf_op jit(solution)/shard_map/ppermute | solution.py:285
  21.9 0.6 %collective-permute-done.8 = f32[32,256]{1,0:T(8,128)S(1)} collective-permute-done((f32[32,256]{1,0:T(8,128)S(1)}, f32[32,256]{1,0:T(8,128)S(1)}, u32[]{:S(2)}, u32[]{:S(2)}) %collective-permute-start.8) | collective-permute-done | bytes 32800 | tf_op jit(solution)/shard_map/ppermute | solution.py:285
  22.4 1.2 %collective-permute-done.7 = f32[32,256]{1,0:T(8,128)S(1)} collective-permute-done((f32[32,256]{1,0:T(8,128)S(1)}, f32[32,256]{1,0:T(8,128)S(1)}, u32[]{:S(2)}, u32[]{:S(2)}) %collective-permute-start.7) | collective-permute-done | bytes 32800 | tf_op jit(solution)/shard_map/ppermute | solution.py:285
  23.6 2.8 %collective-permute-start.10 = (f32[16,256]{1,0:T(8,128)S(1)}, f32[16,256]{1,0:T(8,128)S(1)}, u32[]{:S(2)}, u32[]{:S(2)}) collective-permute-start(f32[16,256]{1,0:T(8,128)S(1)} %slice.25), channel_id=1, source_target_pairs={{0,16},{8,24},{16,0},{24,8},{1,17},{9,25},{17,1},{25,9},{2,18},{10... | collective-permute-start | bytes 49160 | tf_op jit(solution)/shard_map/ppermute | solution.py:285
  26.5 1.9 %collective-permute-done.10 = f32[16,256]{1,0:T(8,128)S(1)} collective-permute-done((f32[16,256]{1,0:T(8,128)S(1)}, f32[16,256]{1,0:T(8,128)S(1)}, u32[]{:S(2)}, u32[]{:S(2)}) %collective-permute-start.10) | collective-permute-done | bytes 16416 | tf_op jit(solution)/shard_map/ppermute | solution.py:285
  28.3 1.8 %collective-permute-start.11 = (f32[8,256]{1,0:T(8,128)S(1)}, f32[8,256]{1,0:T(8,128)S(1)}, u32[]{:S(2)}, u32[]{:S(2)}) collective-permute-start(f32[8,256]{1,0:T(8,128)S(1)} %slice.27), channel_id=1, source_target_pairs={{0,8},{8,0},{16,24},{24,16},{1,9},{9,1},{17,25},{25,17},{2,10},{10... | collective-permute-start | bytes 24584 | tf_op jit(solution)/shard_map/ppermute | solution.py:285
  30.1 1.9 %collective-permute-done.11 = f32[8,256]{1,0:T(8,128)S(1)} collective-permute-done((f32[8,256]{1,0:T(8,128)S(1)}, f32[8,256]{1,0:T(8,128)S(1)}, u32[]{:S(2)}, u32[]{:S(2)}) %collective-permute-start.11) | collective-permute-done | bytes 8224 | tf_op jit(solution)/shard_map/ppermute | solution.py:285
  32.0 6.9 %collective-permute-start.12 = (f32[8,128]{1,0:T(8,128)S(1)}, f32[8,128]{1,0:T(8,128)S(1)}, u32[]{:S(2)}, u32[]{:S(2)}) collective-permute-start(f32[8,128]{1,0:T(8,128)S(1)} %slice.29), channel_id=1, source_target_pairs={{0,1},{1,0},{2,3},{3,2},{4,5},{5,4},{6,7},{7,6},{8,9},{9,8},{10,11... | collective-permute-start | bytes 12296 | tf_op jit(solution)/shard_map/ppermute | solution.py:285
  38.9 0.8 %collective-permute-done.12 = f32[8,128]{1,0:T(8,128)S(1)} collective-permute-done((f32[8,128]{1,0:T(8,128)S(1)}, f32[8,128]{1,0:T(8,128)S(1)}, u32[]{:S(2)}, u32[]{:S(2)}) %collective-permute-start.12) | collective-permute-done | bytes 4128 | tf_op jit(solution)/shard_map/ppermute | solution.py:285
  39.7 0.6 %fusion = f32[128,8]{0,1:T(8,128)} fusion(f32[8,128]{1,0:T(8,128)S(1)} %collective-permute-done.12, f32[8,256]{1,0:T(8,128)S(1)} %slice_add_fusion.1, pred[]{:T(512)S(6)} %eq.5), kind=kLoop, calls=%fused_computation.4 | loop fusion | flops 1024 | bytes 12289 | tf_op jit(solution)/shard_map/transpose | solution.py:358
  (9 shorter events, 0.1 us)
Async XLA Ops:
  1.3 5.8 %collective-permute-start = (f32[132,512]{1,0:T(8,128)S(1)}, f32[132,512]{1,0:T(8,128)S(1)}, u32[]{:S(2)}, u32[]{:S(2)}) collective-permute-start(f32[132,512]{1,0:T(8,128)S(1)} %get-tuple-element.20.two.refs_4_), channel_id=1, source_target_pairs={{0,1},{1,0},{2,3},{3,2},{4,5},{5,4},{6,7},{7,6},{8,9},{9,8},{10,11... | collective-permute-start | bytes 811016 | tf_op jit(solution)/shard_map/ppermute | solution.py:297
  1.9 7.2 %collective-permute-start.3 = (f32[132,512]{1,0:T(8,128)S(1)}, f32[132,512]{1,0:T(8,128)S(1)}, u32[]{:S(2)}, u32[]{:S(2)}) collective-permute-start(f32[132,512]{1,0:T(8,128)S(1)} %get-tuple-element.24), channel_id=1, source_target_pairs={{0,8},{1,7},{2,10},{3,5},{4,12},{5,3},{6,14},{7,1},{8,0},{9,15},{1... | collective-permute-start | bytes 811016 | tf_op jit(solution)/shard_map/ppermute | solution.py:297
  4.5 8.0 %copy-start = (f32[4]{0:T(128)S(1)}, f32[4]{0:T(128)}, u32[]{:S(2)}) copy-start(f32[4]{0:T(128)} %damping_ref.1) | copy-start | bytes 52
  4.5 8.5 %collective-permute-start.4 = (f32[132,512]{1,0:T(8,128)S(1)}, f32[132,512]{1,0:T(8,128)S(1)}, u32[]{:S(2)}, u32[]{:S(2)}) collective-permute-start(f32[132,512]{1,0:T(8,128)S(1)} %get-tuple-element.23), channel_id=1, source_target_pairs={{0,8},{1,3},{2,10},{3,1},{4,12},{5,7},{6,14},{7,5},{8,0},{9,11},{1... | collective-permute-start | bytes 811016 | tf_op jit(solution)/shard_map/ppermute | solution.py:297
  4.6 10.4 %collective-permute-start.1 = (f32[132,512]{1,0:T(8,128)S(1)}, f32[132,512]{1,0:T(8,128)S(1)}, u32[]{:S(2)}, u32[]{:S(2)}) collective-permute-start(f32[132,512]{1,0:T(8,128)S(1)} %get-tuple-element.22), channel_id=1, source_target_pairs={{0,8},{1,5},{2,10},{3,7},{4,12},{5,1},{6,14},{7,3},{8,0},{9,13},{1... | collective-permute-start | bytes 811016 | tf_op jit(solution)/shard_map/ppermute | solution.py:297
  6.5 8.5 %collective-permute-start.2 = (f32[132,512]{1,0:T(8,128)S(1)}, f32[132,512]{1,0:T(8,128)S(1)}, u32[]{:S(2)}, u32[]{:S(2)}) collective-permute-start(f32[132,512]{1,0:T(8,128)S(1)} %get-tuple-element.23), channel_id=1, source_target_pairs={{0,3},{1,0},{2,1},{3,2},{4,7},{5,4},{6,5},{7,6},{8,11},{9,8},{10,9... | collective-permute-start | bytes 811016 | tf_op jit(solution)/shard_map/ppermute | solution.py:297
  7.1 7.9 %collective-permute-start.5 = (f32[132,512]{1,0:T(8,128)S(1)}, f32[132,512]{1,0:T(8,128)S(1)}, u32[]{:S(2)}, u32[]{:S(2)}) collective-permute-start(f32[132,512]{1,0:T(8,128)S(1)} %get-tuple-element.22), channel_id=1, source_target_pairs={{0,5},{1,0},{2,7},{3,2},{4,1},{5,4},{6,3},{7,6},{8,13},{9,8},{10,1... | collective-permute-start | bytes 811016 | tf_op jit(solution)/shard_map/ppermute | solution.py:297
  9.0 8.9 %collective-permute-start.6 = (f32[132,512]{1,0:T(8,128)S(1)}, f32[132,512]{1,0:T(8,128)S(1)}, u32[]{:S(2)}, u32[]{:S(2)}) collective-permute-start(f32[132,512]{1,0:T(8,128)S(1)} %get-tuple-element.24), channel_id=1, source_target_pairs={{0,7},{1,0},{2,5},{3,2},{4,3},{5,4},{6,1},{7,6},{8,15},{9,8},{10,1... | collective-permute-start | bytes 811016 | tf_op jit(solution)/shard_map/ppermute | solution.py:297
  17.9 4.0 %collective-permute-start.9 = (f32[32,256]{1,0:T(8,128)S(1)}, f32[32,256]{1,0:T(8,128)S(1)}, u32[]{:S(2)}, u32[]{:S(2)}) collective-permute-start(f32[32,256]{1,0:T(8,128)S(1)} %get-tuple-element.34), channel_id=1, source_target_pairs={{0,2},{1,3},{2,0},{3,1},{4,6},{5,7},{6,4},{7,5},{8,10},{9,11},{10,... | collective-permute-start | bytes 98312 | tf_op jit(solution)/shard_map/ppermute | solution.py:285
  18.5 3.9 %collective-permute-start.8 = (f32[32,256]{1,0:T(8,128)S(1)}, f32[32,256]{1,0:T(8,128)S(1)}, u32[]{:S(2)}, u32[]{:S(2)}) collective-permute-start(f32[32,256]{1,0:T(8,128)S(1)} %get-tuple-element.33), channel_id=1, source_target_pairs={{0,4},{1,5},{2,6},{3,7},{4,0},{5,1},{6,2},{7,3},{8,12},{9,13},{10,... | collective-permute-start | bytes 98312 | tf_op jit(solution)/shard_map/ppermute | solution.py:285
  18.8 4.8 %collective-permute-start.7 = (f32[32,256]{1,0:T(8,128)S(1)}, f32[32,256]{1,0:T(8,128)S(1)}, u32[]{:S(2)}, u32[]{:S(2)}) collective-permute-start(f32[32,256]{1,0:T(8,128)S(1)} %get-tuple-element.32), channel_id=1, source_target_pairs={{0,6},{1,7},{2,4},{3,5},{4,2},{5,3},{6,0},{7,1},{8,14},{9,15},{10,... | collective-permute-start | bytes 98312 | tf_op jit(solution)/shard_map/ppermute | solution.py:285
  23.6 4.7 %collective-permute-start.10 = (f32[16,256]{1,0:T(8,128)S(1)}, f32[16,256]{1,0:T(8,128)S(1)}, u32[]{:S(2)}, u32[]{:S(2)}) collective-permute-start(f32[16,256]{1,0:T(8,128)S(1)} %slice.25), channel_id=1, source_target_pairs={{0,16},{8,24},{16,0},{24,8},{1,17},{9,25},{17,1},{25,9},{2,18},{10... | collective-permute-start | bytes 49160 | tf_op jit(solution)/shard_map/ppermute | solution.py:285
  28.3 3.7 %collective-permute-start.11 = (f32[8,256]{1,0:T(8,128)S(1)}, f32[8,256]{1,0:T(8,128)S(1)}, u32[]{:S(2)}, u32[]{:S(2)}) collective-permute-start(f32[8,256]{1,0:T(8,128)S(1)} %slice.27), channel_id=1, source_target_pairs={{0,8},{8,0},{16,24},{24,16},{1,9},{9,1},{17,25},{25,17},{2,10},{10... | collective-permute-start | bytes 24584 | tf_op jit(solution)/shard_map/ppermute | solution.py:285
  32.0 7.7 %collective-permute-start.12 = (f32[8,128]{1,0:T(8,128)S(1)}, f32[8,128]{1,0:T(8,128)S(1)}, u32[]{:S(2)}, u32[]{:S(2)}) collective-permute-start(f32[8,128]{1,0:T(8,128)S(1)} %slice.29), channel_id=1, source_target_pairs={{0,1},{1,0},{2,3},{3,2},{4,5},{5,4},{6,7},{7,6},{8,9},{9,8},{10,11... | collective-permute-start | bytes 12296 | tf_op jit(solution)/shard_map/ppermute | solution.py:285

commit v8 on v6

--- a/solution.py
+++ b/solution.py
@@ -178,7 +178,7 @@
     damp_ref, left_ref, right_ref = refs[:3]
     blocks = [refs[3 + CORES * offset : 3 + CORES * (offset + 1)] for offset in range(chips)]
     scores = refs[3 + CORES * chips : 3 + (CORES + 1) * chips]
-    left, right, stack, state, high, low, asked = refs[3 + (CORES + 1) * chips :]
+    first_gram, right_gram, stack, state, high, low, asked = refs[3 + (CORES + 1) * chips :]
     half = left_ref.shape[0]
     width = 2 * half
     chip = lax.axis_index("dp") // CORES
@@ -193,15 +193,15 @@
             [block[rows : rows + per_device] for block in blocks[offset]], 0
         )
 
-    left[...] = left_ref[...]
-    right[...] = right_ref[...]
-    add_gram(rows, [block[1 - SOLVER] for block in blocks[-2:]], left, right, stack)
+    first_gram[...] = left_ref[...]
+    right_gram[...] = right_ref[...]
+    add_gram(rows, [block[1 - SOLVER] for block in blocks[-2:]], first_gram, right_gram, stack)
 
     diagonal = lax.broadcasted_iota(jnp.int32, (half, half), 0) == lax.broadcasted_iota(
         jnp.int32, (half, half), 1
     )
     eye = diagonal.astype(jnp.float32)
-    first, cross, last = left[...], right[0:half], right[half:]
+    first, cross, last = first_gram[...], right_gram[0:half], right_gram[half:]
     trace = jnp.sum((first + last) * eye, keepdims=True).reshape(1, 1)
     shift = (damp_ref[0:1, 0:1] * trace * (1.0 / width)) * eye
     first = first + shift
@@ -223,22 +223,33 @@
 
     for _ in range(SQUARINGS):
         high[...], low[...] = halves(state[...])
-
-        def part(start, stop, column):
-            columns = slice(column, column + half)
-            return product_3(
-                high[start:stop],
-                low[start:stop],
-                high[0:width, columns],
-                low[0:width, columns],
-            )
-
-        state[0:half, 0:half] = 2.0 * state[0:half, 0:half] - part(0, half, 0)
-        new = 2.0 * state[0:width, half:] - part(0, width, half)
-        state[0:width, half:] = new
-        state[half:width, 0:half] = new[0:half].T
-        state[width:, 0:half] = 2.0 * state[width:, 0:half] - part(width, width + total_queries, 0)
-        state[width:, half:] = 2.0 * state[width:, half:] - part(width, width + total_queries, half)
+        high_left, high_right = high[0:width, 0:half], high[0:width, half:]
+        low_left, low_right = low[0:width, 0:half], low[0:width, half:]
+        mixed_left = product(high[0:width], low_left)
+        mixed_right = product(high[0:width], low_right)
+        right = product(high[0:width], high_right)
+        left = product(high[0:half], high_left)
+        new_first = 2.0 * state[0:half, 0:half] - (
+            left + (mixed_left[0:half] + mixed_left[0:half].T)
+        )
+        new_cross = 2.0 * state[0:half, half:] - (
+            right[0:half] + (mixed_right[0:half] + mixed_left[half:].T)
+        )
+        new_last = 2.0 * state[half:width, half:] - (
+            right[half:] + (mixed_right[half:] + mixed_right[half:].T)
+        )
+        state[0:half, half:] = new_cross
+        state[half:width, half:] = new_last
+        state[half:width, 0:half] = state[0:half, half:].T
+        asked_left = 2.0 * state[width:, 0:half] - product_3(
+            high[width:], low[width:], high_left, low_left
+        )
+        asked_right = 2.0 * state[width:, half:] - product_3(
+            high[width:], low[width:], high_right, low_right
+        )
+        state[0:half, 0:half] = new_first
+        state[width:, 0:half] = asked_left
+        state[width:, half:] = asked_right
 
     high[...], low[...] = halves(state[...])
     asked_last = state[width:]

time: 41.3 us -> 40.5 us (0.981)
  starting transfers between devices: 24.6 us -> 23.8 us
    ppermute x6, starting transfers between devices: 14.7 us -> 13.9 us  [swap(): lax.ppermute(value, axis, [(i, i ^ offset) for i in range(lax.axis_size(a...]
where the time goes in v8:
time: 40.5 us; the launch traced here: 40.4 us
  starting transfers between devices  23.8 us (59%)
  waiting for transfers between devices  14 us (35%)
  Pallas kernels  1.88 us (5%)
  other arithmetic  0.61 us (2%)
    ppermute x6, starting transfers between devices, swap(): lax.ppermute(value, axis, [(i, i ^ offset) for i in range(lax.axis_size(a...  13.9 us
    ppermute x7, starting transfers between devices, route(): return lax.ppermute(value, ('mod', 'dp'), pairs)  9.91 us
    ppermute x6, waiting for transfers between devices, swap(): lax.ppermute(value, axis, [(i, i ^ offset) for i in range(lax.axis_size(a...  7.08 us
    ppermute x7, waiting for transfers between devices, route(): return lax.ppermute(value, ('mod', 'dp'), pairs)  6.89 us
    pallas_call x1, Pallas kernels, pack(): pl.pallas_call(pack_kernel, out_shape=[near((rows + queries.shape[0], wid...  1.29 us
  transfers between devices with their start and end apart: 13, of which 9 were waited for; matrix products, arithmetic and copies ran while one was open for 0% of the time, Pallas kernels for 1%

profile of v8, /device:TPU:0, one launch (start us, length us, event | category | flops | bytes accessed | tf_op | source)
XLA Modules:
  0.0 40.4 jit_solution(7856512378253349847)
XLA Ops:
  0.0 1.3 %pack.1 = (f32[132,512]{1,0:T(8,128)S(1)}, f32[132,512]{1,0:T(8,128)S(1)}, f32[132,512]{1,0:T(8,128)S(1)}, f32[132,512]{1,0:T(8,128)S(1)}) custom-call(f32[128,4,512]{2,1,0:T(4,128)} %rows_ref.1, f32[4,4,512]{2,1,0:T(4,128)} %queries_ref.1), custom_call_target="tpu_custom_call" | custom-call | flops 1500000000 | tf_op jit(solution)/shard_map/pack/pallas_call | solution.py:96
  1.3 0.6 %collective-permute-start = (f32[132,512]{1,0:T(8,128)S(1)}, f32[132,512]{1,0:T(8,128)S(1)}, u32[]{:S(2)}, u32[]{:S(2)}) collective-permute-start(f32[132,512]{1,0:T(8,128)S(1)} %get-tuple-element.20.two.refs_4_), channel_id=1, source_target_pairs={{0,1},{1,0},{2,3},{3,2},{4,5},{5,4},{6,7},{7,6},{8,9},{9,8},{10,11... | collective-permute-start | bytes 811016 | tf_op jit(solution)/shard_map/ppermute | solution.py:308
  1.9 2.6 %collective-permute-start.3 = (f32[132,512]{1,0:T(8,128)S(1)}, f32[132,512]{1,0:T(8,128)S(1)}, u32[]{:S(2)}, u32[]{:S(2)}) collective-permute-start(f32[132,512]{1,0:T(8,128)S(1)} %get-tuple-element.24), channel_id=1, source_target_pairs={{0,3},{1,0},{2,1},{3,2},{4,7},{5,4},{6,5},{7,6},{8,11},{9,8},{10,9... | collective-permute-start | bytes 811016 | tf_op jit(solution)/shard_map/ppermute | solution.py:308
  4.4 1.6 %collective-permute-start.4 = (f32[132,512]{1,0:T(8,128)S(1)}, f32[132,512]{1,0:T(8,128)S(1)}, u32[]{:S(2)}, u32[]{:S(2)}) collective-permute-start(f32[132,512]{1,0:T(8,128)S(1)} %get-tuple-element.24), channel_id=1, source_target_pairs={{0,8},{1,3},{2,10},{3,1},{4,12},{5,7},{6,14},{7,5},{8,0},{9,11},{1... | collective-permute-start | bytes 811016 | tf_op jit(solution)/shard_map/ppermute | solution.py:308
  6.0 0.0 copy-start
  6.0 0.4 %collective-permute-start.1 = (f32[132,512]{1,0:T(8,128)S(1)}, f32[132,512]{1,0:T(8,128)S(1)}, u32[]{:S(2)}, u32[]{:S(2)}) collective-permute-start(f32[132,512]{1,0:T(8,128)S(1)} %get-tuple-element.22), channel_id=1, source_target_pairs={{0,8},{1,5},{2,10},{3,7},{4,12},{5,1},{6,14},{7,3},{8,0},{9,13},{1... | collective-permute-start | bytes 811016 | tf_op jit(solution)/shard_map/ppermute | solution.py:308
  6.5 1.6 %collective-permute-start.2 = (f32[132,512]{1,0:T(8,128)S(1)}, f32[132,512]{1,0:T(8,128)S(1)}, u32[]{:S(2)}, u32[]{:S(2)}) collective-permute-start(f32[132,512]{1,0:T(8,128)S(1)} %get-tuple-element.23), channel_id=1, source_target_pairs={{0,8},{1,7},{2,10},{3,5},{4,12},{5,3},{6,14},{7,1},{8,0},{9,15},{1... | collective-permute-start | bytes 811016 | tf_op jit(solution)/shard_map/ppermute | solution.py:308
  8.1 0.0 collective-permute-done.one.refs_3_
  8.1 0.0 collective-permute-start.5
  8.1 3.4 %collective-permute-done.3.one.refs_5_ = f32[132,512]{1,0:T(8,128)S(1)} collective-permute-done((f32[132,512]{1,0:T(8,128)S(1)}, f32[132,512]{1,0:T(8,128)S(1)}, u32[]{:S(2)}, u32[]{:S(2)}) %collective-permute-start.3) | collective-permute-done | bytes 270368 | tf_op jit(solution)/shard_map/ppermute | solution.py:308
  11.5 3.2 %collective-permute-start.6 = (f32[132,512]{1,0:T(8,128)S(1)}, f32[132,512]{1,0:T(8,128)S(1)}, u32[]{:S(2)}, u32[]{:S(2)}) collective-permute-start(f32[132,512]{1,0:T(8,128)S(1)} %get-tuple-element.23), channel_id=1, source_target_pairs={{0,7},{1,0},{2,5},{3,2},{4,3},{5,4},{6,1},{7,6},{8,15},{9,8},{10,1... | collective-permute-start | bytes 811016 | tf_op jit(solution)/shard_map/ppermute | solution.py:308
  14.7 0.0 copy-done
  14.7 0.6 %gram.3 = (f32[256,256]{1,0:T(8,128)S(1)}, f32[512,256]{1,0:T(8,128)S(1)}, f32[8,128]{1,0:T(8,128)S(1)}) custom-call(f32[4]{0:T(128)S(1)} %copy-done, f32[132,512]{1,0:T(8,128)S(1)} %collective-permute-done.one.refs_3_, f32[132,512]{1,0:T(8,128)S(1)} %get-tuple-element.20.two.refs_4_), custom_call_target="tpu_custom_call" | custom-call | flops 600000000 | tf_op jit(solution)/shard_map/gram/pallas_call | solution.py:151
  15.2 0.0 collective-permute-done.4.two.refs_6_
  15.3 0.0 collective-permute-done.1.one.refs_8_
  15.3 1.7 %collective-permute-done.2.two.refs_10_ = f32[132,512]{1,0:T(8,128)S(1)} collective-permute-done((f32[132,512]{1,0:T(8,128)S(1)}, f32[132,512]{1,0:T(8,128)S(1)}, u32[]{:S(2)}, u32[]{:S(2)}) %collective-permute-start.2) | collective-permute-done | bytes 270368 | tf_op jit(solution)/shard_map/ppermute | solution.py:308
  17.0 0.0 collective-permute-done.5.refs_7_
  17.0 1.7 %collective-permute-done.6.refs_9_ = f32[132,512]{1,0:T(8,128)S(1)} collective-permute-done((f32[132,512]{1,0:T(8,128)S(1)}, f32[132,512]{1,0:T(8,128)S(1)}, u32[]{:S(2)}, u32[]{:S(2)}) %collective-permute-start.6) | collective-permute-done | bytes 270368 | tf_op jit(solution)/shard_map/ppermute | solution.py:308
  18.7 0.6 %collective-permute-start.9 = (f32[32,256]{1,0:T(8,128)S(1)}, f32[32,256]{1,0:T(8,128)S(1)}, u32[]{:S(2)}, u32[]{:S(2)}) collective-permute-start(f32[32,256]{1,0:T(8,128)S(1)} %get-tuple-element.34), channel_id=1, source_target_pairs={{0,2},{1,3},{2,0},{3,1},{4,6},{5,7},{6,4},{7,5},{8,10},{9,11},{10,... | collective-permute-start | bytes 98312 | tf_op jit(solution)/shard_map/ppermute | solution.py:296
  19.3 0.4 %collective-permute-start.8 = (f32[32,256]{1,0:T(8,128)S(1)}, f32[32,256]{1,0:T(8,128)S(1)}, u32[]{:S(2)}, u32[]{:S(2)}) collective-permute-start(f32[32,256]{1,0:T(8,128)S(1)} %get-tuple-element.33), channel_id=1, source_target_pairs={{0,4},{1,5},{2,6},{3,7},{4,0},{5,1},{6,2},{7,3},{8,12},{9,13},{10,... | collective-permute-start | bytes 98312 | tf_op jit(solution)/shard_map/ppermute | solution.py:296
  19.8 2.5 %collective-permute-start.7 = (f32[32,256]{1,0:T(8,128)S(1)}, f32[32,256]{1,0:T(8,128)S(1)}, u32[]{:S(2)}, u32[]{:S(2)}) collective-permute-start(f32[32,256]{1,0:T(8,128)S(1)} %get-tuple-element.32), channel_id=1, source_target_pairs={{0,6},{1,7},{2,4},{3,5},{4,2},{5,3},{6,0},{7,1},{8,14},{9,15},{10,... | collective-permute-start | bytes 98312 | tf_op jit(solution)/shard_map/ppermute | solution.py:296
  22.3 0.4 %collective-permute-done.9 = f32[32,256]{1,0:T(8,128)S(1)} collective-permute-done((f32[32,256]{1,0:T(8,128)S(1)}, f32[32,256]{1,0:T(8,128)S(1)}, u32[]{:S(2)}, u32[]{:S(2)}) %collective-permute-start.9) | collective-permute-done | bytes 32800 | tf_op jit(solution)/shard_map/ppermute | solution.py:296
  22.7 0.5 %collective-permute-done.8 = f32[32,256]{1,0:T(8,128)S(1)} collective-permute-done((f32[32,256]{1,0:T(8,128)S(1)}, f32[32,256]{1,0:T(8,128)S(1)}, u32[]{:S(2)}, u32[]{:S(2)}) %collective-permute-start.8) | collective-permute-done | bytes 32800 | tf_op jit(solution)/shard_map/ppermute | solution.py:296
  23.3 1.3 %collective-permute-done.7 = f32[32,256]{1,0:T(8,128)S(1)} collective-permute-done((f32[32,256]{1,0:T(8,128)S(1)}, f32[32,256]{1,0:T(8,128)S(1)}, u32[]{:S(2)}, u32[]{:S(2)}) %collective-permute-start.7) | collective-permute-done | bytes 32800 | tf_op jit(solution)/shard_map/ppermute | solution.py:296
  24.6 2.8 %collective-permute-start.10 = (f32[16,256]{1,0:T(8,128)S(1)}, f32[16,256]{1,0:T(8,128)S(1)}, u32[]{:S(2)}, u32[]{:S(2)}) collective-permute-start(f32[16,256]{1,0:T(8,128)S(1)} %slice.25), channel_id=1, source_target_pairs={{0,16},{8,24},{16,0},{24,8},{1,17},{9,25},{17,1},{25,9},{2,18},{10... | collective-permute-start | bytes 49160 | tf_op jit(solution)/shard_map/ppermute | solution.py:296
  27.4 1.9 %collective-permute-done.10 = f32[16,256]{1,0:T(8,128)S(1)} collective-permute-done((f32[16,256]{1,0:T(8,128)S(1)}, f32[16,256]{1,0:T(8,128)S(1)}, u32[]{:S(2)}, u32[]{:S(2)}) %collective-permute-start.10) | collective-permute-done | bytes 16416 | tf_op jit(solution)/shard_map/ppermute | solution.py:296
  29.3 1.6 %collective-permute-start.11 = (f32[8,256]{1,0:T(8,128)S(1)}, f32[8,256]{1,0:T(8,128)S(1)}, u32[]{:S(2)}, u32[]{:S(2)}) collective-permute-start(f32[8,256]{1,0:T(8,128)S(1)} %slice.27), channel_id=1, source_target_pairs={{0,8},{8,0},{16,24},{24,16},{1,9},{9,1},{17,25},{25,17},{2,10},{10... | collective-permute-start | bytes 24584 | tf_op jit(solution)/shard_map/ppermute | solution.py:296
  31.0 2.0 %collective-permute-done.11 = f32[8,256]{1,0:T(8,128)S(1)} collective-permute-done((f32[8,256]{1,0:T(8,128)S(1)}, f32[8,256]{1,0:T(8,128)S(1)}, u32[]{:S(2)}, u32[]{:S(2)}) %collective-permute-start.11) | collective-permute-done | bytes 8224 | tf_op jit(solution)/shard_map/ppermute | solution.py:296
  33.0 5.9 %collective-permute-start.12 = (f32[8,128]{1,0:T(8,128)S(1)}, f32[8,128]{1,0:T(8,128)S(1)}, u32[]{:S(2)}, u32[]{:S(2)}) collective-permute-start(f32[8,128]{1,0:T(8,128)S(1)} %slice.29), channel_id=1, source_target_pairs={{0,1},{1,0},{2,3},{3,2},{4,5},{5,4},{6,7},{7,6},{8,9},{9,8},{10,11... | collective-permute-start | bytes 12296 | tf_op jit(solution)/shard_map/ppermute | solution.py:296
  38.9 0.8 %collective-permute-done.12 = f32[8,128]{1,0:T(8,128)S(1)} collective-permute-done((f32[8,128]{1,0:T(8,128)S(1)}, f32[8,128]{1,0:T(8,128)S(1)}, u32[]{:S(2)}, u32[]{:S(2)}) %collective-permute-start.12) | collective-permute-done | bytes 4128 | tf_op jit(solution)/shard_map/ppermute | solution.py:296
  39.8 0.6 %fusion = f32[128,8]{0,1:T(8,128)} fusion(f32[8,128]{1,0:T(8,128)S(1)} %collective-permute-done.12, f32[8,256]{1,0:T(8,128)S(1)} %slice_add_fusion.1, pred[]{:T(512)S(6)} %eq.5), kind=kLoop, calls=%fused_computation.4 | loop fusion | flops 1024 | bytes 12289 | tf_op jit(solution)/shard_map/transpose | solution.py:372
  (9 shorter events, 0.1 us)
Async XLA Ops:
  1.3 6.8 %collective-permute-start = (f32[132,512]{1,0:T(8,128)S(1)}, f32[132,512]{1,0:T(8,128)S(1)}, u32[]{:S(2)}, u32[]{:S(2)}) collective-permute-start(f32[132,512]{1,0:T(8,128)S(1)} %get-tuple-element.20.two.refs_4_), channel_id=1, source_target_pairs={{0,1},{1,0},{2,3},{3,2},{4,5},{5,4},{6,7},{7,6},{8,9},{9,8},{10,11... | collective-permute-start | bytes 811016 | tf_op jit(solution)/shard_map/ppermute | solution.py:308
  1.9 9.6 %collective-permute-start.3 = (f32[132,512]{1,0:T(8,128)S(1)}, f32[132,512]{1,0:T(8,128)S(1)}, u32[]{:S(2)}, u32[]{:S(2)}) collective-permute-start(f32[132,512]{1,0:T(8,128)S(1)} %get-tuple-element.24), channel_id=1, source_target_pairs={{0,3},{1,0},{2,1},{3,2},{4,7},{5,4},{6,5},{7,6},{8,11},{9,8},{10,9... | collective-permute-start | bytes 811016 | tf_op jit(solution)/shard_map/ppermute | solution.py:308
  4.4 10.8 %collective-permute-start.4 = (f32[132,512]{1,0:T(8,128)S(1)}, f32[132,512]{1,0:T(8,128)S(1)}, u32[]{:S(2)}, u32[]{:S(2)}) collective-permute-start(f32[132,512]{1,0:T(8,128)S(1)} %get-tuple-element.24), channel_id=1, source_target_pairs={{0,8},{1,3},{2,10},{3,1},{4,12},{5,7},{6,14},{7,5},{8,0},{9,11},{1... | collective-permute-start | bytes 811016 | tf_op jit(solution)/shard_map/ppermute | solution.py:308
  6.0 8.6 %copy-start = (f32[4]{0:T(128)S(1)}, f32[4]{0:T(128)}, u32[]{:S(2)}) copy-start(f32[4]{0:T(128)} %damping_ref.1) | copy-start | bytes 52
  6.0 9.2 %collective-permute-start.1 = (f32[132,512]{1,0:T(8,128)S(1)}, f32[132,512]{1,0:T(8,128)S(1)}, u32[]{:S(2)}, u32[]{:S(2)}) collective-permute-start(f32[132,512]{1,0:T(8,128)S(1)} %get-tuple-element.22), channel_id=1, source_target_pairs={{0,8},{1,5},{2,10},{3,7},{4,12},{5,1},{6,14},{7,3},{8,0},{9,13},{1... | collective-permute-start | bytes 811016 | tf_op jit(solution)/shard_map/ppermute | solution.py:308
  6.5 10.5 %collective-permute-start.2 = (f32[132,512]{1,0:T(8,128)S(1)}, f32[132,512]{1,0:T(8,128)S(1)}, u32[]{:S(2)}, u32[]{:S(2)}) collective-permute-start(f32[132,512]{1,0:T(8,128)S(1)} %get-tuple-element.23), channel_id=1, source_target_pairs={{0,8},{1,7},{2,10},{3,5},{4,12},{5,3},{6,14},{7,1},{8,0},{9,15},{1... | collective-permute-start | bytes 811016 | tf_op jit(solution)/shard_map/ppermute | solution.py:308
  8.1 8.9 %collective-permute-start.5 = (f32[132,512]{1,0:T(8,128)S(1)}, f32[132,512]{1,0:T(8,128)S(1)}, u32[]{:S(2)}, u32[]{:S(2)}) collective-permute-start(f32[132,512]{1,0:T(8,128)S(1)} %get-tuple-element.22), channel_id=1, source_target_pairs={{0,5},{1,0},{2,7},{3,2},{4,1},{5,4},{6,3},{7,6},{8,13},{9,8},{10,1... | collective-permute-start | bytes 811016 | tf_op jit(solution)/shard_map/ppermute | solution.py:308
  11.5 7.2 %collective-permute-start.6 = (f32[132,512]{1,0:T(8,128)S(1)}, f32[132,512]{1,0:T(8,128)S(1)}, u32[]{:S(2)}, u32[]{:S(2)}) collective-permute-start(f32[132,512]{1,0:T(8,128)S(1)} %get-tuple-element.23), channel_id=1, source_target_pairs={{0,7},{1,0},{2,5},{3,2},{4,3},{5,4},{6,1},{7,6},{8,15},{9,8},{10,1... | collective-permute-start | bytes 811016 | tf_op jit(solution)/shard_map/ppermute | solution.py:308
  18.7 4.0 %collective-permute-start.9 = (f32[32,256]{1,0:T(8,128)S(1)}, f32[32,256]{1,0:T(8,128)S(1)}, u32[]{:S(2)}, u32[]{:S(2)}) collective-permute-start(f32[32,256]{1,0:T(8,128)S(1)} %get-tuple-element.34), channel_id=1, source_target_pairs={{0,2},{1,3},{2,0},{3,1},{4,6},{5,7},{6,4},{7,5},{8,10},{9,11},{10,... | collective-permute-start | bytes 98312 | tf_op jit(solution)/shard_map/ppermute | solution.py:296
  19.3 3.9 %collective-permute-start.8 = (f32[32,256]{1,0:T(8,128)S(1)}, f32[32,256]{1,0:T(8,128)S(1)}, u32[]{:S(2)}, u32[]{:S(2)}) collective-permute-start(f32[32,256]{1,0:T(8,128)S(1)} %get-tuple-element.33), channel_id=1, source_target_pairs={{0,4},{1,5},{2,6},{3,7},{4,0},{5,1},{6,2},{7,3},{8,12},{9,13},{10,... | collective-permute-start | bytes 98312 | tf_op jit(solution)/shard_map/ppermute | solution.py:296
  19.8 4.8 %collective-permute-start.7 = (f32[32,256]{1,0:T(8,128)S(1)}, f32[32,256]{1,0:T(8,128)S(1)}, u32[]{:S(2)}, u32[]{:S(2)}) collective-permute-start(f32[32,256]{1,0:T(8,128)S(1)} %get-tuple-element.32), channel_id=1, source_target_pairs={{0,6},{1,7},{2,4},{3,5},{4,2},{5,3},{6,0},{7,1},{8,14},{9,15},{10,... | collective-permute-start | bytes 98312 | tf_op jit(solution)/shard_map/ppermute | solution.py:296
  24.6 4.7 %collective-permute-start.10 = (f32[16,256]{1,0:T(8,128)S(1)}, f32[16,256]{1,0:T(8,128)S(1)}, u32[]{:S(2)}, u32[]{:S(2)}) collective-permute-start(f32[16,256]{1,0:T(8,128)S(1)} %slice.25), channel_id=1, source_target_pairs={{0,16},{8,24},{16,0},{24,8},{1,17},{9,25},{17,1},{25,9},{2,18},{10... | collective-permute-start | bytes 49160 | tf_op jit(solution)/shard_map/ppermute | solution.py:296
  29.3 3.7 %collective-permute-start.11 = (f32[8,256]{1,0:T(8,128)S(1)}, f32[8,256]{1,0:T(8,128)S(1)}, u32[]{:S(2)}, u32[]{:S(2)}) collective-permute-start(f32[8,256]{1,0:T(8,128)S(1)} %slice.27), channel_id=1, source_target_pairs={{0,8},{8,0},{16,24},{24,16},{1,9},{9,1},{17,25},{25,17},{2,10},{10... | collective-permute-start | bytes 24584 | tf_op jit(solution)/shard_map/ppermute | solution.py:296
  33.0 6.8 %collective-permute-start.12 = (f32[8,128]{1,0:T(8,128)S(1)}, f32[8,128]{1,0:T(8,128)S(1)}, u32[]{:S(2)}, u32[]{:S(2)}) collective-permute-start(f32[8,128]{1,0:T(8,128)S(1)} %slice.29), channel_id=1, source_target_pairs={{0,1},{1,0},{2,3},{3,2},{4,5},{5,4},{6,7},{7,6},{8,9},{9,8},{10,11... | collective-permute-start | bytes 12296 | tf_op jit(solution)/shard_map/ppermute | solution.py:296

commit v9 on v8

--- a/solution.py
+++ b/solution.py
@@ -55,11 +55,15 @@
     )
 
 
+def stacked_product(high, both, right_high, right_low, dims=(((1,), (0,)), ((), ()))):
+    count = high.shape[0]
+    sums = product(both, right_high, dims)
+    return sums[:count] + sums[count:] + product(high, right_low, dims)
+
+
 def narrow_product(left, right_high, right_low, dims=(((1,), (0,)), ((), ()))):
     high, low = halves(left)
-    count = left.shape[0]
-    both = product(jnp.concatenate([high, low], 0), right_high, dims)
-    return both[:count] + both[count:] + product(high, right_low, dims)
+    return stacked_product(high, jnp.concatenate([high, low], 0), right_high, right_low, dims)
 
 
 def pack_kernel(rows_ref, queries_ref, *refs):
@@ -225,6 +229,7 @@
         high[...], low[...] = halves(state[...])
         high_left, high_right = high[0:width, 0:half], high[0:width, half:]
         low_left, low_right = low[0:width, 0:half], low[0:width, half:]
+        both = jnp.concatenate([high[width:], low[width:]], 0)
         mixed_left = product(high[0:width], low_left)
         mixed_right = product(high[0:width], low_right)
         right = product(high[0:width], high_right)
@@ -241,11 +246,11 @@
         state[0:half, half:] = new_cross
         state[half:width, half:] = new_last
         state[half:width, 0:half] = state[0:half, half:].T
-        asked_left = 2.0 * state[width:, 0:half] - product_3(
-            high[width:], low[width:], high_left, low_left
-        )
-        asked_right = 2.0 * state[width:, half:] - product_3(
-            high[width:], low[width:], high_right, low_right
+        asked_left = 2.0 * state[width:, 0:half] - stacked_product(
+            high[width:], both, high_left, low_left
+        )
+        asked_right = 2.0 * state[width:, half:] - stacked_product(
+            high[width:], both, high_right, low_right
         )
         state[0:half, 0:half] = new_first
         state[width:, 0:half] = asked_left

time: 40.5 us -> 39.9 us (0.985)
  starting transfers between devices: 23.8 us -> 23.2 us
    ppermute x6, starting transfers between devices: 13.9 us -> 13.3 us  [swap(): lax.ppermute(value, axis, [(i, i ^ offset) for i in range(lax.axis_size(a...]
where the time goes in v9:
time: 39.9 us; the launch traced here: 39.8 us
  starting transfers between devices  23.2 us (58%)
  waiting for transfers between devices  14 us (35%)
  Pallas kernels  1.88 us (5%)
  other arithmetic  0.61 us (2%)
    ppermute x6, starting transfers between devices, swap(): lax.ppermute(value, axis, [(i, i ^ offset) for i in range(lax.axis_size(a...  13.3 us
    ppermute x7, starting transfers between devices, route(): return lax.ppermute(value, ('mod', 'dp'), pairs)  9.91 us
    ppermute x6, waiting for transfers between devices, swap(): lax.ppermute(value, axis, [(i, i ^ offset) for i in range(lax.axis_size(a...  7.08 us
    ppermute x7, waiting for transfers between devices, route(): return lax.ppermute(value, ('mod', 'dp'), pairs)  6.89 us
    pallas_call x1, Pallas kernels, pack(): pl.pallas_call(pack_kernel, out_shape=[near((rows + queries.shape[0], wid...  1.29 us
  transfers between devices with their start and end apart: 13, of which 9 were waited for; matrix products, arithmetic and copies ran while one was open for 0% of the time, Pallas kernels for 1%

profile of v9, /device:TPU:0, one launch (start us, length us, event | category | flops | bytes accessed | tf_op | source)
XLA Modules:
  0.0 39.8 jit_solution(12582241946256471753)
XLA Ops:
  0.0 1.3 %pack.1 = (f32[132,512]{1,0:T(8,128)S(1)}, f32[132,512]{1,0:T(8,128)S(1)}, f32[132,512]{1,0:T(8,128)S(1)}, f32[132,512]{1,0:T(8,128)S(1)}) custom-call(f32[128,4,512]{2,1,0:T(4,128)} %rows_ref.1, f32[4,4,512]{2,1,0:T(4,128)} %queries_ref.1), custom_call_target="tpu_custom_call" | custom-call | flops 1500000000 | tf_op jit(solution)/shard_map/pack/pallas_call | solution.py:100
  1.3 0.6 %collective-permute-start = (f32[132,512]{1,0:T(8,128)S(1)}, f32[132,512]{1,0:T(8,128)S(1)}, u32[]{:S(2)}, u32[]{:S(2)}) collective-permute-start(f32[132,512]{1,0:T(8,128)S(1)} %get-tuple-element.20.two.refs_4_), channel_id=1, source_target_pairs={{0,1},{1,0},{2,3},{3,2},{4,5},{5,4},{6,7},{7,6},{8,9},{9,8},{10,11... | collective-permute-start | bytes 811016 | tf_op jit(solution)/shard_map/ppermute | solution.py:313
  1.9 2.6 %collective-permute-start.3 = (f32[132,512]{1,0:T(8,128)S(1)}, f32[132,512]{1,0:T(8,128)S(1)}, u32[]{:S(2)}, u32[]{:S(2)}) collective-permute-start(f32[132,512]{1,0:T(8,128)S(1)} %get-tuple-element.24), channel_id=1, source_target_pairs={{0,3},{1,0},{2,1},{3,2},{4,7},{5,4},{6,5},{7,6},{8,11},{9,8},{10,9... | collective-permute-start | bytes 811016 | tf_op jit(solution)/shard_map/ppermute | solution.py:313
  4.4 1.6 %collective-permute-start.4 = (f32[132,512]{1,0:T(8,128)S(1)}, f32[132,512]{1,0:T(8,128)S(1)}, u32[]{:S(2)}, u32[]{:S(2)}) collective-permute-start(f32[132,512]{1,0:T(8,128)S(1)} %get-tuple-element.24), channel_id=1, source_target_pairs={{0,8},{1,3},{2,10},{3,1},{4,12},{5,7},{6,14},{7,5},{8,0},{9,11},{1... | collective-permute-start | bytes 811016 | tf_op jit(solution)/shard_map/ppermute | solution.py:313
  6.0 0.0 copy-start
  6.0 0.4 %collective-permute-start.1 = (f32[132,512]{1,0:T(8,128)S(1)}, f32[132,512]{1,0:T(8,128)S(1)}, u32[]{:S(2)}, u32[]{:S(2)}) collective-permute-start(f32[132,512]{1,0:T(8,128)S(1)} %get-tuple-element.22), channel_id=1, source_target_pairs={{0,8},{1,5},{2,10},{3,7},{4,12},{5,1},{6,14},{7,3},{8,0},{9,13},{1... | collective-permute-start | bytes 811016 | tf_op jit(solution)/shard_map/ppermute | solution.py:313
  6.5 1.6 %collective-permute-start.2 = (f32[132,512]{1,0:T(8,128)S(1)}, f32[132,512]{1,0:T(8,128)S(1)}, u32[]{:S(2)}, u32[]{:S(2)}) collective-permute-start(f32[132,512]{1,0:T(8,128)S(1)} %get-tuple-element.23), channel_id=1, source_target_pairs={{0,8},{1,7},{2,10},{3,5},{4,12},{5,3},{6,14},{7,1},{8,0},{9,15},{1... | collective-permute-start | bytes 811016 | tf_op jit(solution)/shard_map/ppermute | solution.py:313
  8.1 0.0 collective-permute-done.one.refs_3_
  8.1 0.0 collective-permute-start.5
  8.1 3.4 %collective-permute-done.3.one.refs_5_ = f32[132,512]{1,0:T(8,128)S(1)} collective-permute-done((f32[132,512]{1,0:T(8,128)S(1)}, f32[132,512]{1,0:T(8,128)S(1)}, u32[]{:S(2)}, u32[]{:S(2)}) %collective-permute-start.3) | collective-permute-done | bytes 270368 | tf_op jit(solution)/shard_map/ppermute | solution.py:313
  11.5 3.2 %collective-permute-start.6 = (f32[132,512]{1,0:T(8,128)S(1)}, f32[132,512]{1,0:T(8,128)S(1)}, u32[]{:S(2)}, u32[]{:S(2)}) collective-permute-start(f32[132,512]{1,0:T(8,128)S(1)} %get-tuple-element.23), channel_id=1, source_target_pairs={{0,7},{1,0},{2,5},{3,2},{4,3},{5,4},{6,1},{7,6},{8,15},{9,8},{10,1... | collective-permute-start | bytes 811016 | tf_op jit(solution)/shard_map/ppermute | solution.py:313
  14.7 0.0 copy-done
  14.7 0.6 %gram.3 = (f32[256,256]{1,0:T(8,128)S(1)}, f32[512,256]{1,0:T(8,128)S(1)}, f32[8,128]{1,0:T(8,128)S(1)}) custom-call(f32[4]{0:T(128)S(1)} %copy-done, f32[132,512]{1,0:T(8,128)S(1)} %collective-permute-done.one.refs_3_, f32[132,512]{1,0:T(8,128)S(1)} %get-tuple-element.20.two.refs_4_), custom_call_target="tpu_custom_call" | custom-call | flops 600000000 | tf_op jit(solution)/shard_map/gram/pallas_call | solution.py:155
  15.2 0.0 collective-permute-done.4.two.refs_6_
  15.3 0.0 collective-permute-done.1.one.refs_8_
  15.3 1.7 %collective-permute-done.2.two.refs_10_ = f32[132,512]{1,0:T(8,128)S(1)} collective-permute-done((f32[132,512]{1,0:T(8,128)S(1)}, f32[132,512]{1,0:T(8,128)S(1)}, u32[]{:S(2)}, u32[]{:S(2)}) %collective-permute-start.2) | collective-permute-done | bytes 270368 | tf_op jit(solution)/shard_map/ppermute | solution.py:313
  17.0 0.0 collective-permute-done.5.refs_7_
  17.0 1.7 %collective-permute-done.6.refs_9_ = f32[132,512]{1,0:T(8,128)S(1)} collective-permute-done((f32[132,512]{1,0:T(8,128)S(1)}, f32[132,512]{1,0:T(8,128)S(1)}, u32[]{:S(2)}, u32[]{:S(2)}) %collective-permute-start.6) | collective-permute-done | bytes 270368 | tf_op jit(solution)/shard_map/ppermute | solution.py:313
  18.7 0.6 %collective-permute-start.9 = (f32[32,256]{1,0:T(8,128)S(1)}, f32[32,256]{1,0:T(8,128)S(1)}, u32[]{:S(2)}, u32[]{:S(2)}) collective-permute-start(f32[32,256]{1,0:T(8,128)S(1)} %get-tuple-element.34), channel_id=1, source_target_pairs={{0,2},{1,3},{2,0},{3,1},{4,6},{5,7},{6,4},{7,5},{8,10},{9,11},{10,... | collective-permute-start | bytes 98312 | tf_op jit(solution)/shard_map/ppermute | solution.py:301
  19.3 0.4 %collective-permute-start.8 = (f32[32,256]{1,0:T(8,128)S(1)}, f32[32,256]{1,0:T(8,128)S(1)}, u32[]{:S(2)}, u32[]{:S(2)}) collective-permute-start(f32[32,256]{1,0:T(8,128)S(1)} %get-tuple-element.33), channel_id=1, source_target_pairs={{0,4},{1,5},{2,6},{3,7},{4,0},{5,1},{6,2},{7,3},{8,12},{9,13},{10,... | collective-permute-start | bytes 98312 | tf_op jit(solution)/shard_map/ppermute | solution.py:301
  19.8 2.5 %collective-permute-start.7 = (f32[32,256]{1,0:T(8,128)S(1)}, f32[32,256]{1,0:T(8,128)S(1)}, u32[]{:S(2)}, u32[]{:S(2)}) collective-permute-start(f32[32,256]{1,0:T(8,128)S(1)} %get-tuple-element.32), channel_id=1, source_target_pairs={{0,6},{1,7},{2,4},{3,5},{4,2},{5,3},{6,0},{7,1},{8,14},{9,15},{10,... | collective-permute-start | bytes 98312 | tf_op jit(solution)/shard_map/ppermute | solution.py:301
  22.3 0.4 %collective-permute-done.9 = f32[32,256]{1,0:T(8,128)S(1)} collective-permute-done((f32[32,256]{1,0:T(8,128)S(1)}, f32[32,256]{1,0:T(8,128)S(1)}, u32[]{:S(2)}, u32[]{:S(2)}) %collective-permute-start.9) | collective-permute-done | bytes 32800 | tf_op jit(solution)/shard_map/ppermute | solution.py:301
  22.7 0.5 %collective-permute-done.8 = f32[32,256]{1,0:T(8,128)S(1)} collective-permute-done((f32[32,256]{1,0:T(8,128)S(1)}, f32[32,256]{1,0:T(8,128)S(1)}, u32[]{:S(2)}, u32[]{:S(2)}) %collective-permute-start.8) | collective-permute-done | bytes 32800 | tf_op jit(solution)/shard_map/ppermute | solution.py:301
  23.3 1.3 %collective-permute-done.7 = f32[32,256]{1,0:T(8,128)S(1)} collective-permute-done((f32[32,256]{1,0:T(8,128)S(1)}, f32[32,256]{1,0:T(8,128)S(1)}, u32[]{:S(2)}, u32[]{:S(2)}) %collective-permute-start.7) | collective-permute-done | bytes 32800 | tf_op jit(solution)/shard_map/ppermute | solution.py:301
  24.6 2.8 %collective-permute-start.10 = (f32[16,256]{1,0:T(8,128)S(1)}, f32[16,256]{1,0:T(8,128)S(1)}, u32[]{:S(2)}, u32[]{:S(2)}) collective-permute-start(f32[16,256]{1,0:T(8,128)S(1)} %slice.25), channel_id=1, source_target_pairs={{0,16},{8,24},{16,0},{24,8},{1,17},{9,25},{17,1},{25,9},{2,18},{10... | collective-permute-start | bytes 49160 | tf_op jit(solution)/shard_map/ppermute | solution.py:301
  27.4 1.9 %collective-permute-done.10 = f32[16,256]{1,0:T(8,128)S(1)} collective-permute-done((f32[16,256]{1,0:T(8,128)S(1)}, f32[16,256]{1,0:T(8,128)S(1)}, u32[]{:S(2)}, u32[]{:S(2)}) %collective-permute-start.10) | collective-permute-done | bytes 16416 | tf_op jit(solution)/shard_map/ppermute | solution.py:301
  29.3 1.6 %collective-permute-start.11 = (f32[8,256]{1,0:T(8,128)S(1)}, f32[8,256]{1,0:T(8,128)S(1)}, u32[]{:S(2)}, u32[]{:S(2)}) collective-permute-start(f32[8,256]{1,0:T(8,128)S(1)} %slice.27), channel_id=1, source_target_pairs={{0,8},{8,0},{16,24},{24,16},{1,9},{9,1},{17,25},{25,17},{2,10},{10... | collective-permute-start | bytes 24584 | tf_op jit(solution)/shard_map/ppermute | solution.py:301
  31.0 2.0 %collective-permute-done.11 = f32[8,256]{1,0:T(8,128)S(1)} collective-permute-done((f32[8,256]{1,0:T(8,128)S(1)}, f32[8,256]{1,0:T(8,128)S(1)}, u32[]{:S(2)}, u32[]{:S(2)}) %collective-permute-start.11) | collective-permute-done | bytes 8224 | tf_op jit(solution)/shard_map/ppermute | solution.py:301
  33.0 5.3 %collective-permute-start.12 = (f32[8,128]{1,0:T(8,128)S(1)}, f32[8,128]{1,0:T(8,128)S(1)}, u32[]{:S(2)}, u32[]{:S(2)}) collective-permute-start(f32[8,128]{1,0:T(8,128)S(1)} %slice.29), channel_id=1, source_target_pairs={{0,1},{1,0},{2,3},{3,2},{4,5},{5,4},{6,7},{7,6},{8,9},{9,8},{10,11... | collective-permute-start | bytes 12296 | tf_op jit(solution)/shard_map/ppermute | solution.py:301
  38.3 0.8 %collective-permute-done.12 = f32[8,128]{1,0:T(8,128)S(1)} collective-permute-done((f32[8,128]{1,0:T(8,128)S(1)}, f32[8,128]{1,0:T(8,128)S(1)}, u32[]{:S(2)}, u32[]{:S(2)}) %collective-permute-start.12) | collective-permute-done | bytes 4128 | tf_op jit(solution)/shard_map/ppermute | solution.py:301
  39.2 0.6 %fusion = f32[128,8]{0,1:T(8,128)} fusion(f32[8,128]{1,0:T(8,128)S(1)} %collective-permute-done.12, f32[8,256]{1,0:T(8,128)S(1)} %slice_add_fusion.1, pred[]{:T(512)S(6)} %eq.5), kind=kLoop, calls=%fused_computation.4 | loop fusion | flops 1024 | bytes 12289 | tf_op jit(solution)/shard_map/transpose | solution.py:377
  (9 shorter events, 0.1 us)
Async XLA Ops:
  1.3 6.8 %collective-permute-start = (f32[132,512]{1,0:T(8,128)S(1)}, f32[132,512]{1,0:T(8,128)S(1)}, u32[]{:S(2)}, u32[]{:S(2)}) collective-permute-start(f32[132,512]{1,0:T(8,128)S(1)} %get-tuple-element.20.two.refs_4_), channel_id=1, source_target_pairs={{0,1},{1,0},{2,3},{3,2},{4,5},{5,4},{6,7},{7,6},{8,9},{9,8},{10,11... | collective-permute-start | bytes 811016 | tf_op jit(solution)/shard_map/ppermute | solution.py:313
  1.9 9.6 %collective-permute-start.3 = (f32[132,512]{1,0:T(8,128)S(1)}, f32[132,512]{1,0:T(8,128)S(1)}, u32[]{:S(2)}, u32[]{:S(2)}) collective-permute-start(f32[132,512]{1,0:T(8,128)S(1)} %get-tuple-element.24), channel_id=1, source_target_pairs={{0,3},{1,0},{2,1},{3,2},{4,7},{5,4},{6,5},{7,6},{8,11},{9,8},{10,9... | collective-permute-start | bytes 811016 | tf_op jit(solution)/shard_map/ppermute | solution.py:313
  4.4 10.8 %collective-permute-start.4 = (f32[132,512]{1,0:T(8,128)S(1)}, f32[132,512]{1,0:T(8,128)S(1)}, u32[]{:S(2)}, u32[]{:S(2)}) collective-permute-start(f32[132,512]{1,0:T(8,128)S(1)} %get-tuple-element.24), channel_id=1, source_target_pairs={{0,8},{1,3},{2,10},{3,1},{4,12},{5,7},{6,14},{7,5},{8,0},{9,11},{1... | collective-permute-start | bytes 811016 | tf_op jit(solution)/shard_map/ppermute | solution.py:313
  6.0 8.6 %copy-start = (f32[4]{0:T(128)S(1)}, f32[4]{0:T(128)}, u32[]{:S(2)}) copy-start(f32[4]{0:T(128)} %damping_ref.1) | copy-start | bytes 52
  6.0 9.2 %collective-permute-start.1 = (f32[132,512]{1,0:T(8,128)S(1)}, f32[132,512]{1,0:T(8,128)S(1)}, u32[]{:S(2)}, u32[]{:S(2)}) collective-permute-start(f32[132,512]{1,0:T(8,128)S(1)} %get-tuple-element.22), channel_id=1, source_target_pairs={{0,8},{1,5},{2,10},{3,7},{4,12},{5,1},{6,14},{7,3},{8,0},{9,13},{1... | collective-permute-start | bytes 811016 | tf_op jit(solution)/shard_map/ppermute | solution.py:313
  6.5 10.5 %collective-permute-start.2 = (f32[132,512]{1,0:T(8,128)S(1)}, f32[132,512]{1,0:T(8,128)S(1)}, u32[]{:S(2)}, u32[]{:S(2)}) collective-permute-start(f32[132,512]{1,0:T(8,128)S(1)} %get-tuple-element.23), channel_id=1, source_target_pairs={{0,8},{1,7},{2,10},{3,5},{4,12},{5,3},{6,14},{7,1},{8,0},{9,15},{1... | collective-permute-start | bytes 811016 | tf_op jit(solution)/shard_map/ppermute | solution.py:313
  8.1 8.9 %collective-permute-start.5 = (f32[132,512]{1,0:T(8,128)S(1)}, f32[132,512]{1,0:T(8,128)S(1)}, u32[]{:S(2)}, u32[]{:S(2)}) collective-permute-start(f32[132,512]{1,0:T(8,128)S(1)} %get-tuple-element.22), channel_id=1, source_target_pairs={{0,5},{1,0},{2,7},{3,2},{4,1},{5,4},{6,3},{7,6},{8,13},{9,8},{10,1... | collective-permute-start | bytes 811016 | tf_op jit(solution)/shard_map/ppermute | solution.py:313
  11.5 7.2 %collective-permute-start.6 = (f32[132,512]{1,0:T(8,128)S(1)}, f32[132,512]{1,0:T(8,128)S(1)}, u32[]{:S(2)}, u32[]{:S(2)}) collective-permute-start(f32[132,512]{1,0:T(8,128)S(1)} %get-tuple-element.23), channel_id=1, source_target_pairs={{0,7},{1,0},{2,5},{3,2},{4,3},{5,4},{6,1},{7,6},{8,15},{9,8},{10,1... | collective-permute-start | bytes 811016 | tf_op jit(solution)/shard_map/ppermute | solution.py:313
  18.7 4.0 %collective-permute-start.9 = (f32[32,256]{1,0:T(8,128)S(1)}, f32[32,256]{1,0:T(8,128)S(1)}, u32[]{:S(2)}, u32[]{:S(2)}) collective-permute-start(f32[32,256]{1,0:T(8,128)S(1)} %get-tuple-element.34), channel_id=1, source_target_pairs={{0,2},{1,3},{2,0},{3,1},{4,6},{5,7},{6,4},{7,5},{8,10},{9,11},{10,... | collective-permute-start | bytes 98312 | tf_op jit(solution)/shard_map/ppermute | solution.py:301
  19.3 3.9 %collective-permute-start.8 = (f32[32,256]{1,0:T(8,128)S(1)}, f32[32,256]{1,0:T(8,128)S(1)}, u32[]{:S(2)}, u32[]{:S(2)}) collective-permute-start(f32[32,256]{1,0:T(8,128)S(1)} %get-tuple-element.33), channel_id=1, source_target_pairs={{0,4},{1,5},{2,6},{3,7},{4,0},{5,1},{6,2},{7,3},{8,12},{9,13},{10,... | collective-permute-start | bytes 98312 | tf_op jit(solution)/shard_map/ppermute | solution.py:301
  19.8 4.8 %collective-permute-start.7 = (f32[32,256]{1,0:T(8,128)S(1)}, f32[32,256]{1,0:T(8,128)S(1)}, u32[]{:S(2)}, u32[]{:S(2)}) collective-permute-start(f32[32,256]{1,0:T(8,128)S(1)} %get-tuple-element.32), channel_id=1, source_target_pairs={{0,6},{1,7},{2,4},{3,5},{4,2},{5,3},{6,0},{7,1},{8,14},{9,15},{10,... | collective-permute-start | bytes 98312 | tf_op jit(solution)/shard_map/ppermute | solution.py:301
  24.6 4.7 %collective-permute-start.10 = (f32[16,256]{1,0:T(8,128)S(1)}, f32[16,256]{1,0:T(8,128)S(1)}, u32[]{:S(2)}, u32[]{:S(2)}) collective-permute-start(f32[16,256]{1,0:T(8,128)S(1)} %slice.25), channel_id=1, source_target_pairs={{0,16},{8,24},{16,0},{24,8},{1,17},{9,25},{17,1},{25,9},{2,18},{10... | collective-permute-start | bytes 49160 | tf_op jit(solution)/shard_map/ppermute | solution.py:301
  29.3 3.7 %collective-permute-start.11 = (f32[8,256]{1,0:T(8,128)S(1)}, f32[8,256]{1,0:T(8,128)S(1)}, u32[]{:S(2)}, u32[]{:S(2)}) collective-permute-start(f32[8,256]{1,0:T(8,128)S(1)} %slice.27), channel_id=1, source_target_pairs={{0,8},{8,0},{16,24},{24,16},{1,9},{9,1},{17,25},{25,17},{2,10},{10... | collective-permute-start | bytes 24584 | tf_op jit(solution)/shard_map/ppermute | solution.py:301
  33.0 6.2 %collective-permute-start.12 = (f32[8,128]{1,0:T(8,128)S(1)}, f32[8,128]{1,0:T(8,128)S(1)}, u32[]{:S(2)}, u32[]{:S(2)}) collective-permute-start(f32[8,128]{1,0:T(8,128)S(1)} %slice.29), channel_id=1, source_target_pairs={{0,1},{1,0},{2,3},{3,2},{4,5},{5,4},{6,7},{7,6},{8,9},{9,8},{10,11... | collective-permute-start | bytes 12296 | tf_op jit(solution)/shard_map/ppermute | solution.py:301

commit v10 on v9

--- a/solution.py
+++ b/solution.py
@@ -207,12 +207,13 @@
     eye = diagonal.astype(jnp.float32)
     first, cross, last = first_gram[...], right_gram[0:half], right_gram[half:]
     trace = jnp.sum((first + last) * eye, keepdims=True).reshape(1, 1)
-    shift = (damp_ref[0:1, 0:1] * trace * (1.0 / width)) * eye
-    first = first + shift
-    last = last + shift
     squares = first * first + last * last + 2.0 * (cross * cross)
-    squares = jnp.sum(squares, keepdims=True).reshape(1, 1) * (1.0 / total_rows**2)
-    inverse_norm = lax.rsqrt(squares + epsilon)
+    squares = jnp.sum(squares, keepdims=True).reshape(1, 1)
+    shift = damp_ref[0:1, 0:1] * trace * (1.0 / width)
+    squares = squares + 2.0 * shift * trace + shift * shift * width
+    first = first + shift * eye
+    last = last + shift * eye
+    inverse_norm = lax.rsqrt(squares * (1.0 / total_rows**2) + epsilon)
     per_row = inverse_norm * (1.0 / total_rows)
     cross = cross * per_row
     state[0:half, 0:half] = first * per_row
@@ -366,7 +367,8 @@
     scores = solve(sizes, damp, given, sum(blocks, []))
     total = scores[0]
     for offset in range(chips - 1, 0, -1):
-        total = total + swap(scores[offset], "dp", CORES * offset)
+        sent = swap(scores[offset], "dp", CORES * offset)
+        total = total + sent
     bit = groups // 2
     while bit:
         keep = total.shape[0] // 2

time: 39.9 us -> 39.7 us (level)
  no operation moved by 1% of the time
where the time goes in v10:
time: 39.7 us; the launch traced here: 39.6 us
  starting transfers between devices  23 us (58%)
  waiting for transfers between devices  14 us (35%)
  Pallas kernels  1.88 us (5%)
  other arithmetic  0.61 us (2%)
    ppermute x6, starting transfers between devices, swap(): lax.ppermute(value, axis, [(i, i ^ offset) for i in range(lax.axis_size(a...  13.1 us
    ppermute x7, starting transfers between devices, route(): return lax.ppermute(value, ('mod', 'dp'), pairs)  9.91 us
    ppermute x6, waiting for transfers between devices, swap(): lax.ppermute(value, axis, [(i, i ^ offset) for i in range(lax.axis_size(a...  7.08 us
    ppermute x7, waiting for transfers between devices, route(): return lax.ppermute(value, ('mod', 'dp'), pairs)  6.89 us
    pallas_call x1, Pallas kernels, pack(): pl.pallas_call(pack_kernel, out_shape=[near((rows + queries.shape[0], wid...  1.29 us
  transfers between devices with their start and end apart: 13, of which 9 were waited for; matrix products, arithmetic and copies ran while one was open for 0% of the time, Pallas kernels for 1%

profile of v10, /device:TPU:0, one launch (start us, length us, event | category | flops | bytes accessed | tf_op | source)
XLA Modules:
  0.0 39.6 jit_solution(621984101303608875)
XLA Ops:
  0.0 1.3 %pack.1 = (f32[132,512]{1,0:T(8,128)S(1)}, f32[132,512]{1,0:T(8,128)S(1)}, f32[132,512]{1,0:T(8,128)S(1)}, f32[132,512]{1,0:T(8,128)S(1)}) custom-call(f32[128,4,512]{2,1,0:T(4,128)} %rows_ref.1, f32[4,4,512]{2,1,0:T(4,128)} %queries_ref.1), custom_call_target="tpu_custom_call" | custom-call | flops 1500000000 | tf_op jit(solution)/shard_map/pack/pallas_call | solution.py:100
  1.3 0.6 %collective-permute-start = (f32[132,512]{1,0:T(8,128)S(1)}, f32[132,512]{1,0:T(8,128)S(1)}, u32[]{:S(2)}, u32[]{:S(2)}) collective-permute-start(f32[132,512]{1,0:T(8,128)S(1)} %get-tuple-element.20.two.refs_4_), channel_id=1, source_target_pairs={{0,1},{1,0},{2,3},{3,2},{4,5},{5,4},{6,7},{7,6},{8,9},{9,8},{10,11... | collective-permute-start | bytes 811016 | tf_op jit(solution)/shard_map/ppermute | solution.py:314
  1.9 2.6 %collective-permute-start.3 = (f32[132,512]{1,0:T(8,128)S(1)}, f32[132,512]{1,0:T(8,128)S(1)}, u32[]{:S(2)}, u32[]{:S(2)}) collective-permute-start(f32[132,512]{1,0:T(8,128)S(1)} %get-tuple-element.24), channel_id=1, source_target_pairs={{0,3},{1,0},{2,1},{3,2},{4,7},{5,4},{6,5},{7,6},{8,11},{9,8},{10,9... | collective-permute-start | bytes 811016 | tf_op jit(solution)/shard_map/ppermute | solution.py:314
  4.4 1.6 %collective-permute-start.4 = (f32[132,512]{1,0:T(8,128)S(1)}, f32[132,512]{1,0:T(8,128)S(1)}, u32[]{:S(2)}, u32[]{:S(2)}) collective-permute-start(f32[132,512]{1,0:T(8,128)S(1)} %get-tuple-element.24), channel_id=1, source_target_pairs={{0,8},{1,3},{2,10},{3,1},{4,12},{5,7},{6,14},{7,5},{8,0},{9,11},{1... | collective-permute-start | bytes 811016 | tf_op jit(solution)/shard_map/ppermute | solution.py:314
  6.0 0.0 copy-start
  6.0 0.4 %collective-permute-start.1 = (f32[132,512]{1,0:T(8,128)S(1)}, f32[132,512]{1,0:T(8,128)S(1)}, u32[]{:S(2)}, u32[]{:S(2)}) collective-permute-start(f32[132,512]{1,0:T(8,128)S(1)} %get-tuple-element.22), channel_id=1, source_target_pairs={{0,8},{1,5},{2,10},{3,7},{4,12},{5,1},{6,14},{7,3},{8,0},{9,13},{1... | collective-permute-start | bytes 811016 | tf_op jit(solution)/shard_map/ppermute | solution.py:314
  6.5 1.6 %collective-permute-start.2 = (f32[132,512]{1,0:T(8,128)S(1)}, f32[132,512]{1,0:T(8,128)S(1)}, u32[]{:S(2)}, u32[]{:S(2)}) collective-permute-start(f32[132,512]{1,0:T(8,128)S(1)} %get-tuple-element.23), channel_id=1, source_target_pairs={{0,8},{1,7},{2,10},{3,5},{4,12},{5,3},{6,14},{7,1},{8,0},{9,15},{1... | collective-permute-start | bytes 811016 | tf_op jit(solution)/shard_map/ppermute | solution.py:314
  8.1 0.0 collective-permute-done.one.refs_3_
  8.1 0.0 collective-permute-start.5
  8.1 3.4 %collective-permute-done.3.one.refs_5_ = f32[132,512]{1,0:T(8,128)S(1)} collective-permute-done((f32[132,512]{1,0:T(8,128)S(1)}, f32[132,512]{1,0:T(8,128)S(1)}, u32[]{:S(2)}, u32[]{:S(2)}) %collective-permute-start.3) | collective-permute-done | bytes 270368 | tf_op jit(solution)/shard_map/ppermute | solution.py:314
  11.5 3.2 %collective-permute-start.6 = (f32[132,512]{1,0:T(8,128)S(1)}, f32[132,512]{1,0:T(8,128)S(1)}, u32[]{:S(2)}, u32[]{:S(2)}) collective-permute-start(f32[132,512]{1,0:T(8,128)S(1)} %get-tuple-element.23), channel_id=1, source_target_pairs={{0,7},{1,0},{2,5},{3,2},{4,3},{5,4},{6,1},{7,6},{8,15},{9,8},{10,1... | collective-permute-start | bytes 811016 | tf_op jit(solution)/shard_map/ppermute | solution.py:314
  14.7 0.0 copy-done
  14.7 0.6 %gram.3 = (f32[256,256]{1,0:T(8,128)S(1)}, f32[512,256]{1,0:T(8,128)S(1)}, f32[8,128]{1,0:T(8,128)S(1)}) custom-call(f32[4]{0:T(128)S(1)} %copy-done, f32[132,512]{1,0:T(8,128)S(1)} %collective-permute-done.one.refs_3_, f32[132,512]{1,0:T(8,128)S(1)} %get-tuple-element.20.two.refs_4_), custom_call_target="tpu_custom_call" | custom-call | flops 600000000 | tf_op jit(solution)/shard_map/gram/pallas_call | solution.py:155
  15.2 0.0 collective-permute-done.4.two.refs_6_
  15.3 0.0 collective-permute-done.1.one.refs_8_
  15.3 1.7 %collective-permute-done.2.two.refs_10_ = f32[132,512]{1,0:T(8,128)S(1)} collective-permute-done((f32[132,512]{1,0:T(8,128)S(1)}, f32[132,512]{1,0:T(8,128)S(1)}, u32[]{:S(2)}, u32[]{:S(2)}) %collective-permute-start.2) | collective-permute-done | bytes 270368 | tf_op jit(solution)/shard_map/ppermute | solution.py:314
  17.0 0.0 collective-permute-done.5.refs_7_
  17.0 1.7 %collective-permute-done.6.refs_9_ = f32[132,512]{1,0:T(8,128)S(1)} collective-permute-done((f32[132,512]{1,0:T(8,128)S(1)}, f32[132,512]{1,0:T(8,128)S(1)}, u32[]{:S(2)}, u32[]{:S(2)}) %collective-permute-start.6) | collective-permute-done | bytes 270368 | tf_op jit(solution)/shard_map/ppermute | solution.py:314
  18.7 0.6 %collective-permute-start.9 = (f32[32,256]{1,0:T(8,128)S(1)}, f32[32,256]{1,0:T(8,128)S(1)}, u32[]{:S(2)}, u32[]{:S(2)}) collective-permute-start(f32[32,256]{1,0:T(8,128)S(1)} %get-tuple-element.34), channel_id=1, source_target_pairs={{0,2},{1,3},{2,0},{3,1},{4,6},{5,7},{6,4},{7,5},{8,10},{9,11},{10,... | collective-permute-start | bytes 98312 | tf_op jit(solution)/shard_map/ppermute | solution.py:302
  19.3 0.4 %collective-permute-start.8 = (f32[32,256]{1,0:T(8,128)S(1)}, f32[32,256]{1,0:T(8,128)S(1)}, u32[]{:S(2)}, u32[]{:S(2)}) collective-permute-start(f32[32,256]{1,0:T(8,128)S(1)} %get-tuple-element.33), channel_id=1, source_target_pairs={{0,4},{1,5},{2,6},{3,7},{4,0},{5,1},{6,2},{7,3},{8,12},{9,13},{10,... | collective-permute-start | bytes 98312 | tf_op jit(solution)/shard_map/ppermute | solution.py:302
  19.8 2.5 %collective-permute-start.7 = (f32[32,256]{1,0:T(8,128)S(1)}, f32[32,256]{1,0:T(8,128)S(1)}, u32[]{:S(2)}, u32[]{:S(2)}) collective-permute-start(f32[32,256]{1,0:T(8,128)S(1)} %get-tuple-element.32), channel_id=1, source_target_pairs={{0,6},{1,7},{2,4},{3,5},{4,2},{5,3},{6,0},{7,1},{8,14},{9,15},{10,... | collective-permute-start | bytes 98312 | tf_op jit(solution)/shard_map/ppermute | solution.py:302
  22.3 0.4 %collective-permute-done.9 = f32[32,256]{1,0:T(8,128)S(1)} collective-permute-done((f32[32,256]{1,0:T(8,128)S(1)}, f32[32,256]{1,0:T(8,128)S(1)}, u32[]{:S(2)}, u32[]{:S(2)}) %collective-permute-start.9) | collective-permute-done | bytes 32800 | tf_op jit(solution)/shard_map/ppermute | solution.py:302
  22.7 0.5 %collective-permute-done.8 = f32[32,256]{1,0:T(8,128)S(1)} collective-permute-done((f32[32,256]{1,0:T(8,128)S(1)}, f32[32,256]{1,0:T(8,128)S(1)}, u32[]{:S(2)}, u32[]{:S(2)}) %collective-permute-start.8) | collective-permute-done | bytes 32800 | tf_op jit(solution)/shard_map/ppermute | solution.py:302
  23.3 1.3 %collective-permute-done.7 = f32[32,256]{1,0:T(8,128)S(1)} collective-permute-done((f32[32,256]{1,0:T(8,128)S(1)}, f32[32,256]{1,0:T(8,128)S(1)}, u32[]{:S(2)}, u32[]{:S(2)}) %collective-permute-start.7) | collective-permute-done | bytes 32800 | tf_op jit(solution)/shard_map/ppermute | solution.py:302
  24.6 2.8 %collective-permute-start.10 = (f32[16,256]{1,0:T(8,128)S(1)}, f32[16,256]{1,0:T(8,128)S(1)}, u32[]{:S(2)}, u32[]{:S(2)}) collective-permute-start(f32[16,256]{1,0:T(8,128)S(1)} %slice.25), channel_id=1, source_target_pairs={{0,16},{8,24},{16,0},{24,8},{1,17},{9,25},{17,1},{25,9},{2,18},{10... | collective-permute-start | bytes 49160 | tf_op jit(solution)/shard_map/ppermute | solution.py:302
  27.4 1.9 %collective-permute-done.10 = f32[16,256]{1,0:T(8,128)S(1)} collective-permute-done((f32[16,256]{1,0:T(8,128)S(1)}, f32[16,256]{1,0:T(8,128)S(1)}, u32[]{:S(2)}, u32[]{:S(2)}) %collective-permute-start.10) | collective-permute-done | bytes 16416 | tf_op jit(solution)/shard_map/ppermute | solution.py:302
  29.3 1.6 %collective-permute-start.11 = (f32[8,256]{1,0:T(8,128)S(1)}, f32[8,256]{1,0:T(8,128)S(1)}, u32[]{:S(2)}, u32[]{:S(2)}) collective-permute-start(f32[8,256]{1,0:T(8,128)S(1)} %slice.27), channel_id=1, source_target_pairs={{0,8},{8,0},{16,24},{24,16},{1,9},{9,1},{17,25},{25,17},{2,10},{10... | collective-permute-start | bytes 24584 | tf_op jit(solution)/shard_map/ppermute | solution.py:302
  31.0 2.0 %collective-permute-done.11 = f32[8,256]{1,0:T(8,128)S(1)} collective-permute-done((f32[8,256]{1,0:T(8,128)S(1)}, f32[8,256]{1,0:T(8,128)S(1)}, u32[]{:S(2)}, u32[]{:S(2)}) %collective-permute-start.11) | collective-permute-done | bytes 8224 | tf_op jit(solution)/shard_map/ppermute | solution.py:302
  33.0 5.2 %collective-permute-start.12 = (f32[8,128]{1,0:T(8,128)S(1)}, f32[8,128]{1,0:T(8,128)S(1)}, u32[]{:S(2)}, u32[]{:S(2)}) collective-permute-start(f32[8,128]{1,0:T(8,128)S(1)} %slice.29), channel_id=1, source_target_pairs={{0,1},{1,0},{2,3},{3,2},{4,5},{5,4},{6,7},{7,6},{8,9},{9,8},{10,11... | collective-permute-start | bytes 12296 | tf_op jit(solution)/shard_map/ppermute | solution.py:302
  38.2 0.8 %collective-permute-done.12 = f32[8,128]{1,0:T(8,128)S(1)} collective-permute-done((f32[8,128]{1,0:T(8,128)S(1)}, f32[8,128]{1,0:T(8,128)S(1)}, u32[]{:S(2)}, u32[]{:S(2)}) %collective-permute-start.12) | collective-permute-done | bytes 4128 | tf_op jit(solution)/shard_map/ppermute | solution.py:302
  39.0 0.6 %fusion = f32[128,8]{0,1:T(8,128)} fusion(f32[8,128]{1,0:T(8,128)S(1)} %collective-permute-done.12, f32[8,256]{1,0:T(8,128)S(1)} %slice_add_fusion.1, pred[]{:T(512)S(6)} %eq.5), kind=kLoop, calls=%fused_computation.4 | loop fusion | flops 1024 | bytes 12289 | tf_op jit(solution)/shard_map/transpose | solution.py:379
  (9 shorter events, 0.1 us)
Async XLA Ops:
  1.3 6.8 %collective-permute-start = (f32[132,512]{1,0:T(8,128)S(1)}, f32[132,512]{1,0:T(8,128)S(1)}, u32[]{:S(2)}, u32[]{:S(2)}) collective-permute-start(f32[132,512]{1,0:T(8,128)S(1)} %get-tuple-element.20.two.refs_4_), channel_id=1, source_target_pairs={{0,1},{1,0},{2,3},{3,2},{4,5},{5,4},{6,7},{7,6},{8,9},{9,8},{10,11... | collective-permute-start | bytes 811016 | tf_op jit(solution)/shard_map/ppermute | solution.py:314
  1.9 9.6 %collective-permute-start.3 = (f32[132,512]{1,0:T(8,128)S(1)}, f32[132,512]{1,0:T(8,128)S(1)}, u32[]{:S(2)}, u32[]{:S(2)}) collective-permute-start(f32[132,512]{1,0:T(8,128)S(1)} %get-tuple-element.24), channel_id=1, source_target_pairs={{0,3},{1,0},{2,1},{3,2},{4,7},{5,4},{6,5},{7,6},{8,11},{9,8},{10,9... | collective-permute-start | bytes 811016 | tf_op jit(solution)/shard_map/ppermute | solution.py:314
  4.4 10.8 %collective-permute-start.4 = (f32[132,512]{1,0:T(8,128)S(1)}, f32[132,512]{1,0:T(8,128)S(1)}, u32[]{:S(2)}, u32[]{:S(2)}) collective-permute-start(f32[132,512]{1,0:T(8,128)S(1)} %get-tuple-element.24), channel_id=1, source_target_pairs={{0,8},{1,3},{2,10},{3,1},{4,12},{5,7},{6,14},{7,5},{8,0},{9,11},{1... | collective-permute-start | bytes 811016 | tf_op jit(solution)/shard_map/ppermute | solution.py:314
  6.0 8.6 %copy-start = (f32[4]{0:T(128)S(1)}, f32[4]{0:T(128)}, u32[]{:S(2)}) copy-start(f32[4]{0:T(128)} %damping_ref.1) | copy-start | bytes 52
  6.0 9.2 %collective-permute-start.1 = (f32[132,512]{1,0:T(8,128)S(1)}, f32[132,512]{1,0:T(8,128)S(1)}, u32[]{:S(2)}, u32[]{:S(2)}) collective-permute-start(f32[132,512]{1,0:T(8,128)S(1)} %get-tuple-element.22), channel_id=1, source_target_pairs={{0,8},{1,5},{2,10},{3,7},{4,12},{5,1},{6,14},{7,3},{8,0},{9,13},{1... | collective-permute-start | bytes 811016 | tf_op jit(solution)/shard_map/ppermute | solution.py:314
  6.5 10.5 %collective-permute-start.2 = (f32[132,512]{1,0:T(8,128)S(1)}, f32[132,512]{1,0:T(8,128)S(1)}, u32[]{:S(2)}, u32[]{:S(2)}) collective-permute-start(f32[132,512]{1,0:T(8,128)S(1)} %get-tuple-element.23), channel_id=1, source_target_pairs={{0,8},{1,7},{2,10},{3,5},{4,12},{5,3},{6,14},{7,1},{8,0},{9,15},{1... | collective-permute-start | bytes 811016 | tf_op jit(solution)/shard_map/ppermute | solution.py:314
  8.1 8.9 %collective-permute-start.5 = (f32[132,512]{1,0:T(8,128)S(1)}, f32[132,512]{1,0:T(8,128)S(1)}, u32[]{:S(2)}, u32[]{:S(2)}) collective-permute-start(f32[132,512]{1,0:T(8,128)S(1)} %get-tuple-element.22), channel_id=1, source_target_pairs={{0,5},{1,0},{2,7},{3,2},{4,1},{5,4},{6,3},{7,6},{8,13},{9,8},{10,1... | collective-permute-start | bytes 811016 | tf_op jit(solution)/shard_map/ppermute | solution.py:314
  11.5 7.2 %collective-permute-start.6 = (f32[132,512]{1,0:T(8,128)S(1)}, f32[132,512]{1,0:T(8,128)S(1)}, u32[]{:S(2)}, u32[]{:S(2)}) collective-permute-start(f32[132,512]{1,0:T(8,128)S(1)} %get-tuple-element.23), channel_id=1, source_target_pairs={{0,7},{1,0},{2,5},{3,2},{4,3},{5,4},{6,1},{7,6},{8,15},{9,8},{10,1... | collective-permute-start | bytes 811016 | tf_op jit(solution)/shard_map/ppermute | solution.py:314
  18.7 4.0 %collective-permute-start.9 = (f32[32,256]{1,0:T(8,128)S(1)}, f32[32,256]{1,0:T(8,128)S(1)}, u32[]{:S(2)}, u32[]{:S(2)}) collective-permute-start(f32[32,256]{1,0:T(8,128)S(1)} %get-tuple-element.34), channel_id=1, source_target_pairs={{0,2},{1,3},{2,0},{3,1},{4,6},{5,7},{6,4},{7,5},{8,10},{9,11},{10,... | collective-permute-start | bytes 98312 | tf_op jit(solution)/shard_map/ppermute | solution.py:302
  19.3 3.9 %collective-permute-start.8 = (f32[32,256]{1,0:T(8,128)S(1)}, f32[32,256]{1,0:T(8,128)S(1)}, u32[]{:S(2)}, u32[]{:S(2)}) collective-permute-start(f32[32,256]{1,0:T(8,128)S(1)} %get-tuple-element.33), channel_id=1, source_target_pairs={{0,4},{1,5},{2,6},{3,7},{4,0},{5,1},{6,2},{7,3},{8,12},{9,13},{10,... | collective-permute-start | bytes 98312 | tf_op jit(solution)/shard_map/ppermute | solution.py:302
  19.8 4.8 %collective-permute-start.7 = (f32[32,256]{1,0:T(8,128)S(1)}, f32[32,256]{1,0:T(8,128)S(1)}, u32[]{:S(2)}, u32[]{:S(2)}) collective-permute-start(f32[32,256]{1,0:T(8,128)S(1)} %get-tuple-element.32), channel_id=1, source_target_pairs={{0,6},{1,7},{2,4},{3,5},{4,2},{5,3},{6,0},{7,1},{8,14},{9,15},{10,... | collective-permute-start | bytes 98312 | tf_op jit(solution)/shard_map/ppermute | solution.py:302
  24.6 4.7 %collective-permute-start.10 = (f32[16,256]{1,0:T(8,128)S(1)}, f32[16,256]{1,0:T(8,128)S(1)}, u32[]{:S(2)}, u32[]{:S(2)}) collective-permute-start(f32[16,256]{1,0:T(8,128)S(1)} %slice.25), channel_id=1, source_target_pairs={{0,16},{8,24},{16,0},{24,8},{1,17},{9,25},{17,1},{25,9},{2,18},{10... | collective-permute-start | bytes 49160 | tf_op jit(solution)/shard_map/ppermute | solution.py:302
  29.3 3.7 %collective-permute-start.11 = (f32[8,256]{1,0:T(8,128)S(1)}, f32[8,256]{1,0:T(8,128)S(1)}, u32[]{:S(2)}, u32[]{:S(2)}) collective-permute-start(f32[8,256]{1,0:T(8,128)S(1)} %slice.27), channel_id=1, source_target_pairs={{0,8},{8,0},{16,24},{24,16},{1,9},{9,1},{17,25},{25,17},{2,10},{10... | collective-permute-start | bytes 24584 | tf_op jit(solution)/shard_map/ppermute | solution.py:302
  33.0 6.0 %collective-permute-start.12 = (f32[8,128]{1,0:T(8,128)S(1)}, f32[8,128]{1,0:T(8,128)S(1)}, u32[]{:S(2)}, u32[]{:S(2)}) collective-permute-start(f32[8,128]{1,0:T(8,128)S(1)} %slice.29), channel_id=1, source_target_pairs={{0,1},{1,0},{2,3},{3,2},{4,5},{5,4},{6,7},{7,6},{8,9},{9,8},{10,11... | collective-permute-start | bytes 12296 | tf_op jit(solution)/shard_map/ppermute | solution.py:302
